TPU v7x, 512 devices: a whole 4x4x16 slice. The times are simulated.
512 devices in a mesh: row: 128 (over x, z_hi, y, core), col: 4 (over z_lo).
Axes of the slice: x: 4, y: 4, z: 16 (z_hi: 4, z_lo: 4; z = z_hi * 4 + z_lo), core: 2. Of those that a mesh axis runs over, the one named last changes fastest.
Arguments:
- diag_inverse: float32 [512, 512], replicated, may hold values from -1 to 2, as said below
- panel: float32 [12288, 512], P('row', 'col'), may hold values from -0.3 to 0.3
- trailing: float32 [12288, 12288], P('row', 'col'), may hold values from -6 to 6
- agg_vals: float32 [128, 4, 192, 1024], P('row', 'col'), may hold values from -6 to 6
- agg_dest: int32 [128, 4, 192, 1], P('row', 'col'), may hold values from 0 to 127; in each aligned block of 192 rows (0 to 191, 192 to 383, ..., all dimensions but the last counted through in order) at most 2 rows name the same one
- agg_tile: int32 [128, 4, 192], P('row', 'col'), may hold values from 0 to 287
Outputs:
- updated: float32 [12288, 12288], P('row', 'col')
- panel_factor: float32 [12288, 512], P('row', 'col')
Inputs may be any that keep to these rules, and one draw needn't show every extreme that they name: `diag_inverse`: lower triangular with diagonal entries between 0.5 and 2. `agg_dest`: among the aggregates of one device no row index is named more than 2 times, and in some device one is named exactly 2 times.
All inputs are finite; a program needn't handle non-finite values.
Results may differ from a plain program's by a relative error of at most 0.000071.
Values sent between devices are 32-bit elements; how exact they have to be, the bound alone decides.
A program may use at most 64 MiB of HBM per device.

v0:
```python
import jax
import jax.numpy as jnp
from jax import lax
from jax.sharding import PartitionSpec as P

TILE_ROWS = 8
TILE_COLS = 128
CAP = 2


def per_device(diag_inverse, panel, trailing, agg_vals, agg_dest, agg_tile):
    row_devices = lax.axis_size("row")
    col_devices = lax.axis_size("col")
    local_rows, local_cols = trailing.shape
    panel_width = diag_inverse.shape[0]
    part_width = panel_width // col_devices
    col_index = lax.axis_index("col")
    contract_last = (((1,), (1,)), ((), ()))
    panel_whole = lax.all_gather(panel, "col", axis=1, tiled=True)
    own_full = jnp.dot(
        panel_whole,
        diag_inverse.T,
        precision=lax.Precision.HIGHEST,
        preferred_element_type=jnp.float32,
    )
    own_block = lax.dynamic_slice_in_dim(own_full, col_index * part_width, part_width, 1)
    column_all = lax.all_gather(own_block, "row", axis=0, tiled=True)
    split_rows = column_all.reshape(col_devices, local_cols, part_width)
    swapped = lax.all_to_all(split_rows, "col", split_axis=0, concat_axis=2, tiled=True)
    partner = swapped.reshape(local_cols, panel_width)
    tile_rows = local_rows // TILE_ROWS
    tile_cols = local_cols // TILE_COLS
    tiles_dev = tile_rows * tile_cols
    tile_values = agg_vals.reshape(agg_vals.shape[2], agg_vals.shape[3])
    targets = agg_dest.reshape(-1)
    tile_ids = agg_tile.reshape(-1)
    matches = (targets[:, None] == jnp.arange(row_devices, dtype=jnp.int32)[None, :]).astype(
        jnp.int32
    )
    earlier = jnp.cumsum(matches, axis=0) - matches
    ranks = jnp.sum(earlier * matches, axis=1)
    position = targets * CAP + ranks
    send_values = (
        jnp.zeros((row_devices * CAP, tile_values.shape[1]), jnp.float32)
        .at[position]
        .set(tile_values)
    )
    send_ids = (
        jnp.full((row_devices * CAP,), float(tiles_dev), jnp.float32)
        .at[position]
        .set(tile_ids.astype(jnp.float32))
    )
    got_values, got_ids = (
        lax.all_to_all(send_values, "row", split_axis=0, concat_axis=0, tiled=True),
        lax.all_to_all(send_ids, "row", split_axis=0, concat_axis=0, tiled=True),
    )
    landing = got_ids.astype(jnp.int32)
    blocked = trailing.reshape(tile_rows, TILE_ROWS, tile_cols, TILE_COLS)
    blocked = blocked.at[landing // tile_cols, :, landing % tile_cols, :].add(
        got_values.reshape(-1, TILE_ROWS, TILE_COLS), mode="drop"
    )
    assembled = blocked.reshape(local_rows, local_cols)
    product = lax.dot_general(
        own_full,
        partner,
        contract_last,
        precision=lax.Precision.HIGHEST,
        preferred_element_type=jnp.float32,
    )
    updated = assembled - product
    return (updated, own_block)


def solution(mesh):
    in_specs = (
        P(),
        P("row", "col"),
        P("row", "col"),
        P("row", "col", None, None),
        P("row", "col", None, None),
        P("row", "col", None),
    )
    out_specs = (P("row", "col"), P("row", "col"))
    return jax.shard_map(
        per_device, mesh=mesh, in_specs=in_specs, out_specs=out_specs, check_vma=False
    )
```

profile of v0, /device:TPU:1, one launch (start us, length us, event | category | flops | bytes accessed | tf_op | source)
XLA Modules:
  0.0 355.4 jit_solution(15490305446457586598)
XLA Ops:
  7.2 0.0 copy-start
  7.2 0.0 all-gather.2.cloned.1.call-start
  7.2 0.8 copy-done.4
  8.1 13.3 %all_gather.6 = f32[96,512]{1,0:T(8,128)S(1)} all-gather(f32[96,128]{1,0:T(8,128)S(1)} %copy-done.4), channel_id=1, replica_groups=mesh['row'=128,'col'=4] {'col'}, dimensions={1}, use_global_device_ids=true | all-gather | bytes 245760 | tf_op jit(solution)/shard_map/all_gather | solution.py:19
  21.4 1.1 fusion.10
  22.5 0.6 constant_dynamic-slice_fusion
  23.1 0.0 all-gather.2.cloned.1.call-update
  23.2 0.1 iota_compare_fusion
  23.3 0.1 fusion.3
  23.5 0.2 fusion.6
  23.7 1.2 scatter_custom_fusion
  24.9 0.8 all_to_all.23
  25.7 23.4 %all-to-all-start = ((f32[128,2,1]{1,2,0:T(1,128)}), f32[128,2,1]{1,2,0:T(1,128)S(1)}, u32[]{:S(2)}, u32[]{:S(2)}) async-start(f32[128,2,1]{1,2,0:T(1,128)} %bitcast.10), calls=%async_computation | async-start | bytes 131072 | tf_op jit(solution)/shard_map/all_to_all | solution.py:55
  49.1 1.5 scatter_custom_fusion.1
  50.6 1.6 all_to_all.25
  52.2 13.9 %all-to-all-done = f32[128,2,1]{1,2,0:T(1,128)S(1)} async-done(((f32[128,2,1]{1,2,0:T(1,128)}), f32[128,2,1]{1,2,0:T(1,128)S(1)}, u32[]{:S(2)}, u32[]{:S(2)}) %all-to-all-start) | async-done | bytes 1056 | tf_op jit(solution)/shard_map/all_to_all | solution.py:55
  66.1 6.9 %all-to-all-start.1 = ((f32[128,2,1024]{2,1,0:T(2,128)}), f32[128,2,1024]{2,1,0:T(2,128)S(1)}, u32[]{:S(2)}, u32[]{:S(2)}) async-start(f32[128,2,1024]{2,1,0:T(2,128)} %all_to_all.25), calls=%async_computation.1 | async-start | bytes 2097152 | tf_op jit(solution)/shard_map/all_to_all | solution.py:54
  73.0 117.3 %all-gather.2.cloned.1.call-done = f32[12288,128]{1,0:T(8,128)} async-done(((f32[96,128]{1,0:T(8,128)}), f32[12288,128]{1,0:T(8,128)}) %all-gather.2.cloned.1.call-update) | async-done | bytes 6291472 | tf_op jit(solution)/shard_map/all_gather | solution.py:27
  190.3 6.5 %copy.14 = f32[4,3072,128]{1,2,0:T(8,128)} copy(f32[4,3072,128]{2,1,0:T(8,128)} %bitcast.37) | data formatting | bytes 12582912 | tf_op jit(solution)/shard_map/reshape | solution.py:28
  196.8 0.0 all-to-all-done.1
  196.8 1.0 copy-done.2
  197.8 5.4 %all-to-all-start.2 = ((f32[4,3072,128]{1,2,0:T(8,128)}), f32[4,3072,128]{1,2,0:T(8,128)}, u32[]{:S(2)}, u32[]{:S(2)}) async-start(f32[4,3072,128]{1,2,0:T(8,128)} %copy.14), calls=%async_computation.2 | async-start | bytes 12582912 | tf_op jit(solution)/shard_map/all_to_all | solution.py:29
  203.2 0.5 divide_reduce_fusion
  203.7 0.0 copy-start.1
  203.7 0.1 rem.30
  203.9 0.1 div.17
  204.0 0.3 compare_reduce_fusion
  204.3 0.1 ne.52
  204.5 2.1 reshape.174
  206.6 11.5 %scatter_fusion = f32[12,8,24,128]{3,1,2,0:T(8,128)S(1)} fusion(f32[12,8,24,128]{3,1,2,0:T(8,128)S(1)} %bitcast.36, s32[256]{0:T(256)S(1)} %bitcast.35, f32[256,8,128]{2,1,0:T(8,128)S(1)} %reshape.174), kind=kCustom, calls=%fused_computation.2 | custom fusion | flops 262144 | bytes 3147776 | tf_op jit(solution)/shard_map/scatter-add | solution.py:59
  218.1 123.0 %all-to-all-done.2 = f32[4,3072,128]{1,2,0:T(8,128)} async-done(((f32[4,3072,128]{1,2,0:T(8,128)}), f32[4,3072,128]{1,2,0:T(8,128)}, u32[]{:S(2)}, u32[]{:S(2)}) %all-to-all-start.2) | async-done | bytes 6291488 | tf_op jit(solution)/shard_map/all_to_all | solution.py:29
  341.1 7.5 %convolution_subtract_fusion = f32[96,3072]{1,0:T(8,128)} fusion(f32[96,512]{1,0:T(8,128)S(1)} %fusion.10, f32[3072,512]{0,1:T(8,128)} %bitcast.17, f32[12,8,24,128]{3,1,2,0:T(8,128)S(1)} %scatter_fusion), kind=kOutput, calls=%fused_computation.3 | convolution fusion | flops 1812234240 | bytes 8847360 | tf_op jit(solution)/shard_map/dot_general | solution.py:63
  (20 shorter events, 0.1 us)
Async XLA Ops:
  7.2 14.2 %copy-start = (f32[512,512]{1,0:T(8,128)S(1)}, f32[512,512]{1,0:T(8,128)}, u32[]{:S(2)}) copy-start(f32[512,512]{1,0:T(8,128)} %param.6) | copy-start | bytes 3145732
  7.2 0.9 copy-start.4
  7.2 183.1 %all-gather.2.cloned.1.call-start = ((), (), s32[]{:S(2)}) async-start(), calls=%async_computation.3 | async-start | bytes 6340608 | tf_op jit(solution)/shard_map/all_gather | solution.py:27
  7.2 15.9 %copy-start.5 = (s32[1,1,192,1]{2,3,1,0:T(1,128)S(1)}, s32[1,1,192,1]{2,3,1,0:T(1,128)}, u32[]{:S(2)}) copy-start(s32[1,1,192,1]{2,3,1,0:T(1,128)} %param.10) | copy-start | bytes 2308
  21.4 2.2 copy-start.6
  21.4 27.7 %copy-start.3 = (f32[1,1,192,1024]{3,2,1,0:T(8,128)S(1)}, f32[1,1,192,1024]{3,2,1,0:T(8,128)}, u32[]{:S(2)}) copy-start(f32[1,1,192,1024]{3,2,1,0:T(8,128)} %param.9) | copy-start | bytes 2359300
  25.7 40.4 %all-to-all-start = ((f32[128,2,1]{1,2,0:T(1,128)}), f32[128,2,1]{1,2,0:T(1,128)S(1)}, u32[]{:S(2)}, u32[]{:S(2)}) async-start(f32[128,2,1]{1,2,0:T(1,128)} %bitcast.10), calls=%async_computation | async-start | bytes 131072 | tf_op jit(solution)/shard_map/all_to_all | solution.py:55
  66.1 130.7 %all-to-all-start.1 = ((f32[128,2,1024]{2,1,0:T(2,128)}), f32[128,2,1024]{2,1,0:T(2,128)S(1)}, u32[]{:S(2)}, u32[]{:S(2)}) async-start(f32[128,2,1024]{2,1,0:T(2,128)} %all_to_all.25), calls=%async_computation.1 | async-start | bytes 2097152 | tf_op jit(solution)/shard_map/all_to_all | solution.py:54
  196.8 1.0 copy-start.2
  197.8 143.3 %all-to-all-start.2 = ((f32[4,3072,128]{1,2,0:T(8,128)}), f32[4,3072,128]{1,2,0:T(8,128)}, u32[]{:S(2)}, u32[]{:S(2)}) async-start(f32[4,3072,128]{1,2,0:T(8,128)} %copy.14), calls=%async_computation.2 | async-start | bytes 12582912 | tf_op jit(solution)/shard_map/all_to_all | solution.py:29
  203.7 2.9 copy-start.1
Sparse Core Ops, SparseCore 0:
  23.3 166.9 all-gather.1
where the time goes:
time: 356 us; the launch traced here: 355 us
  waiting for transfers between devices  254 us (71%)
  starting transfers between devices  35.7 us (10%)
  local copies, waits for them, and re-layouts  16.6 us (5%)
  between operations  14.2 us (4%)
  blocking collectives  13.3 us (4%)
  other arithmetic  12.8 us (4%)
  matrix products  8.63 us (2%)
    all_to_all x1, waiting for transfers between devices, per_device(): lax.all_to_all(split_rows, 'col', split_axis=0, concat_axis=2, tiled=True)  123 us
    all_gather x1, waiting for transfers between devices, per_device(): column_all = lax.all_gather(own_block, 'row', axis=0, tiled=True)  117 us
    all_to_all x1, starting transfers between devices, per_device(): lax.all_to_all(send_ids, 'row', split_axis=0, concat_axis=0, tiled=True)  23.4 us
    all_to_all x1, waiting for transfers between devices, per_device(): lax.all_to_all(send_ids, 'row', split_axis=0, concat_axis=0, tiled=True)  13.9 us
    all_gather x1, blocking collectives, per_device(): panel_whole = lax.all_gather(panel, 'col', axis=1, tiled=True)  13.3 us
    scatter-add x1, other arithmetic, per_device(): blocked.at[landing // tile_cols, :, landing % tile_cols, :]  11.5 us
    dot_general x1, matrix products, per_device(): lax.dot_general(own_full, partner, contract_last, precision=lax.Precision...  7.5 us
  transfers between devices with their start and end apart: 4, of which 3 were waited for; matrix products, arithmetic and copies ran while one was open for 7% of the time, Pallas kernels for 0%

commit v1 on v0

--- a/solution.py
+++ b/solution.py
@@ -1,19 +1,21 @@
 import jax
 import jax.numpy as jnp
+import numpy as np
 from jax import lax
+from jax.sharding import Mesh
 from jax.sharding import PartitionSpec as P
 
 TILE_ROWS = 8
 TILE_COLS = 128
 CAP = 2
+ROW_AXES = ("rx", "rin")
 
 
 def per_device(diag_inverse, panel, trailing, agg_vals, agg_dest, agg_tile):
-    row_devices = lax.axis_size("row")
-    col_devices = lax.axis_size("col")
+    row_devices = lax.axis_size(ROW_AXES)
     local_rows, local_cols = trailing.shape
     panel_width = diag_inverse.shape[0]
-    part_width = panel_width // col_devices
+    part_width = panel_width // lax.axis_size("col")
     col_index = lax.axis_index("col")
     contract_last = (((1,), (1,)), ((), ()))
     panel_whole = lax.all_gather(panel, "col", axis=1, tiled=True)
@@ -24,10 +26,9 @@
         preferred_element_type=jnp.float32,
     )
     own_block = lax.dynamic_slice_in_dim(own_full, col_index * part_width, part_width, 1)
-    column_all = lax.all_gather(own_block, "row", axis=0, tiled=True)
-    split_rows = column_all.reshape(col_devices, local_cols, part_width)
-    swapped = lax.all_to_all(split_rows, "col", split_axis=0, concat_axis=2, tiled=True)
-    partner = swapped.reshape(local_cols, panel_width)
+    across = lax.all_gather(own_full, "rx", axis=0, tiled=False)
+    chosen = lax.dynamic_index_in_dim(across, col_index, 0, keepdims=False)
+    partner = lax.all_gather(chosen, "rin", axis=0, tiled=True)
     tile_rows = local_rows // TILE_ROWS
     tile_cols = local_cols // TILE_COLS
     tiles_dev = tile_rows * tile_cols
@@ -51,8 +52,8 @@
         .set(tile_ids.astype(jnp.float32))
     )
     got_values, got_ids = (
-        lax.all_to_all(send_values, "row", split_axis=0, concat_axis=0, tiled=True),
-        lax.all_to_all(send_ids, "row", split_axis=0, concat_axis=0, tiled=True),
+        lax.all_to_all(send_values, ROW_AXES, split_axis=0, concat_axis=0, tiled=True),
+        lax.all_to_all(send_ids, ROW_AXES, split_axis=0, concat_axis=0, tiled=True),
     )
     landing = got_ids.astype(jnp.int32)
     blocked = trailing.reshape(tile_rows, TILE_ROWS, tile_cols, TILE_COLS)
@@ -72,15 +73,18 @@
 
 
 def solution(mesh):
+    n_row, n_col = mesh.devices.shape
+    split = Mesh(mesh.devices.reshape(n_col, n_row // n_col, n_col), ROW_AXES + ("col",))
+    rows = ROW_AXES
     in_specs = (
         P(),
-        P("row", "col"),
-        P("row", "col"),
-        P("row", "col", None, None),
-        P("row", "col", None, None),
-        P("row", "col", None),
+        P(rows, "col"),
+        P(rows, "col"),
+        P(rows, "col", None, None),
+        P(rows, "col", None, None),
+        P(rows, "col", None),
     )
-    out_specs = (P("row", "col"), P("row", "col"))
+    out_specs = (P(rows, "col"), P(rows, "col"))
     return jax.shard_map(
-        per_device, mesh=mesh, in_specs=in_specs, out_specs=out_specs, check_vma=False
+        per_device, mesh=split, in_specs=in_specs, out_specs=out_specs, check_vma=False
     )

time: 356 us -> 223 us (0.63)
  waiting for transfers between devices: 254 us -> 117 us
  blocking collectives: 13.3 us -> 24.3 us
  local copies, waits for them, and re-layouts: 16.6 us -> 9.79 us
    all_gather x1, waiting for transfers between devices: 117 us -> 0.02 us  [per_device(): partner = lax.all_gather(chosen, 'rin', axis=0, tiled=True)]
    all_to_all x3 -> x2, waiting for transfers between devices: 137 us -> 117 us  [the longest x1 98.9 us: per_device(): lax.all_to_all(send_values, ROW_AXES, split_axis=0, concat_axis=0, tiled=...]
    all_gather x0 -> x1, blocking collectives: none -> 11 us  [per_device(): across = lax.all_gather(own_full, 'rx', axis=0, tiled=False)]
    reshape x1 -> x0, local copies, waits for them, and re-layouts: 6.52 us -> none  [per_device(): split_rows = column_all.reshape(col_devices, local_cols, part_width)]
    all_to_all x3 -> x2, starting transfers between devices: 35.7 us -> 33 us  [the longest x1 25.4 us: per_device(): lax.all_to_all(send_ids, ROW_AXES, split_axis=0, concat_axis=0, tiled=True)]
  transfers between devices with their start and end apart: 4 -> 3, of which waited for: 3 -> 2; matrix products, arithmetic and copies ran while one was open for 7% -> 9% of each run, Pallas kernels for 0% -> 0%
where the time goes in v1:
time: 223 us
  waiting for transfers between devices  117 us (52%)
  starting transfers between devices  33.1 us (15%)
  blocking collectives  24.3 us (11%)
  between operations  14.2 us (6%)
  other arithmetic  13.1 us (6%)
  matrix products  11 us (5%)
  local copies, waits for them, and re-layouts  9.79 us (4%)
    all_to_all x1, waiting for transfers between devices, per_device(): lax.all_to_all(send_values, ROW_AXES, split_axis=0, concat_axis=0, tiled=...  98.9 us
    all_to_all x1, starting transfers between devices, per_device(): lax.all_to_all(send_ids, ROW_AXES, split_axis=0, concat_axis=0, tiled=True)  25.4 us
    all_to_all x1, waiting for transfers between devices, per_device(): lax.all_to_all(send_ids, ROW_AXES, split_axis=0, concat_axis=0, tiled=True)  18.2 us
    all_gather x1, blocking collectives, per_device(): panel_whole = lax.all_gather(panel, 'col', axis=1, tiled=True)  13.3 us
    scatter-add x1, other arithmetic, per_device(): blocked.at[landing // tile_cols, :, landing % tile_cols, :]  11.8 us
    all_gather x1, blocking collectives, per_device(): across = lax.all_gather(own_full, 'rx', axis=0, tiled=False)  11 us
    dot_general x1, matrix products, per_device(): lax.dot_general(own_full, partner, contract_last, precision=lax.Precision...  9.87 us
    all_to_all x1, starting transfers between devices, per_device(): lax.all_to_all(send_values, ROW_AXES, split_axis=0, concat_axis=0, tiled=...  7.64 us
  transfers between devices with their start and end apart: 3, of which 2 were waited for; matrix products, arithmetic and copies ran while one was open for 9% of the time, Pallas kernels for 0%

profile of v1, /device:TPU:1, one launch (start us, length us, event | category | flops | bytes accessed | tf_op | source)
XLA Modules:
  0.0 222.6 jit_solution(13095345503135978365)
XLA Ops:
  7.2 0.0 copy-start
  7.2 0.0 all-gather.4.cloned.1.call-start
  7.2 0.8 copy-done.3
  8.1 13.3 %all_gather.12 = f32[96,512]{1,0:T(8,128)S(1)} all-gather(f32[96,128]{1,0:T(8,128)S(1)} %copy-done.3), channel_id=1, replica_groups=mesh['rx'=4,'rin'=32,'col'=4] {'col'}, dimensions={1}, use_global_device_ids=true | all-gather | bytes 245760 | tf_op jit(solution)/shard_map/all_gather | solution.py:21
  21.4 1.1 fusion.15
  22.5 0.0 copy-start.5
  22.5 11.0 %all-gather = f32[384,512]{1,0:T(8,128)S(1)} all-gather(f32[96,512]{1,0:T(8,128)S(1)} %fusion.15), channel_id=2, replica_groups=mesh['rx'=4,'rin'=32,'col'=4] {'rx'}, dimensions={0}, use_global_device_ids=true | all-gather | bytes 983040 | tf_op jit(solution)/shard_map/all_gather | solution.py:29
  33.5 0.7 constant_dynamic-slice_fusion.1
  34.2 0.0 all-gather.4.cloned.1.call-update
  34.3 0.0 copy-done.4
  34.3 0.1 iota_compare_fusion
  34.4 0.1 fusion.8
  34.6 0.2 fusion.11
  34.8 1.2 scatter_custom_fusion
  36.0 0.8 all_to_all.12
  36.8 25.4 %all-to-all-start = ((f32[128,2,1]{1,2,0:T(1,128)}), f32[128,2,1]{1,2,0:T(1,128)S(1)}, u32[]{:S(2)}, u32[]{:S(2)}) async-start(f32[128,2,1]{1,2,0:T(1,128)} %bitcast.10), calls=%async_computation | async-start | bytes 131072 | tf_op jit(solution)/shard_map/all_to_all | solution.py:56
  62.2 1.5 scatter_custom_fusion.1
  63.7 1.6 all_to_all.14
  65.3 18.2 %all-to-all-done = f32[128,2,1]{1,2,0:T(1,128)S(1)} async-done(((f32[128,2,1]{1,2,0:T(1,128)}), f32[128,2,1]{1,2,0:T(1,128)S(1)}, u32[]{:S(2)}, u32[]{:S(2)}) %all-to-all-start) | async-done | bytes 1056 | tf_op jit(solution)/shard_map/all_to_all | solution.py:56
  83.5 7.6 %all-to-all-start.1 = ((f32[128,2,1024]{2,1,0:T(2,128)}), f32[128,2,1024]{2,1,0:T(2,128)}, u32[]{:S(2)}, u32[]{:S(2)}) async-start(f32[128,2,1024]{2,1,0:T(2,128)} %all_to_all.14), calls=%async_computation.1 | async-start | bytes 2097152 | tf_op jit(solution)/shard_map/all_to_all | solution.py:55
  91.2 0.6 constant_dynamic-slice_fusion
  91.8 0.5 divide_reduce_fusion
  92.3 0.0 copy-start.1
  92.3 0.1 div.17
  92.5 0.1 rem.30
  92.6 0.3 compare_reduce_fusion
  92.9 0.1 ne.52
  93.1 98.9 %all-to-all-done.1 = f32[128,2,1024]{2,1,0:T(2,128)} async-done(((f32[128,2,1024]{2,1,0:T(2,128)}), f32[128,2,1024]{2,1,0:T(2,128)}, u32[]{:S(2)}, u32[]{:S(2)}) %all-to-all-start.1) | async-done | bytes 1048608 | tf_op jit(solution)/shard_map/all_to_all | solution.py:55
  192.0 2.1 reshape.165
  194.1 11.8 %scatter_fusion = f32[12,8,24,128]{3,1,2,0:T(8,128)S(1)} fusion(f32[12,8,24,128]{3,1,2,0:T(8,128)S(1)} %bitcast.35, s32[256]{0:T(256)S(1)} %bitcast.34, f32[256,8,128]{2,1,0:T(8,128)S(1)} %reshape.165), kind=kCustom, calls=%fused_computation.2 | custom fusion | flops 262144 | bytes 3147776 | tf_op jit(solution)/shard_map/scatter-add | solution.py:60
  205.9 0.0 all-gather.4.cloned.1.call-done
  205.9 9.9 %fusion.2 = f32[96,3072]{1,0:T(8,128)} fusion(f32[96,512]{1,0:T(8,128)S(1)} %fusion.15, f32[1,3072,512]{2,1,0:T(8,128)} %all-gather.4.cloned.1.call-done, f32[12,8,24,128]{3,1,2,0:T(8,128)S(1)} %scatter_fusion), kind=kOutput, calls=%fused_computation.5 | convolution fusion | flops 1812234240 | bytes 8847360 | tf_op jit(solution)/shard_map/dot_general | solution.py:64
  (17 shorter events, 0.1 us)
Async XLA Ops:
  7.2 14.2 %copy-start = (f32[512,512]{1,0:T(8,128)S(1)}, f32[512,512]{1,0:T(8,128)}, u32[]{:S(2)}) copy-start(f32[512,512]{1,0:T(8,128)} %param.6) | copy-start | bytes 3145732
  7.2 0.9 copy-start.3
  7.2 198.7 %all-gather.4.cloned.1.call-start = ((), (), s32[]{:S(2)}) async-start(), calls=%async_computation.2 | async-start | bytes 6488064 | tf_op jit(solution)/shard_map/all_gather | solution.py:31
  21.4 12.9 %copy-start.4 = (s32[1,1,192,1]{2,3,1,0:T(1,128)S(1)}, s32[1,1,192,1]{2,3,1,0:T(1,128)}, u32[]{:S(2)}) copy-start(s32[1,1,192,1]{2,3,1,0:T(1,128)} %param.10) | copy-start | bytes 2308
  22.5 12.1 %copy-start.5 = (s32[1,1,192]{2,1,0:T(1,128)S(1)}, s32[1,1,192]{2,1,0:T(1,128)}, u32[]{:S(2)}) copy-start(s32[1,1,192]{2,1,0:T(1,128)} %param.11) | copy-start | bytes 2308
  33.5 28.7 %copy-start.2 = (f32[1,1,192,1024]{3,2,1,0:T(8,128)S(1)}, f32[1,1,192,1024]{3,2,1,0:T(8,128)}, u32[]{:S(2)}) copy-start(f32[1,1,192,1024]{3,2,1,0:T(8,128)} %param.9) | copy-start | bytes 2359300
  36.8 46.7 %all-to-all-start = ((f32[128,2,1]{1,2,0:T(1,128)}), f32[128,2,1]{1,2,0:T(1,128)S(1)}, u32[]{:S(2)}, u32[]{:S(2)}) async-start(f32[128,2,1]{1,2,0:T(1,128)} %bitcast.10), calls=%async_computation | async-start | bytes 131072 | tf_op jit(solution)/shard_map/all_to_all | solution.py:56
  83.5 108.5 %all-to-all-start.1 = ((f32[128,2,1024]{2,1,0:T(2,128)}), f32[128,2,1024]{2,1,0:T(2,128)}, u32[]{:S(2)}, u32[]{:S(2)}) async-start(f32[128,2,1024]{2,1,0:T(2,128)} %all_to_all.14), calls=%async_computation.1 | async-start | bytes 2097152 | tf_op jit(solution)/shard_map/all_to_all | solution.py:55
  92.3 101.7 %copy-start.1 = (f32[96,3072]{1,0:T(8,128)S(1)}, f32[96,3072]{1,0:T(8,128)}, u32[]{:S(2)}) copy-start(f32[96,3072]{1,0:T(8,128)} %param.8) | copy-start | bytes 3538948
Sparse Core Ops, SparseCore 0:
  34.4 160.4 all-gather.3

commit v2 on v1

--- a/solution.py
+++ b/solution.py
@@ -8,7 +8,7 @@
 TILE_ROWS = 8
 TILE_COLS = 128
 CAP = 2
-ROW_AXES = ("rx", "rin")
+ROW_AXES = ("x", "zh", "y", "core")
 
 
 def per_device(diag_inverse, panel, trailing, agg_vals, agg_dest, agg_tile):
@@ -26,9 +26,20 @@
         preferred_element_type=jnp.float32,
     )
     own_block = lax.dynamic_slice_in_dim(own_full, col_index * part_width, part_width, 1)
-    across = lax.all_gather(own_full, "rx", axis=0, tiled=False)
-    chosen = lax.dynamic_index_in_dim(across, col_index, 0, keepdims=False)
-    partner = lax.all_gather(chosen, "rin", axis=0, tiled=True)
+    z_quarters = lax.all_gather(own_block, "zh", axis=0, tiled=False)
+    z_full = lax.all_gather(z_quarters, "col", axis=2, tiled=True)
+    x_index = lax.axis_index("x")
+    n_x = lax.axis_size("x")
+    n_c = lax.axis_size("col")
+    shift = (x_index - col_index) % n_x
+    chosen = z_full
+    for step in range(1, n_x):
+        pairs = [(c * n_c + c, ((c + step) % n_x) * n_c + c) for c in range(n_c)]
+        got = lax.ppermute(z_full, ("x", "col"), pairs)
+        chosen = jnp.where(shift == step, got, chosen)
+    gathered = lax.all_gather(chosen, ("y", "core"), axis=0, tiled=False)
+    n_yc = gathered.shape[0]
+    n_zh = gathered.shape[1]
     tile_rows = local_rows // TILE_ROWS
     tile_cols = local_cols // TILE_COLS
     tiles_dev = tile_rows * tile_cols
@@ -61,6 +72,7 @@
         got_values.reshape(-1, TILE_ROWS, TILE_COLS), mode="drop"
     )
     assembled = blocked.reshape(local_rows, local_cols)
+    partner = gathered.reshape(n_yc * n_zh * local_rows, panel_width)
     product = lax.dot_general(
         own_full,
         partner,
@@ -68,13 +80,19 @@
         precision=lax.Precision.HIGHEST,
         preferred_element_type=jnp.float32,
     )
+    product = (
+        product.reshape(local_rows, n_yc, n_zh, local_rows)
+        .transpose(0, 2, 1, 3)
+        .reshape(local_rows, local_cols)
+    )
     updated = assembled - product
     return (updated, own_block)
 
 
 def solution(mesh):
     n_row, n_col = mesh.devices.shape
-    split = Mesh(mesh.devices.reshape(n_col, n_row // n_col, n_col), ROW_AXES + ("col",))
+    shape = (n_col, n_col, n_col, n_row // n_col**3, n_col)
+    split = Mesh(mesh.devices.reshape(shape), ROW_AXES + ("col",))
     rows = ROW_AXES
     in_specs = (
         P(),

time: 223 us -> 234 us (1.049)
  waiting for transfers between devices: 117 us -> 90.2 us
  blocking collectives: 24.3 us -> 51 us
  starting transfers between devices: 33.1 us -> 39.5 us
  local copies, waits for them, and re-layouts: 9.79 us -> 13.1 us
  other arithmetic: 13.1 us -> 15.5 us
    all_to_all x1, waiting for transfers between devices: 98.9 us -> 55 us  [per_device(): lax.all_to_all(send_values, ROW_AXES, split_axis=0, concat_axis=0, tiled=...]
    all_gather x1 -> x2, blocking collectives: 11 us -> 37.7 us  [the longest x1 23.1 us: per_device(): z_quarters = lax.all_gather(own_block, 'zh', axis=0, tiled=False)]
    ppermute x0 -> x3, waiting for transfers between devices: none -> 21.6 us  [per_device(): got = lax.ppermute(z_full, ('x', 'col'), pairs)]
    ppermute x0 -> x3, starting transfers between devices: none -> 8.79 us  [per_device(): got = lax.ppermute(z_full, ('x', 'col'), pairs)]
    all_to_all x1, waiting for transfers between devices: 18.2 us -> 13.5 us  [per_device(): lax.all_to_all(send_ids, ROW_AXES, split_axis=0, concat_axis=0, tiled=True)]
  transfers between devices with their start and end apart: 3 -> 6, of which waited for: 2 -> 5; matrix products, arithmetic and copies ran while one was open for 9% -> 8% of each run, Pallas kernels for 0% -> 0%
where the time goes in v2:
time: 234 us
  waiting for transfers between devices  90.2 us (39%)
  blocking collectives  51 us (22%)
  starting transfers between devices  39.5 us (17%)
  other arithmetic  15.5 us (7%)
  between operations  14.2 us (6%)
  local copies, waits for them, and re-layouts  13.1 us (6%)
  matrix products  10.3 us (4%)
    all_to_all x1, waiting for transfers between devices, per_device(): lax.all_to_all(send_values, ROW_AXES, split_axis=0, concat_axis=0, tiled=...  55 us
    all_to_all x1, starting transfers between devices, per_device(): lax.all_to_all(send_ids, ROW_AXES, split_axis=0, concat_axis=0, tiled=True)  23.6 us
    all_gather x1, blocking collectives, per_device(): z_quarters = lax.all_gather(own_block, 'zh', axis=0, tiled=False)  23.1 us
    ppermute x3, waiting for transfers between devices, per_device(): got = lax.ppermute(z_full, ('x', 'col'), pairs)  21.6 us
    all_gather x1, blocking collectives, per_device(): z_full = lax.all_gather(z_quarters, 'col', axis=2, tiled=True)  14.6 us
    all_to_all x1, waiting for transfers between devices, per_device(): lax.all_to_all(send_ids, ROW_AXES, split_axis=0, concat_axis=0, tiled=True)  13.5 us
    all_gather x1, blocking collectives, per_device(): panel_whole = lax.all_gather(panel, 'col', axis=1, tiled=True)  13.3 us
    scatter-add x1, other arithmetic, per_device(): blocked.at[landing // tile_cols, :, landing % tile_cols, :]  11.8 us
  transfers between devices with their start and end apart: 6, of which 5 were waited for; matrix products, arithmetic and copies ran while one was open for 8% of the time, Pallas kernels for 0%

profile of v2, /device:TPU:1, one launch (start us, length us, event | category | flops | bytes accessed | tf_op | source)
XLA Modules:
  0.0 233.8 jit_solution(14567154936892402232)
XLA Ops:
  7.2 0.8 copy-done.4
  8.1 13.3 %all_gather.18 = f32[96,512]{1,0:T(8,128)S(1)} all-gather(f32[96,128]{1,0:T(8,128)S(1)} %copy-done.4), channel_id=1, replica_groups=mesh['x'=4,'zh'=4,'y'=4,'core'=2,'col'=4] {'col'}, dimensions={1}, use_global_device_ids=true | all-gather | bytes 245760 | tf_op jit(solution)/shard_map/all_gather | solution.py:21
  21.4 1.1 fusion.11
  22.5 23.1 %all-gather = f32[384,128]{1,0:T(8,128)S(1)} all-gather(f32[96,128]{1,0:T(8,128)S(1)} %constant_dynamic-slice_fusion), channel_id=2, replica_groups=mesh['x'=4,'zh'=4,'y'=4,'core'=2,'col'=4] {'zh'}, dimensions={0}, use_global_device_ids=true | all-gather | bytes 245760 | tf_op jit(solution)/shard_map/all_gather | solution.py:29
  45.6 14.6 %all_gather.21 = f32[4,96,512]{2,1,0:T(8,128)S(1)} all-gather(f32[4,96,128]{2,1,0:T(8,128)S(1)} %bitcast.42), channel_id=1, replica_groups=mesh['x'=4,'zh'=4,'y'=4,'core'=2,'col'=4] {'col'}, dimensions={2}, use_global_device_ids=true | all-gather | bytes 983040 | tf_op jit(solution)/shard_map/all_gather | solution.py:30
  60.2 4.4 %collective-permute-start = (f32[4,96,512]{2,1,0:T(8,128)S(1)}, f32[4,96,512]{2,1,0:T(8,128)S(1)}, u32[]{:S(2)}, u32[]{:S(2)}) collective-permute-start(f32[4,96,512]{2,1,0:T(8,128)S(1)} %all_gather.21), channel_id=1, source_target_pairs={{0,384},{129,1},{258,130},{387,259},{4,388},{133,5},{262,134},{391... | collective-permute-start | bytes 2359304 | tf_op jit(solution)/shard_map/ppermute | solution.py:38
  64.7 2.2 collective-permute-start.1
  66.8 2.2 collective-permute-start.2
  69.0 4.5 %collective-permute-done = f32[4,96,512]{2,1,0:T(8,128)S(1)} collective-permute-done((f32[4,96,512]{2,1,0:T(8,128)S(1)}, f32[4,96,512]{2,1,0:T(8,128)S(1)}, u32[]{:S(2)}, u32[]{:S(2)}) %collective-permute-start) | collective-permute-done | bytes 786464 | tf_op jit(solution)/shard_map/ppermute | solution.py:38
  73.5 1.3 collective-permute-done.1
  74.9 15.8 %collective-permute-done.2 = f32[4,96,512]{2,1,0:T(8,128)} collective-permute-done((f32[4,96,512]{2,1,0:T(8,128)S(1)}, f32[4,96,512]{2,1,0:T(8,128)}, u32[]{:S(2)}, u32[]{:S(2)}) %collective-permute-start.2) | collective-permute-done | bytes 786464 | tf_op jit(solution)/shard_map/ppermute | solution.py:38
  90.7 1.2 select_select_fusion
  92.3 0.3 copy-done.6
  92.6 0.2 fusion.7
  92.8 1.2 scatter_custom_fusion
  94.0 0.8 all_to_all.12
  94.8 23.6 %all-to-all-start = ((f32[128,2,1]{1,2,0:T(1,128)}), f32[128,2,1]{1,2,0:T(1,128)S(1)}, u32[]{:S(2)}, u32[]{:S(2)}) async-start(f32[128,2,1]{1,2,0:T(1,128)} %bitcast.10), calls=%async_computation | async-start | bytes 131072 | tf_op jit(solution)/shard_map/all_to_all | solution.py:67
  118.4 1.5 scatter_custom_fusion.1
  120.0 1.6 all_to_all.14
  121.5 13.5 %all-to-all-done = f32[128,2,1]{1,2,0:T(1,128)S(1)} async-done(((f32[128,2,1]{1,2,0:T(1,128)}), f32[128,2,1]{1,2,0:T(1,128)S(1)}, u32[]{:S(2)}, u32[]{:S(2)}) %all-to-all-start) | async-done | bytes 1056 | tf_op jit(solution)/shard_map/all_to_all | solution.py:67
  135.1 7.0 %all-to-all-start.1 = ((f32[128,2,1024]{2,1,0:T(2,128)}), f32[128,2,1024]{2,1,0:T(2,128)}, u32[]{:S(2)}, u32[]{:S(2)}) async-start(f32[128,2,1024]{2,1,0:T(2,128)} %all_to_all.14), calls=%async_computation.1 | async-start | bytes 2097152 | tf_op jit(solution)/shard_map/all_to_all | solution.py:66
  142.1 0.5 divide_reduce_fusion
  142.8 0.1 rem.44
  143.0 0.3 compare_reduce_fusion
  143.3 0.1 ne.58
  143.4 55.0 %all-to-all-done.1 = f32[128,2,1024]{2,1,0:T(2,128)} async-done(((f32[128,2,1024]{2,1,0:T(2,128)}), f32[128,2,1024]{2,1,0:T(2,128)}, u32[]{:S(2)}, u32[]{:S(2)}) %all-to-all-start.1) | async-done | bytes 1048608 | tf_op jit(solution)/shard_map/all_to_all | solution.py:66
  198.4 2.1 reshape.173
  200.5 11.8 %scatter_fusion = f32[12,8,24,128]{3,1,2,0:T(8,128)S(1)} fusion(f32[12,8,24,128]{3,1,2,0:T(8,128)S(1)} %bitcast.40, s32[256]{0:T(256)S(1)} %bitcast.39, f32[256,8,128]{2,1,0:T(8,128)S(1)} %reshape.173), kind=kCustom, calls=%fused_computation.2 | custom fusion | flops 262144 | bytes 3147776 | tf_op jit(solution)/shard_map/scatter-add | solution.py:71
  212.3 9.2 %convolution_bitcast_fusion = f32[96,4,8,96]{3,0,1,2:T(8,128)S(1)} fusion(f32[8,4,96,512]{3,2,1,0:T(8,128)} %bitcast.41, f32[96,512]{1,0:T(8,128)S(1)} %fusion.11), kind=kOutput, calls=%fused_computation.3 | convolution fusion | flops 1811939328 | bytes 7667712 | tf_op jit(solution)/shard_map/dot_general | solution.py:76
  221.5 2.1 copy.14
  223.6 2.3 reshape.153
  225.8 1.1 bitcast_subtract_fusion
  (29 shorter events, 0.6 us)
Async XLA Ops:
  7.2 14.2 %copy-start = (f32[512,512]{1,0:T(8,128)S(1)}, f32[512,512]{1,0:T(8,128)}, u32[]{:S(2)}) copy-start(f32[512,512]{1,0:T(8,128)} %param.6) | copy-start | bytes 3145732
  7.2 0.9 copy-start.4
  7.2 205.1 %all-gather.4.cloned.1.call-start = ((), (), s32[]{:S(2)}) async-start(), calls=%async_computation.2 | async-start | bytes 7077888 | tf_op jit(solution)/shard_map/all_gather | solution.py:40
  22.5 69.4 %copy-start.3 = (f32[96,128]{1,0:T(8,128)}, f32[96,128]{1,0:T(8,128)S(1)}, u32[]{:S(2)}) copy-start(f32[96,128]{1,0:T(8,128)S(1)} %constant_dynamic-slice_fusion) | copy-start | bytes 147460
  60.2 13.3 %collective-permute-start = (f32[4,96,512]{2,1,0:T(8,128)S(1)}, f32[4,96,512]{2,1,0:T(8,128)S(1)}, u32[]{:S(2)}, u32[]{:S(2)}) collective-permute-start(f32[4,96,512]{2,1,0:T(8,128)S(1)} %all_gather.21), channel_id=1, source_target_pairs={{0,384},{129,1},{258,130},{387,259},{4,388},{133,5},{262,134},{391... | collective-permute-start | bytes 2359304 | tf_op jit(solution)/shard_map/ppermute | solution.py:38
  64.7 10.2 %collective-permute-start.1 = (f32[4,96,512]{2,1,0:T(8,128)S(1)}, f32[4,96,512]{2,1,0:T(8,128)}, u32[]{:S(2)}, u32[]{:S(2)}) collective-permute-start(f32[4,96,512]{2,1,0:T(8,128)S(1)} %all_gather.21), channel_id=1, source_target_pairs={{0,256},{129,385},{258,2},{387,131},{4,260},{133,389},{262,6},{391... | collective-permute-start | bytes 2359304 | tf_op jit(solution)/shard_map/ppermute | solution.py:38
  66.8 23.8 %collective-permute-start.2 = (f32[4,96,512]{2,1,0:T(8,128)S(1)}, f32[4,96,512]{2,1,0:T(8,128)}, u32[]{:S(2)}, u32[]{:S(2)}) collective-permute-start(f32[4,96,512]{2,1,0:T(8,128)S(1)} %all_gather.21), channel_id=1, source_target_pairs={{0,128},{129,257},{258,386},{387,3},{4,132},{133,261},{262,390},{3... | collective-permute-start | bytes 2359304 | tf_op jit(solution)/shard_map/ppermute | solution.py:38
  69.0 22.9 %copy-start.5 = (s32[1,1,192,1]{2,3,1,0:T(1,128)S(1)}, s32[1,1,192,1]{2,3,1,0:T(1,128)}, u32[]{:S(2)}) copy-start(s32[1,1,192,1]{2,3,1,0:T(1,128)} %param.10) | copy-start | bytes 2308
  91.9 0.7 copy-start.6
  91.9 26.5 %copy-start.2 = (f32[1,1,192,1024]{3,2,1,0:T(8,128)S(1)}, f32[1,1,192,1024]{3,2,1,0:T(8,128)}, u32[]{:S(2)}) copy-start(f32[1,1,192,1024]{3,2,1,0:T(8,128)} %param.9) | copy-start | bytes 2359300
  94.8 40.3 %all-to-all-start = ((f32[128,2,1]{1,2,0:T(1,128)}), f32[128,2,1]{1,2,0:T(1,128)S(1)}, u32[]{:S(2)}, u32[]{:S(2)}) async-start(f32[128,2,1]{1,2,0:T(1,128)} %bitcast.10), calls=%async_computation | async-start | bytes 131072 | tf_op jit(solution)/shard_map/all_to_all | solution.py:67
  135.1 63.3 %all-to-all-start.1 = ((f32[128,2,1024]{2,1,0:T(2,128)}), f32[128,2,1024]{2,1,0:T(2,128)}, u32[]{:S(2)}, u32[]{:S(2)}) async-start(f32[128,2,1024]{2,1,0:T(2,128)} %all_to_all.14), calls=%async_computation.1 | async-start | bytes 2097152 | tf_op jit(solution)/shard_map/all_to_all | solution.py:66
  142.7 57.8 %copy-start.1 = (f32[96,3072]{1,0:T(8,128)S(1)}, f32[96,3072]{1,0:T(8,128)}, u32[]{:S(2)}) copy-start(f32[96,3072]{1,0:T(8,128)} %param.8) | copy-start | bytes 3538948
Sparse Core Ops, SparseCore 0:
  92.1 56.2 all-gather.3

commit v3 on v1

v3 whole, which is shorter than its diff:
```python
import jax
import jax.numpy as jnp
from jax import lax
from jax.sharding import Mesh
from jax.sharding import PartitionSpec as P

TILE_ROWS = 8
TILE_COLS = 128
CAP = 2
ROW_AXES = ("x", "zh", "y", "core")


def per_device(diag_inverse, panel, trailing, agg_vals, agg_dest, agg_tile):
    row_devices = lax.axis_size(ROW_AXES)
    local_rows, local_cols = trailing.shape
    panel_width = diag_inverse.shape[0]
    part_width = panel.shape[1]
    col_index = lax.axis_index("col")
    zh_index = lax.axis_index("zh")

    tile_rows = local_rows // TILE_ROWS
    tile_cols = local_cols // TILE_COLS
    tiles_dev = tile_rows * tile_cols
    tile_values = agg_vals.reshape(agg_vals.shape[2], agg_vals.shape[3])
    targets = agg_dest.reshape(-1)
    tile_ids = agg_tile.reshape(-1)
    matches = (targets[:, None] == jnp.arange(row_devices, dtype=jnp.int32)[None, :]).astype(
        jnp.int32
    )
    earlier = jnp.cumsum(matches, axis=0) - matches
    ranks = jnp.sum(earlier * matches, axis=1)
    position = targets * CAP + ranks
    id_lanes = jnp.broadcast_to(tile_ids.astype(jnp.float32)[:, None], (tile_ids.shape[0], TILE_COLS))
    payload = jnp.concatenate([tile_values, id_lanes], axis=1)
    send = (
        jnp.zeros((row_devices * CAP, payload.shape[1]), jnp.float32)
        .at[:, tile_values.shape[1]:]
        .set(float(tiles_dev))
        .at[position]
        .set(payload)
    )
    got = lax.all_to_all(send, ROW_AXES, split_axis=0, concat_axis=0, tiled=True)
    got_values = got[:, : tile_values.shape[1]]
    landing = got[:, tile_values.shape[1]].astype(jnp.int32)

    ring_panel = lax.all_gather(panel, ("zh", "col"), axis=0, tiled=False)
    n_zh = lax.axis_size("zh")
    n_c = lax.axis_size("col")
    ring_panel = ring_panel.reshape(n_zh, n_c, local_rows, part_width)
    ring_panel = ring_panel.transpose(0, 2, 1, 3).reshape(n_zh * local_rows, n_c * part_width)
    ring_factor = jnp.dot(
        ring_panel,
        diag_inverse.T,
        precision=lax.Precision.HIGHEST,
        preferred_element_type=jnp.float32,
    ).reshape(n_zh, local_rows, panel_width)
    own_full = lax.dynamic_index_in_dim(ring_factor, zh_index, 0, keepdims=False)
    own_block = lax.dynamic_slice_in_dim(own_full, col_index * part_width, part_width, 1)

    x_index = lax.axis_index("x")
    n_x = lax.axis_size("x")
    shift = (x_index - col_index) % n_x
    chosen = ring_factor
    for step in range(1, n_x):
        pairs = [(c * n_c + c, ((c + step) % n_x) * n_c + c) for c in range(n_c)]
        moved = lax.ppermute(ring_factor, ("x", "col"), pairs)
        chosen = jnp.where(shift == step, moved, chosen)
    gathered = lax.all_gather(chosen, ("y", "core"), axis=1, tiled=False)
    partner = gathered.reshape(local_cols, panel_width)

    blocked = trailing.reshape(tile_rows, TILE_ROWS, tile_cols, TILE_COLS)
    blocked = blocked.at[landing // tile_cols, :, landing % tile_cols, :].add(
        got_values.reshape(-1, TILE_ROWS, TILE_COLS), mode="drop"
    )
    assembled = blocked.reshape(local_rows, local_cols)
    product = lax.dot_general(
        own_full,
        partner,
        (((1,), (1,)), ((), ())),
        precision=lax.Precision.HIGHEST,
        preferred_element_type=jnp.float32,
    )
    updated = assembled - product
    return (updated, own_block)


def solution(mesh):
    n_row, n_col = mesh.devices.shape
    shape = (n_col, n_col, n_col, n_row // n_col**3, n_col)
    split = Mesh(mesh.devices.reshape(shape), ROW_AXES + ("col",))
    rows = ROW_AXES
    in_specs = (
        P(),
        P(rows, "col"),
        P(rows, "col"),
        P(rows, "col", None, None),
        P(rows, "col", None, None),
        P(rows, "col", None),
    )
    out_specs = (P(rows, "col"), P(rows, "col"))
    return jax.shard_map(
        per_device, mesh=split, in_specs=in_specs, out_specs=out_specs, check_vma=False
    )
```

time: 223 us -> 199 us (0.89)
  waiting for transfers between devices: 117 us -> 83.7 us
  blocking collectives: 24.3 us -> 33.9 us
  other arithmetic: 13.1 us -> 15.9 us
    all_to_all x2 -> x1, waiting for transfers between devices: 117 us -> 60.8 us  [per_device(): lax.all_to_all(send, ROW_AXES, split_axis=0, concat_axis=0, tiled=True)]
    ppermute x0 -> x3, waiting for transfers between devices: none -> 22.9 us  [per_device(): moved = lax.ppermute(ring_factor, ('x', 'col'), pairs)]
    all_to_all x2 -> x1, starting transfers between devices: 33 us -> 22.3 us  [per_device(): lax.all_to_all(send, ROW_AXES, split_axis=0, concat_axis=0, tiled=True)]
    all_gather x2 -> x1, blocking collectives: 24.3 us -> 33.9 us  [per_device(): ring_panel = lax.all_gather(panel, ('zh', 'col'), axis=0, tiled=False)]
    ppermute x0 -> x3, starting transfers between devices: none -> 8.8 us  [per_device(): moved = lax.ppermute(ring_factor, ('x', 'col'), pairs)]
    scatter x2, local copies, waits for them, and re-layouts: 2.72 us -> 0.09 us  [per_device(): send = jnp.zeros((row_devices * CAP, payload.shape[1]), jnp.float32).at[:...]
    scatter x0 -> x1, other arithmetic: none -> 2.39 us  [per_device(): send = jnp.zeros((row_devices * CAP, payload.shape[1]), jnp.float32).at[:...]
  transfers between devices with their start and end apart: 3 -> 5, of which waited for: 2 -> 4; matrix products, arithmetic and copies ran while one was open for 9% -> 8% of each run, Pallas kernels for 0% -> 0%
where the time goes in v3:
time: 199 us
  waiting for transfers between devices  83.7 us (42%)
  blocking collectives  33.9 us (17%)
  starting transfers between devices  31.1 us (16%)
  other arithmetic  15.9 us (8%)
  between operations  14.2 us (7%)
  matrix products  12.6 us (6%)
  local copies, waits for them, and re-layouts  7.62 us (4%)
    all_to_all x1, waiting for transfers between devices, per_device(): lax.all_to_all(send, ROW_AXES, split_axis=0, concat_axis=0, tiled=True)  60.8 us
    all_gather x1, blocking collectives, per_device(): ring_panel = lax.all_gather(panel, ('zh', 'col'), axis=0, tiled=False)  33.9 us
    ppermute x3, waiting for transfers between devices, per_device(): moved = lax.ppermute(ring_factor, ('x', 'col'), pairs)  22.9 us
    all_to_all x1, starting transfers between devices, per_device(): lax.all_to_all(send, ROW_AXES, split_axis=0, concat_axis=0, tiled=True)  22.3 us
    scatter-add x1, other arithmetic, per_device(): blocked.at[landing // tile_cols, :, landing % tile_cols, :]  11.8 us
    dot_general x1, matrix products, per_device(): lax.dot_general(own_full, partner, (((1,), (1,)), ((), ())), precision=la...  9.99 us
    ppermute x3, starting transfers between devices, per_device(): moved = lax.ppermute(ring_factor, ('x', 'col'), pairs)  8.8 us
  transfers between devices with their start and end apart: 5, of which 4 were waited for; matrix products, arithmetic and copies ran while one was open for 8% of the time, Pallas kernels for 0%

profile of v3, /device:TPU:1, one launch (start us, length us, event | category | flops | bytes accessed | tf_op | source)
XLA Modules:
  0.0 199.0 jit_solution(9828623200081971384)
XLA Ops:
  7.2 0.0 all-gather.4.cloned.1.call-start
  7.2 0.8 copy-done.3
  8.1 33.9 %all-gather = f32[1536,128]{1,0:T(8,128)S(1)} all-gather(f32[96,128]{1,0:T(8,128)S(1)} %copy-done.3), channel_id=2, replica_groups=mesh['x'=4,'zh'=4,'y'=4,'core'=2,'col'=4] {'zh','col'}, dimensions={0}, use_global_device_ids=true | all-gather | bytes 835584 | tf_op jit(solution)/shard_map/all_gather | solution.py:46
  42.0 0.5 copy.25
  42.5 1.2 dot_general.8
  43.7 2.6 %fusion = f32[4,96,512]{2,1,0:T(8,128)S(1)} fusion(f32[4,96,512]{2,1,0:T(8,128)} %dot_general.8, f32[512,512]{1,0:T(8,128)S(1)} %copy-done), kind=kOutput, calls=%fused_computation.4 | convolution fusion | flops 1207959552 | bytes 2621440 | tf_op jit(solution)/shard_map/dot_general | solution.py:51
  46.3 4.4 %collective-permute-start = (f32[4,96,512]{2,1,0:T(8,128)S(1)}, f32[4,96,512]{2,1,0:T(8,128)S(1)}, u32[]{:S(2)}, u32[]{:S(2)}) collective-permute-start(f32[4,96,512]{2,1,0:T(8,128)S(1)} %fusion), channel_id=1, source_target_pairs={{0,384},{129,1},{258,130},{387,259},{4,388},{133,5},{262,134},{391... | collective-permute-start | bytes 2359304 | tf_op jit(solution)/shard_map/ppermute | solution.py:66
  50.7 2.2 %collective-permute-start.1 = (f32[4,96,512]{2,1,0:T(8,128)S(1)}, f32[4,96,512]{2,1,0:T(8,128)}, u32[]{:S(2)}, u32[]{:S(2)}) collective-permute-start(f32[4,96,512]{2,1,0:T(8,128)S(1)} %fusion), channel_id=1, source_target_pairs={{0,256},{129,385},{258,2},{387,131},{4,260},{133,389},{262,6},{391... | collective-permute-start | bytes 2359304 | tf_op jit(solution)/shard_map/ppermute | solution.py:66
  52.9 2.2 %collective-permute-start.2 = (f32[4,96,512]{2,1,0:T(8,128)S(1)}, f32[4,96,512]{2,1,0:T(8,128)}, u32[]{:S(2)}, u32[]{:S(2)}) collective-permute-start(f32[4,96,512]{2,1,0:T(8,128)S(1)} %fusion), channel_id=1, source_target_pairs={{0,128},{129,257},{258,386},{387,3},{4,132},{133,261},{262,390},{3... | collective-permute-start | bytes 2359304 | tf_op jit(solution)/shard_map/ppermute | solution.py:66
  55.1 4.5 %collective-permute-done = f32[4,96,512]{2,1,0:T(8,128)S(1)} collective-permute-done((f32[4,96,512]{2,1,0:T(8,128)S(1)}, f32[4,96,512]{2,1,0:T(8,128)S(1)}, u32[]{:S(2)}, u32[]{:S(2)}) %collective-permute-start) | collective-permute-done | bytes 786464 | tf_op jit(solution)/shard_map/ppermute | solution.py:66
  59.6 1.3 collective-permute-done.1
  60.9 17.0 %collective-permute-done.2 = f32[4,96,512]{2,1,0:T(8,128)} collective-permute-done((f32[4,96,512]{2,1,0:T(8,128)S(1)}, f32[4,96,512]{2,1,0:T(8,128)}, u32[]{:S(2)}, u32[]{:S(2)}) %collective-permute-start.2) | collective-permute-done | bytes 786464 | tf_op jit(solution)/shard_map/ppermute | solution.py:66
  77.9 1.2 select_select_fusion
  79.2 0.1 iota_compare_fusion
  79.3 0.1 fusion.8
  79.5 0.3 copy-done.5
  79.9 0.2 fusion.11
  80.1 0.1 scatter.15
  80.1 0.1 broadcast_in_dim.2
  80.2 2.4 %scatter_custom_fusion = f32[256,1152]{1,0:T(8,128)S(1)} fusion(f32[256,1152]{1,0:T(8,128)S(1)} %scatter.15, s32[192]{0:T(256)S(1)} %bitcast.56, f32[192,128]{1,0:T(8,128)S(1)} %broadcast_in_dim.2, f32[]{:T(128)} %constant.144, f32[192,1024]{1,0:T(8,128)} %bitcast.46), kind=kCustom, calls=%fused_computation.6 | custom fusion | flops 221184 | bytes 2064388 | tf_op jit(solution)/shard_map/scatter | solution.py:40
  82.6 1.7 all_to_all.8
  84.3 22.3 %all-to-all-start = ((f32[128,2,1152]{2,1,0:T(2,128)}), f32[128,2,1152]{2,1,0:T(2,128)S(1)}, u32[]{:S(2)}, u32[]{:S(2)}) async-start(f32[128,2,1152]{2,1,0:T(2,128)} %all_to_all.8), calls=%async_computation | async-start | bytes 2359296 | tf_op jit(solution)/shard_map/all_to_all | solution.py:42
  106.7 0.7 dynamic-slice_bitcast_fusion
  107.4 60.8 %all-to-all-done = f32[128,2,1152]{2,1,0:T(2,128)S(1)} async-done(((f32[128,2,1152]{2,1,0:T(2,128)}), f32[128,2,1152]{2,1,0:T(2,128)S(1)}, u32[]{:S(2)}, u32[]{:S(2)}) %all-to-all-start) | async-done | bytes 1179680 | tf_op jit(solution)/shard_map/all_to_all | solution.py:42
  168.1 0.8 all_to_all.10
  169.0 0.1 slice_bitcast_fusion
  169.1 0.2 copy.21
  169.3 0.1 copy.20
  169.4 0.9 copy-done.1
  170.4 11.8 %scatter_fusion = f32[12,8,24,128]{3,1,2,0:T(8,128)S(1)} fusion(f32[12,8,24,128]{3,1,2,0:T(8,128)S(1)} %bitcast.41, s32[256]{0:T(256)S(1)} %bitcast.40, f32[256,8,128]{2,1,0:T(8,128)S(1)} %bitcast.43), kind=kCustom, calls=%fused_computation.1 | custom fusion | flops 262144 | bytes 3147776 | tf_op jit(solution)/shard_map/scatter-add | solution.py:72
  182.1 0.0 all-gather.4.cloned.1.call-done
  182.2 10.0 %convolution_subtract_fusion = f32[96,3072]{1,0:T(8,128)} fusion(f32[3072,512]{1,0:T(8,128)} %bitcast.42, f32[12,8,24,128]{3,1,2,0:T(8,128)S(1)} %scatter_fusion, f32[4,96,512]{2,1,0:T(8,128)} %copy-done.2, s32[]{:T(128)S(6)} %select_n.74), kind=kOutput, calls=%fused_computation.2 | convolution fusion | flops 1812234240 | bytes 8847364 | tf_op jit(solution)/shard_map/dot_general | solution.py:76
  (23 shorter events, 0.2 us)
Async XLA Ops:
  7.2 36.5 %copy-start = (f32[512,512]{1,0:T(8,128)S(1)}, f32[512,512]{1,0:T(8,128)}, u32[]{:S(2)}) copy-start(f32[512,512]{1,0:T(8,128)} %param.8) | copy-start | bytes 3145732
  7.2 0.9 copy-start.3
  7.2 175.0 %all-gather.4.cloned.1.call-start = ((), (), s32[]{:S(2)}) async-start(), calls=%async_computation.1 | async-start | bytes 7077888 | tf_op jit(solution)/shard_map/all_gather | solution.py:68
  46.2 60.4 %copy-start.2 = (f32[4,96,512]{2,1,0:T(8,128)}, f32[4,96,512]{2,1,0:T(8,128)S(1)}, u32[]{:S(2)}) copy-start(f32[4,96,512]{2,1,0:T(8,128)S(1)} %fusion) | copy-start | bytes 2359300
  46.3 13.3 %collective-permute-start = (f32[4,96,512]{2,1,0:T(8,128)S(1)}, f32[4,96,512]{2,1,0:T(8,128)S(1)}, u32[]{:S(2)}, u32[]{:S(2)}) collective-permute-start(f32[4,96,512]{2,1,0:T(8,128)S(1)} %fusion), channel_id=1, source_target_pairs={{0,384},{129,1},{258,130},{387,259},{4,388},{133,5},{262,134},{391... | collective-permute-start | bytes 2359304 | tf_op jit(solution)/shard_map/ppermute | solution.py:66
  50.7 10.2 %collective-permute-start.1 = (f32[4,96,512]{2,1,0:T(8,128)S(1)}, f32[4,96,512]{2,1,0:T(8,128)}, u32[]{:S(2)}, u32[]{:S(2)}) collective-permute-start(f32[4,96,512]{2,1,0:T(8,128)S(1)} %fusion), channel_id=1, source_target_pairs={{0,256},{129,385},{258,2},{387,131},{4,260},{133,389},{262,6},{391... | collective-permute-start | bytes 2359304 | tf_op jit(solution)/shard_map/ppermute | solution.py:66
  52.9 25.0 %collective-permute-start.2 = (f32[4,96,512]{2,1,0:T(8,128)S(1)}, f32[4,96,512]{2,1,0:T(8,128)}, u32[]{:S(2)}, u32[]{:S(2)}) collective-permute-start(f32[4,96,512]{2,1,0:T(8,128)S(1)} %fusion), channel_id=1, source_target_pairs={{0,128},{129,257},{258,386},{387,3},{4,132},{133,261},{262,390},{3... | collective-permute-start | bytes 2359304 | tf_op jit(solution)/shard_map/ppermute | solution.py:66
  55.1 24.1 %copy-start.4 = (s32[1,1,192,1]{2,3,1,0:T(1,128)S(1)}, s32[1,1,192,1]{2,3,1,0:T(1,128)}, u32[]{:S(2)}) copy-start(s32[1,1,192,1]{2,3,1,0:T(1,128)} %param.12) | copy-start | bytes 2308
  79.2 0.7 copy-start.5
  84.3 83.8 %all-to-all-start = ((f32[128,2,1152]{2,1,0:T(2,128)}), f32[128,2,1152]{2,1,0:T(2,128)S(1)}, u32[]{:S(2)}, u32[]{:S(2)}) async-start(f32[128,2,1152]{2,1,0:T(2,128)} %all_to_all.8), calls=%async_computation | async-start | bytes 2359296 | tf_op jit(solution)/shard_map/all_to_all | solution.py:42
  169.1 1.3 copy-start.1
Sparse Core Ops, SparseCore 0:
  79.3 58.1 all-gather.3

commit v4 on v3

--- a/solution.py
+++ b/solution.py
@@ -1,6 +1,10 @@
+import functools
+
 import jax
 import jax.numpy as jnp
 from jax import lax
+from jax.experimental import pallas as pl
+from jax.experimental.pallas import tpu as pltpu
 from jax.sharding import Mesh
 from jax.sharding import PartitionSpec as P
 
@@ -8,6 +12,66 @@
 TILE_COLS = 128
 CAP = 2
 ROW_AXES = ("x", "zh", "y", "core")
+MESH_IDS = pl.DeviceIdType.MESH
+
+
+def _ring_gather_kernel(n_zh, n_c, block_ref, out_ref, send_sem, recv_sem):
+    n = n_zh * n_c
+    me = lax.axis_index("zh") * n_c + lax.axis_index("col")
+    right = lax.rem(me + 1, n)
+    left = lax.rem(me + n - 1, n)
+
+    def where(p):
+        return {"zh": p // n_c, "col": lax.rem(p, n_c)}
+
+    barrier = pltpu.get_barrier_semaphore()
+    for other in (left, right):
+        pl.semaphore_signal(barrier, 1, device_id=where(other), device_id_type=MESH_IDS)
+    pl.semaphore_wait(barrier, 2)
+    out_ref[me] = block_ref[...]
+    counts = (n // 2, n - 1 - n // 2)
+    targets = (right, left)
+    signs = (-1, 1)
+    sent = ([], [])
+    for step in range(max(counts)):
+        for d in range(2):
+            if step >= counts[d]:
+                continue
+            slot = lax.rem(me + signs[d] * step + n, n)
+            if step > 0:
+                sent[d][step - 1].wait_recv()
+            src = block_ref if step == 0 else out_ref.at[slot]
+            copy = pltpu.make_async_remote_copy(
+                src_ref=src,
+                dst_ref=out_ref.at[slot],
+                send_sem=send_sem.at[d, step],
+                recv_sem=recv_sem.at[d, step],
+                device_id=where(targets[d]),
+                device_id_type=MESH_IDS,
+            )
+            copy.start()
+            sent[d].append(copy)
+    for d in range(2):
+        if sent[d]:
+            sent[d][-1].wait_recv()
+        for copy in sent[d]:
+            copy.wait_send()
+
+
+def ring_gather(block, n_zh, n_c):
+    n = n_zh * n_c
+    steps = max(n // 2, 1)
+    return pl.pallas_call(
+        functools.partial(_ring_gather_kernel, n_zh, n_c),
+        out_shape=jax.ShapeDtypeStruct((n,) + block.shape, block.dtype),
+        in_specs=[pl.BlockSpec(memory_space=pltpu.VMEM)],
+        out_specs=pl.BlockSpec(memory_space=pltpu.VMEM),
+        scratch_shapes=[
+            pltpu.SemaphoreType.DMA((2, steps)),
+            pltpu.SemaphoreType.DMA((2, steps)),
+        ],
+        compiler_params=pltpu.CompilerParams(collective_id=0, has_side_effects=True),
+    )(block)
 
 
 def per_device(diag_inverse, panel, trailing, agg_vals, agg_dest, agg_tile):
@@ -43,9 +107,9 @@
     got_values = got[:, : tile_values.shape[1]]
     landing = got[:, tile_values.shape[1]].astype(jnp.int32)
 
-    ring_panel = lax.all_gather(panel, ("zh", "col"), axis=0, tiled=False)
     n_zh = lax.axis_size("zh")
     n_c = lax.axis_size("col")
+    ring_panel = ring_gather(panel, n_zh, n_c)
     ring_panel = ring_panel.reshape(n_zh, n_c, local_rows, part_width)
     ring_panel = ring_panel.transpose(0, 2, 1, 3).reshape(n_zh * local_rows, n_c * part_width)
     ring_factor = jnp.dot(

time: 199 us -> 195 us (0.980)
  blocking collectives: 33.9 us -> 0 us
  Pallas kernels: 0 us -> 32.9 us
  local copies, waits for them, and re-layouts: 7.62 us -> 5.08 us
    all_gather x1 -> x0, blocking collectives: 33.9 us -> none  [per_device(): ring_panel = lax.all_gather(panel, ('zh', 'col'), axis=0, tiled=False)]
    pallas_call x0 -> x1, Pallas kernels: none -> 32.9 us  [ring_gather(): pl.pallas_call(functools.partial(_ring_gather_kernel, n_zh, n_c), out_sha...]
where the time goes in v4:
time: 195 us
  waiting for transfers between devices  84.5 us (43%)
  Pallas kernels  32.9 us (17%)
  starting transfers between devices  30.1 us (15%)
  other arithmetic  15.6 us (8%)
  between operations  14.2 us (7%)
  matrix products  12.6 us (6%)
  local copies, waits for them, and re-layouts  5.08 us (3%)
    all_to_all x1, waiting for transfers between devices, per_device(): lax.all_to_all(send, ROW_AXES, split_axis=0, concat_axis=0, tiled=True)  61.5 us
    pallas_call x1, Pallas kernels, ring_gather(): pl.pallas_call(functools.partial(_ring_gather_kernel, n_zh, n_c), out_sha...  32.9 us
    ppermute x3, waiting for transfers between devices, per_device(): moved = lax.ppermute(ring_factor, ('x', 'col'), pairs)  22.9 us
    all_to_all x1, starting transfers between devices, per_device(): lax.all_to_all(send, ROW_AXES, split_axis=0, concat_axis=0, tiled=True)  21.3 us
    scatter-add x1, other arithmetic, per_device(): blocked.at[landing // tile_cols, :, landing % tile_cols, :]  11.4 us
    dot_general x1, matrix products, per_device(): lax.dot_general(own_full, partner, (((1,), (1,)), ((), ())), precision=la...  9.99 us
    ppermute x3, starting transfers between devices, per_device(): moved = lax.ppermute(ring_factor, ('x', 'col'), pairs)  8.8 us
  transfers between devices with their start and end apart: 5, of which 4 were waited for; matrix products, arithmetic and copies ran while one was open for 8% of the time, Pallas kernels for 0%

profile of v4, /device:TPU:1, one launch (start us, length us, event | category | flops | bytes accessed | tf_op | source)
XLA Modules:
  0.0 195.0 jit_solution(10073247962329607859)
XLA Ops:
  7.2 0.0 copy-start
  7.2 0.0 all-gather.3.cloned.1.call-start
  7.2 32.9 %shard_map.77 = f32[16,96,128]{2,1,0:T(8,128)} custom-call(f32[96,128]{1,0:T(8,128)} %block_ref.1), custom_call_target="tpu_custom_call" | custom-call | tf_op jit(solution)/shard_map/pallas_call | solution.py:64
  40.1 2.6 %fusion = f32[4,96,512]{2,1,0:T(8,128)S(1)} fusion(f32[512,512]{1,0:T(8,128)S(1)} %copy-done, f32[4,4,12,8,128]{4,3,2,1,0:T(8,128)} %bitcast.46), kind=kOutput, calls=%fused_computation.4 | convolution fusion | flops 1207959552 | bytes 2621440 | tf_op jit(solution)/shard_map/dot_general | solution.py:115
  42.7 4.4 %collective-permute-start = (f32[4,96,512]{2,1,0:T(8,128)S(1)}, f32[4,96,512]{2,1,0:T(8,128)S(1)}, u32[]{:S(2)}, u32[]{:S(2)}) collective-permute-start(f32[4,96,512]{2,1,0:T(8,128)S(1)} %fusion), channel_id=1, source_target_pairs={{0,384},{129,1},{258,130},{387,259},{4,388},{133,5},{262,134},{391... | collective-permute-start | bytes 2359304 | tf_op jit(solution)/shard_map/ppermute | solution.py:130
  47.1 2.2 %collective-permute-start.1 = (f32[4,96,512]{2,1,0:T(8,128)S(1)}, f32[4,96,512]{2,1,0:T(8,128)}, u32[]{:S(2)}, u32[]{:S(2)}) collective-permute-start(f32[4,96,512]{2,1,0:T(8,128)S(1)} %fusion), channel_id=1, source_target_pairs={{0,256},{129,385},{258,2},{387,131},{4,260},{133,389},{262,6},{391... | collective-permute-start | bytes 2359304 | tf_op jit(solution)/shard_map/ppermute | solution.py:130
  49.3 2.2 %collective-permute-start.2 = (f32[4,96,512]{2,1,0:T(8,128)S(1)}, f32[4,96,512]{2,1,0:T(8,128)}, u32[]{:S(2)}, u32[]{:S(2)}) collective-permute-start(f32[4,96,512]{2,1,0:T(8,128)S(1)} %fusion), channel_id=1, source_target_pairs={{0,128},{129,257},{258,386},{387,3},{4,132},{133,261},{262,390},{3... | collective-permute-start | bytes 2359304 | tf_op jit(solution)/shard_map/ppermute | solution.py:130
  51.5 4.7 %collective-permute-done = f32[4,96,512]{2,1,0:T(8,128)S(1)} collective-permute-done((f32[4,96,512]{2,1,0:T(8,128)S(1)}, f32[4,96,512]{2,1,0:T(8,128)S(1)}, u32[]{:S(2)}, u32[]{:S(2)}) %collective-permute-start) | collective-permute-done | bytes 786464 | tf_op jit(solution)/shard_map/ppermute | solution.py:130
  56.2 1.3 collective-permute-done.1
  57.6 16.9 %collective-permute-done.2 = f32[4,96,512]{2,1,0:T(8,128)} collective-permute-done((f32[4,96,512]{2,1,0:T(8,128)S(1)}, f32[4,96,512]{2,1,0:T(8,128)}, u32[]{:S(2)}, u32[]{:S(2)}) %collective-permute-start.2) | collective-permute-done | bytes 786464 | tf_op jit(solution)/shard_map/ppermute | solution.py:130
  74.4 1.2 select_select_fusion
  75.7 0.0 all-gather.3.cloned.1.call-update
  75.7 0.1 iota_compare_fusion
  75.8 0.1 fusion.10
  76.1 0.3 copy-done.4
  76.4 0.2 fusion.13
  76.6 0.1 scatter.15
  76.7 0.1 broadcast_in_dim.2
  76.7 2.4 %scatter_custom_fusion = f32[256,1152]{1,0:T(8,128)S(1)} fusion(f32[256,1152]{1,0:T(8,128)S(1)} %scatter.15, s32[192]{0:T(256)S(1)} %bitcast.57, f32[192,128]{1,0:T(8,128)S(1)} %broadcast_in_dim.2, f32[]{:T(128)} %constant.144, f32[192,1024]{1,0:T(8,128)} %bitcast.47), kind=kCustom, calls=%fused_computation.6 | custom fusion | flops 221184 | bytes 2064388 | tf_op jit(solution)/shard_map/scatter | solution.py:104
  79.1 1.7 all_to_all.8
  80.9 21.3 %all-to-all-start = ((f32[128,2,1152]{2,1,0:T(2,128)}), f32[128,2,1152]{2,1,0:T(2,128)S(1)}, u32[]{:S(2)}, u32[]{:S(2)}) async-start(f32[128,2,1152]{2,1,0:T(2,128)} %all_to_all.8), calls=%async_computation | async-start | bytes 2359296 | tf_op jit(solution)/shard_map/all_to_all | solution.py:106
  102.2 0.7 dynamic-slice_bitcast_fusion
  102.9 61.5 %all-to-all-done = f32[128,2,1152]{2,1,0:T(2,128)S(1)} async-done(((f32[128,2,1152]{2,1,0:T(2,128)}), f32[128,2,1152]{2,1,0:T(2,128)S(1)}, u32[]{:S(2)}, u32[]{:S(2)}) %all-to-all-start) | async-done | bytes 1179680 | tf_op jit(solution)/shard_map/all_to_all | solution.py:106
  164.4 0.8 all_to_all.10
  165.3 0.1 slice_bitcast_fusion
  165.4 0.0 copy-start.1
  165.4 0.2 copy.22
  165.6 0.1 copy.20
  165.7 0.9 copy-done.1
  166.7 11.4 %scatter_fusion = f32[12,8,24,128]{3,1,2,0:T(8,128)S(1)} fusion(f32[12,8,24,128]{3,1,2,0:T(8,128)S(1)} %bitcast.43, s32[256]{0:T(256)S(1)} %bitcast.42, f32[256,8,128]{2,1,0:T(8,128)S(1)} %bitcast.45), kind=kCustom, calls=%fused_computation.1 | custom fusion | flops 262144 | bytes 3147776 | tf_op jit(solution)/shard_map/scatter-add | solution.py:136
  178.1 0.0 all-gather.3.cloned.1.call-done
  178.1 10.0 %convolution_subtract_fusion = f32[96,3072]{1,0:T(8,128)} fusion(f32[3072,512]{1,0:T(8,128)} %bitcast.44, f32[12,8,24,128]{3,1,2,0:T(8,128)S(1)} %scatter_fusion, f32[4,96,512]{2,1,0:T(8,128)} %copy-done.2, s32[]{:T(128)S(6)} %select_n.74), kind=kOutput, calls=%fused_computation.2 | convolution fusion | flops 1812234240 | bytes 8847364 | tf_op jit(solution)/shard_map/dot_general | solution.py:140
  (19 shorter events, 0.2 us)
Async XLA Ops:
  7.2 32.9 %copy-start = (f32[512,512]{1,0:T(8,128)S(1)}, f32[512,512]{1,0:T(8,128)}, u32[]{:S(2)}) copy-start(f32[512,512]{1,0:T(8,128)} %param.8) | copy-start | bytes 3145732
  7.2 171.0 %all-gather.3.cloned.1.call-start = ((), (), s32[]{:S(2)}) async-start(), calls=%async_computation.1 | async-start | bytes 7077888 | tf_op jit(solution)/shard_map/all_gather | solution.py:132
  42.7 59.5 %copy-start.2 = (f32[4,96,512]{2,1,0:T(8,128)}, f32[4,96,512]{2,1,0:T(8,128)S(1)}, u32[]{:S(2)}) copy-start(f32[4,96,512]{2,1,0:T(8,128)S(1)} %fusion) | copy-start | bytes 2359300
  42.7 13.5 %collective-permute-start = (f32[4,96,512]{2,1,0:T(8,128)S(1)}, f32[4,96,512]{2,1,0:T(8,128)S(1)}, u32[]{:S(2)}, u32[]{:S(2)}) collective-permute-start(f32[4,96,512]{2,1,0:T(8,128)S(1)} %fusion), channel_id=1, source_target_pairs={{0,384},{129,1},{258,130},{387,259},{4,388},{133,5},{262,134},{391... | collective-permute-start | bytes 2359304 | tf_op jit(solution)/shard_map/ppermute | solution.py:130
  47.1 10.5 %collective-permute-start.1 = (f32[4,96,512]{2,1,0:T(8,128)S(1)}, f32[4,96,512]{2,1,0:T(8,128)}, u32[]{:S(2)}, u32[]{:S(2)}) collective-permute-start(f32[4,96,512]{2,1,0:T(8,128)S(1)} %fusion), channel_id=1, source_target_pairs={{0,256},{129,385},{258,2},{387,131},{4,260},{133,389},{262,6},{391... | collective-permute-start | bytes 2359304 | tf_op jit(solution)/shard_map/ppermute | solution.py:130
  49.3 25.1 %collective-permute-start.2 = (f32[4,96,512]{2,1,0:T(8,128)S(1)}, f32[4,96,512]{2,1,0:T(8,128)}, u32[]{:S(2)}, u32[]{:S(2)}) collective-permute-start(f32[4,96,512]{2,1,0:T(8,128)S(1)} %fusion), channel_id=1, source_target_pairs={{0,128},{129,257},{258,386},{387,3},{4,132},{133,261},{262,390},{3... | collective-permute-start | bytes 2359304 | tf_op jit(solution)/shard_map/ppermute | solution.py:130
  51.5 24.2 %copy-start.3 = (s32[1,1,192,1]{2,3,1,0:T(1,128)S(1)}, s32[1,1,192,1]{2,3,1,0:T(1,128)}, u32[]{:S(2)}) copy-start(s32[1,1,192,1]{2,3,1,0:T(1,128)} %param.12) | copy-start | bytes 2308
  75.7 0.7 copy-start.4
  80.9 83.6 %all-to-all-start = ((f32[128,2,1152]{2,1,0:T(2,128)}), f32[128,2,1152]{2,1,0:T(2,128)S(1)}, u32[]{:S(2)}, u32[]{:S(2)}) async-start(f32[128,2,1152]{2,1,0:T(2,128)} %all_to_all.8), calls=%async_computation | async-start | bytes 2359296 | tf_op jit(solution)/shard_map/all_to_all | solution.py:106
  165.4 1.3 copy-start.1
Sparse Core Ops, SparseCore 0:
  75.8 57.7 all-gather.2

commit v5 on v4

--- a/solution.py
+++ b/solution.py
@@ -15,20 +15,56 @@
 MESH_IDS = pl.DeviceIdType.MESH
 
 
-def _ring_gather_kernel(n_zh, n_c, block_ref, out_ref, send_sem, recv_sem):
+def _front_kernel(n_x, n_zh, n_c, block_ref, ring_ref, moved_ref, send_sem, recv_sem,
+                  xsend_sem, xrecv_sem, local_sem):
     n = n_zh * n_c
-    me = lax.axis_index("zh") * n_c + lax.axis_index("col")
+    col = lax.axis_index("col")
+    x = lax.axis_index("x")
+    me = lax.axis_index("zh") * n_c + col
     right = lax.rem(me + 1, n)
     left = lax.rem(me + n - 1, n)
-
-    def where(p):
+    is_source = x == col
+
+    def on_ring(p):
         return {"zh": p // n_c, "col": lax.rem(p, n_c)}
+
+    def x_peer(k):
+        return {"x": lax.rem(x + k, n_x)}
 
     barrier = pltpu.get_barrier_semaphore()
     for other in (left, right):
-        pl.semaphore_signal(barrier, 1, device_id=where(other), device_id_type=MESH_IDS)
-    pl.semaphore_wait(barrier, 2)
-    out_ref[me] = block_ref[...]
+        pl.semaphore_signal(barrier, 1, device_id=on_ring(other), device_id_type=MESH_IDS)
+
+    @pl.when(is_source)
+    def _():
+        for k in range(1, n_x):
+            pl.semaphore_signal(barrier, 1, device_id=x_peer(k), device_id_type=MESH_IDS)
+        pl.semaphore_wait(barrier, 2 + n_x - 1)
+
+    @pl.when(jnp.logical_not(is_source))
+    def _():
+        pl.semaphore_signal(barrier, 1, device_id={"x": col}, device_id_type=MESH_IDS)
+        pl.semaphore_wait(barrier, 3)
+
+    ring_ref[me] = block_ref[...]
+
+    def x_copy(slot, src, k):
+        return pltpu.make_async_remote_copy(
+            src_ref=src,
+            dst_ref=moved_ref.at[slot],
+            send_sem=xsend_sem.at[slot, k - 1],
+            recv_sem=xrecv_sem.at[0],
+            device_id=x_peer(k),
+            device_id_type=MESH_IDS,
+        )
+
+    def forward_x(slot, src):
+        @pl.when(is_source)
+        def _():
+            for k in range(1, n_x):
+                x_copy(slot, src, k).start()
+
+    forward_x(me, block_ref)
     counts = (n // 2, n - 1 - n // 2)
     targets = (right, left)
     signs = (-1, 1)
@@ -40,13 +76,14 @@
             slot = lax.rem(me + signs[d] * step + n, n)
             if step > 0:
                 sent[d][step - 1].wait_recv()
-            src = block_ref if step == 0 else out_ref.at[slot]
+                forward_x(slot, ring_ref.at[slot])
+            src = block_ref if step == 0 else ring_ref.at[slot]
             copy = pltpu.make_async_remote_copy(
                 src_ref=src,
-                dst_ref=out_ref.at[slot],
+                dst_ref=ring_ref.at[slot],
                 send_sem=send_sem.at[d, step],
                 recv_sem=recv_sem.at[d, step],
-                device_id=where(targets[d]),
+                device_id=on_ring(targets[d]),
                 device_id_type=MESH_IDS,
             )
             copy.start()
@@ -54,25 +91,51 @@
     for d in range(2):
         if sent[d]:
             sent[d][-1].wait_recv()
+            last = lax.rem(me + signs[d] * counts[d] + n, n)
+            forward_x(last, ring_ref.at[last])
         for copy in sent[d]:
             copy.wait_send()
 
-
-def ring_gather(block, n_zh, n_c):
+    @pl.when(is_source)
+    def _():
+        for slot in range(n):
+            for k in range(1, n_x):
+                x_copy(slot, ring_ref.at[slot], k).wait_send()
+        local = pltpu.make_async_copy(ring_ref, moved_ref, local_sem.at[0])
+        local.start()
+        local.wait()
+
+    @pl.when(jnp.logical_not(is_source))
+    def _():
+        whole = pltpu.make_async_remote_copy(
+            src_ref=ring_ref,
+            dst_ref=moved_ref,
+            send_sem=local_sem.at[0],
+            recv_sem=xrecv_sem.at[0],
+            device_id={"x": col},
+            device_id_type=MESH_IDS,
+        )
+        whole.wait_recv()
+
+
+def front_exchange(block, n_x, n_zh, n_c):
     n = n_zh * n_c
     steps = max(n // 2, 1)
+    shape = jax.ShapeDtypeStruct((n,) + block.shape, block.dtype)
     return pl.pallas_call(
-        functools.partial(_ring_gather_kernel, n_zh, n_c),
-        out_shape=jax.ShapeDtypeStruct((n,) + block.shape, block.dtype),
+        functools.partial(_front_kernel, n_x, n_zh, n_c),
+        out_shape=(shape, shape),
         in_specs=[pl.BlockSpec(memory_space=pltpu.VMEM)],
-        out_specs=pl.BlockSpec(memory_space=pltpu.VMEM),
+        out_specs=(pl.BlockSpec(memory_space=pltpu.VMEM), pl.BlockSpec(memory_space=pltpu.VMEM)),
         scratch_shapes=[
             pltpu.SemaphoreType.DMA((2, steps)),
             pltpu.SemaphoreType.DMA((2, steps)),
+            pltpu.SemaphoreType.DMA((n, max(n_x - 1, 1))),
+            pltpu.SemaphoreType.DMA((1,)),
+            pltpu.SemaphoreType.DMA((1,)),
         ],
         compiler_params=pltpu.CompilerParams(collective_id=0, has_side_effects=True),
     )(block)
-
 
 def per_device(diag_inverse, panel, trailing, agg_vals, agg_dest, agg_tile):
     row_devices = lax.axis_size(ROW_AXES)
@@ -109,26 +172,29 @@
 
     n_zh = lax.axis_size("zh")
     n_c = lax.axis_size("col")
-    ring_panel = ring_gather(panel, n_zh, n_c)
-    ring_panel = ring_panel.reshape(n_zh, n_c, local_rows, part_width)
-    ring_panel = ring_panel.transpose(0, 2, 1, 3).reshape(n_zh * local_rows, n_c * part_width)
-    ring_factor = jnp.dot(
-        ring_panel,
+    n_x = lax.axis_size("x")
+    ring_panel, moved_panel = front_exchange(panel, n_x, n_zh, n_c)
+
+    def to_rows(blocks):
+        blocks = blocks.reshape(n_zh, n_c, local_rows, part_width).transpose(0, 2, 1, 3)
+        return blocks.reshape(n_zh * local_rows, n_c * part_width)
+
+    own_panel = lax.dynamic_index_in_dim(
+        to_rows(ring_panel).reshape(n_zh, local_rows, panel_width), zh_index, 0, keepdims=False
+    )
+    own_full = jnp.dot(
+        own_panel,
+        diag_inverse.T,
+        precision=lax.Precision.HIGHEST,
+        preferred_element_type=jnp.float32,
+    )
+    own_block = lax.dynamic_slice_in_dim(own_full, col_index * part_width, part_width, 1)
+    chosen = jnp.dot(
+        to_rows(moved_panel),
         diag_inverse.T,
         precision=lax.Precision.HIGHEST,
         preferred_element_type=jnp.float32,
     ).reshape(n_zh, local_rows, panel_width)
-    own_full = lax.dynamic_index_in_dim(ring_factor, zh_index, 0, keepdims=False)
-    own_block = lax.dynamic_slice_in_dim(own_full, col_index * part_width, part_width, 1)
-
-    x_index = lax.axis_index("x")
-    n_x = lax.axis_size("x")
-    shift = (x_index - col_index) % n_x
-    chosen = ring_factor
-    for step in range(1, n_x):
-        pairs = [(c * n_c + c, ((c + step) % n_x) * n_c + c) for c in range(n_c)]
-        moved = lax.ppermute(ring_factor, ("x", "col"), pairs)
-        chosen = jnp.where(shift == step, moved, chosen)
     gathered = lax.all_gather(chosen, ("y", "core"), axis=1, tiled=False)
     partner = gathered.reshape(local_cols, panel_width)
 

time: 195 us -> 173 us (0.89); the launches traced: 195 us -> 170 us
  waiting for transfers between devices: 84.5 us -> 53.8 us
  Pallas kernels: 32.9 us -> 48.2 us
  starting transfers between devices: 30.1 us -> 16.1 us
  local copies, waits for them, and re-layouts: 5.08 us -> 8.79 us
  matrix products: 12.6 us -> 15.4 us
    ppermute x3 -> x0, waiting for transfers between devices: 22.9 us -> none  [per_device(): moved = lax.ppermute(ring_factor, ('x', 'col'), pairs)]
    pallas_call x1, Pallas kernels: 32.9 us -> 48.2 us  [front_exchange(): pl.pallas_call(functools.partial(_front_kernel, n_x, n_zh, n_c), out_shap...]
    ppermute x3 -> x0, starting transfers between devices: 8.8 us -> none  [per_device(): moved = lax.ppermute(ring_factor, ('x', 'col'), pairs)]
    all_to_all x1, waiting for transfers between devices: 61.5 us -> 53.8 us  [per_device(): lax.all_to_all(send, ROW_AXES, split_axis=0, concat_axis=0, tiled=True)]
    all_to_all x1, starting transfers between devices: 21.3 us -> 16 us  [per_device(): lax.all_to_all(send, ROW_AXES, split_axis=0, concat_axis=0, tiled=True)]
    dot_general x1 -> x2, matrix products: 2.57 us -> 5.53 us  [the longest x1 3.48 us: per_device(): jnp.dot(to_rows(moved_panel), diag_inverse.T, precision=lax.Precision.HIG...]
  transfers between devices with their start and end apart: 5 -> 2, of which waited for: 4 -> 1; matrix products, arithmetic and copies ran while one was open for 8% -> 12% of each run, Pallas kernels for 0% -> 0%
where the time goes in v5:
time: 173 us; the launch traced here: 170 us
  waiting for transfers between devices  53.8 us (31%)
  Pallas kernels  48.2 us (28%)
  starting transfers between devices  16.1 us (9%)
  matrix products  15.4 us (9%)
  between operations  14.3 us (8%)
  other arithmetic  13.7 us (8%)
  local copies, waits for them, and re-layouts  8.79 us (5%)
    all_to_all x1, waiting for transfers between devices, per_device(): lax.all_to_all(send, ROW_AXES, split_axis=0, concat_axis=0, tiled=True)  53.8 us
    pallas_call x1, Pallas kernels, front_exchange(): pl.pallas_call(functools.partial(_front_kernel, n_x, n_zh, n_c), out_shap...  48.2 us
    all_to_all x1, starting transfers between devices, per_device(): lax.all_to_all(send, ROW_AXES, split_axis=0, concat_axis=0, tiled=True)  16 us
    scatter-add x1, other arithmetic, per_device(): blocked.at[landing // tile_cols, :, landing % tile_cols, :]  11.4 us
    dot_general x1, matrix products, per_device(): lax.dot_general(own_full, partner, (((1,), (1,)), ((), ())), precision=la...  9.87 us
    dot_general x1, matrix products, per_device(): jnp.dot(to_rows(moved_panel), diag_inverse.T, precision=lax.Precision.HIG...  3.48 us
  transfers between devices with their start and end apart: 2, of which 1 were waited for; matrix products, arithmetic and copies ran while one was open for 12% of the time, Pallas kernels for 0%

profile of v5, /device:TPU:1, one launch (start us, length us, event | category | flops | bytes accessed | tf_op | source)
XLA Modules:
  0.0 170.3 jit_solution(4117206018701902056)
XLA Ops:
  7.2 0.0 copy-start
  7.2 0.0 all-gather.3.cloned.1.call-start
  7.2 48.2 %shard_map.77 = (f32[16,96,128]{2,1,0:T(8,128)}, f32[16,96,128]{2,1,0:T(8,128)}) custom-call(f32[96,128]{1,0:T(8,128)} %block_ref.1), custom_call_target="tpu_custom_call" | custom-call | tf_op jit(solution)/shard_map/pallas_call | solution.py:125
  55.5 0.0 copy-start.6
  55.5 0.0 copy-start.5
  55.5 3.5 %fusion = f32[4,96,512]{2,1,0:T(8,128)} fusion(f32[512,512]{1,0:T(8,128)S(1)} %copy-done, f32[4,4,12,8,128]{4,3,2,1,0:T(8,128)} %bitcast.54), kind=kOutput, calls=%fused_computation.4 | convolution fusion | flops 1207959552 | bytes 2621440 | tf_op jit(solution)/shard_map/dot_general | solution.py:192
  59.0 0.0 all-gather.3.cloned.1.call-update
  59.0 0.1 iota_compare_fusion
  59.1 0.0 copy-start.4
  59.1 0.1 fusion.11
  59.4 0.2 fusion.14
  59.6 0.1 broadcast_in_dim.2
  59.7 0.1 scatter.15
  59.8 0.5 copy-done.4
  60.3 1.8 %scatter_custom_fusion = f32[256,1152]{1,0:T(8,128)S(1)} fusion(f32[256,1152]{1,0:T(8,128)S(1)} %scatter.15, s32[192]{0:T(256)S(1)} %bitcast.64, f32[192,128]{1,0:T(8,128)S(1)} %broadcast_in_dim.2, f32[]{:T(128)} %constant.109, f32[192,1024]{1,0:T(8,128)S(1)} %bitcast.52), kind=kCustom, calls=%fused_computation.6 | custom fusion | flops 221184 | bytes 2064388 | tf_op jit(solution)/shard_map/scatter | solution.py:167
  62.0 1.7 %all_to_all.8 = f32[128,2,1152]{2,1,0:T(2,128)} reshape(f32[256,1152]{1,0:T(8,128)S(1)} %scatter_custom_fusion) | data formatting | bytes 2359296 | tf_op jit(solution)/shard_map/all_to_all | solution.py:169
  63.8 16.0 %all-to-all-start = ((f32[128,2,1152]{2,1,0:T(2,128)}), f32[128,2,1152]{2,1,0:T(2,128)S(1)}, u32[]{:S(2)}, u32[]{:S(2)}) async-start(f32[128,2,1152]{2,1,0:T(2,128)} %all_to_all.8), calls=%async_computation | async-start | bytes 2359296 | tf_op jit(solution)/shard_map/all_to_all | solution.py:169
  79.8 1.6 copy.33
  81.5 1.2 reshape_reshape.3
  82.7 2.1 %fusion.8 = f32[96,512]{1,0:T(8,128)S(1)} fusion(f32[512,512]{1,0:T(8,128)S(1)} %copy-done, f32[4,96,512]{2,1,0:T(8,128)} %reshape_reshape.3, s32[]{:T(128)S(6)} %select_n.44), kind=kOutput, calls=%fused_computation.13 | convolution fusion | flops 301989888 | bytes 1441796 | tf_op jit(solution)/shard_map/dot_general | solution.py:185
  84.7 0.7 copy-done.2
  85.4 0.6 constant_dynamic-slice_fusion
  86.0 53.8 %all-to-all-done = f32[128,2,1152]{2,1,0:T(2,128)S(1)} async-done(((f32[128,2,1152]{2,1,0:T(2,128)}), f32[128,2,1152]{2,1,0:T(2,128)S(1)}, u32[]{:S(2)}, u32[]{:S(2)}) %all-to-all-start) | async-done | bytes 1179680 | tf_op jit(solution)/shard_map/all_to_all | solution.py:169
  139.8 0.8 all_to_all.10
  140.6 0.1 copy.23
  140.7 0.1 slice_bitcast_fusion
  140.8 0.0 copy-start.1
  140.8 0.2 copy.25
  141.1 1.0 copy-done.1
  142.1 11.4 %scatter_fusion = f32[12,8,24,128]{3,1,2,0:T(8,128)S(1)} fusion(f32[12,8,24,128]{3,1,2,0:T(8,128)S(1)} %bitcast.48, s32[256]{0:T(256)S(1)} %bitcast.47, f32[256,8,128]{2,1,0:T(8,128)S(1)} %bitcast.50), kind=kCustom, calls=%fused_computation.1 | custom fusion | flops 262144 | bytes 3147776 | tf_op jit(solution)/shard_map/scatter-add | solution.py:202
  153.5 0.0 all-gather.3.cloned.1.call-done
  153.6 9.9 %convolution_subtract_fusion = f32[96,3072]{1,0:T(8,128)} fusion(f32[96,512]{1,0:T(8,128)S(1)} %copy-done.3, f32[3072,512]{1,0:T(8,128)} %bitcast.49, f32[12,8,24,128]{3,1,2,0:T(8,128)S(1)} %scatter_fusion), kind=kOutput, calls=%fused_computation.2 | convolution fusion | flops 1812234240 | bytes 8847360 | tf_op jit(solution)/shard_map/dot_general | solution.py:206
  (19 shorter events, 0.2 us)
Async XLA Ops:
  7.2 48.3 %copy-start = (f32[512,512]{1,0:T(8,128)S(1)}, f32[512,512]{1,0:T(8,128)}, u32[]{:S(2)}) copy-start(f32[512,512]{1,0:T(8,128)} %param.8) | copy-start | bytes 3145732
  7.2 146.4 %all-gather.3.cloned.1.call-start = ((), (), s32[]{:S(2)}) async-start(), calls=%async_computation.1 | async-start | bytes 7077888 | tf_op jit(solution)/shard_map/all_gather | solution.py:198
  55.5 3.5 %copy-start.6 = (s32[1,1,192]{2,1,0:T(1,128)S(1)}, s32[1,1,192]{2,1,0:T(1,128)}, u32[]{:S(2)}) copy-start(s32[1,1,192]{2,1,0:T(1,128)} %param.13) | copy-start | bytes 2308
  55.5 3.5 %copy-start.5 = (s32[1,1,192,1]{2,3,1,0:T(1,128)S(1)}, s32[1,1,192,1]{2,3,1,0:T(1,128)}, u32[]{:S(2)}) copy-start(s32[1,1,192,1]{2,3,1,0:T(1,128)} %param.12) | copy-start | bytes 2308
  59.1 1.1 copy-start.4
  63.8 76.0 %all-to-all-start = ((f32[128,2,1152]{2,1,0:T(2,128)}), f32[128,2,1152]{2,1,0:T(2,128)S(1)}, u32[]{:S(2)}, u32[]{:S(2)}) async-start(f32[128,2,1152]{2,1,0:T(2,128)} %all_to_all.8), calls=%async_computation | async-start | bytes 2359296 | tf_op jit(solution)/shard_map/all_to_all | solution.py:169
  84.7 0.7 copy-start.2
  140.8 1.3 copy-start.1
  142.1 11.5 %copy-start.3 = (f32[96,512]{1,0:T(8,128)S(1)}, f32[96,512]{1,0:T(8,128)}, u32[]{:S(2)}) copy-start(f32[96,512]{1,0:T(8,128)} %copy-done.2) | copy-start | bytes 589828
Sparse Core Ops, SparseCore 0:
  59.1 53.6 all-gather.2

commit v6 on v5

--- a/solution.py
+++ b/solution.py
@@ -137,6 +137,64 @@
         compiler_params=pltpu.CompilerParams(collective_id=0, has_side_effects=True),
     )(block)
 
+
+def _exchange_kernel(sizes, send_ref, recv_ref, send_sem, recv_sem, local_sem):
+    n = 1
+    me = 0
+    for axis, size in zip(ROW_AXES, sizes):
+        me = me * size + lax.axis_index(axis)
+        n *= size
+
+    def where(d):
+        place = {}
+        for axis, size in reversed(list(zip(ROW_AXES, sizes))):
+            place[axis] = lax.rem(d, size)
+            d = d // size
+        return place
+
+    local = pltpu.make_async_copy(send_ref.at[me], recv_ref.at[me], local_sem.at[0])
+    local.start()
+
+    def body(k, carry):
+        d = lax.rem(me + k, n)
+        pltpu.make_async_remote_copy(
+            src_ref=send_ref.at[d],
+            dst_ref=recv_ref.at[me],
+            send_sem=send_sem.at[0],
+            recv_sem=recv_sem.at[0],
+            device_id=where(d),
+            device_id_type=MESH_IDS,
+        ).start()
+        return carry
+
+    lax.fori_loop(1, n, body, 0)
+    every = pltpu.make_async_remote_copy(
+        src_ref=send_ref.at[pl.ds(0, n - 1)],
+        dst_ref=recv_ref.at[pl.ds(0, n - 1)],
+        send_sem=send_sem.at[0],
+        recv_sem=recv_sem.at[0],
+        device_id=where(lax.rem(me + 1, n)),
+        device_id_type=MESH_IDS,
+    )
+    every.wait_send()
+    every.wait_recv()
+    local.wait()
+
+
+def row_exchange(send, sizes):
+    return pl.pallas_call(
+        functools.partial(_exchange_kernel, sizes),
+        out_shape=jax.ShapeDtypeStruct(send.shape, send.dtype),
+        in_specs=[pl.BlockSpec(memory_space=pl.ANY)],
+        out_specs=pl.BlockSpec(memory_space=pl.ANY),
+        scratch_shapes=[
+            pltpu.SemaphoreType.DMA((1,)),
+            pltpu.SemaphoreType.DMA((1,)),
+            pltpu.SemaphoreType.DMA((1,)),
+        ],
+        compiler_params=pltpu.CompilerParams(has_side_effects=True),
+    )(send)
+
 def per_device(diag_inverse, panel, trailing, agg_vals, agg_dest, agg_tile):
     row_devices = lax.axis_size(ROW_AXES)
     local_rows, local_cols = trailing.shape
@@ -166,7 +224,9 @@
         .at[position]
         .set(payload)
     )
-    got = lax.all_to_all(send, ROW_AXES, split_axis=0, concat_axis=0, tiled=True)
+    row_sizes = tuple(lax.axis_size(axis) for axis in ROW_AXES)
+    slabs = send.reshape(row_devices, CAP * payload.shape[1] // TILE_COLS, TILE_COLS)
+    got = row_exchange(slabs, row_sizes).reshape(send.shape)
     got_values = got[:, : tile_values.shape[1]]
     landing = got[:, tile_values.shape[1]].astype(jnp.int32)
 

time: 173 us -> 180 us (1.040)
  Pallas kernels: 48.2 us -> 125 us
  waiting for transfers between devices: 53.8 us -> 0.02 us
  starting transfers between devices: 16.1 us -> 0.04 us
    pallas_call x0 -> x1, Pallas kernels: none -> 77.1 us  [row_exchange(): pl.pallas_call(functools.partial(_exchange_kernel, sizes), out_shape=jax....]
    all_to_all x1 -> x0, waiting for transfers between devices: 53.8 us -> none  [per_device(): lax.all_to_all(send, ROW_AXES, split_axis=0, concat_axis=0, tiled=True)]
    all_to_all x1 -> x0, starting transfers between devices: 16 us -> none  [per_device(): lax.all_to_all(send, ROW_AXES, split_axis=0, concat_axis=0, tiled=True)]
    reshape x0 -> x2, local copies, waits for them, and re-layouts: none -> 3.08 us  [the longest x1 1.6 us: per_device(): got = row_exchange(slabs, row_sizes).reshape(send.shape)]
    all_to_all x2 -> x0, local copies, waits for them, and re-layouts: 2.52 us -> none  [per_device(): lax.all_to_all(send, ROW_AXES, split_axis=0, concat_axis=0, tiled=True)]
  transfers between devices with their start and end apart: 2 -> 1, of which waited for: 1 -> 0; matrix products, arithmetic and copies ran while one was open for 12% -> 13% of each run, Pallas kernels for 0% -> 43%
where the time goes in v6:
time: 180 us; the launch traced here: 178 us
  Pallas kernels  125 us (69%)
  matrix products  15.4 us (9%)
  between operations  14.3 us (8%)
  other arithmetic  13.8 us (8%)
  local copies, waits for them, and re-layouts  9.57 us (5%)
    pallas_call x1, Pallas kernels, row_exchange(): pl.pallas_call(functools.partial(_exchange_kernel, sizes), out_shape=jax....  77.1 us
    pallas_call x1, Pallas kernels, front_exchange(): pl.pallas_call(functools.partial(_front_kernel, n_x, n_zh, n_c), out_shap...  48.2 us
    scatter-add x1, other arithmetic, per_device(): blocked.at[landing // tile_cols, :, landing % tile_cols, :]  11.5 us
    dot_general x1, matrix products, per_device(): lax.dot_general(own_full, partner, (((1,), (1,)), ((), ())), precision=la...  9.87 us
  transfers between devices with their start and end apart: 1, of which 0 were waited for; matrix products, arithmetic and copies ran while one was open for 13% of the time, Pallas kernels for 43%

profile of v6, /device:TPU:1, one launch (start us, length us, event | category | flops | bytes accessed | tf_op | source)
XLA Modules:
  0.0 178.4 jit_solution(1010814737815745108)
XLA Ops:
  7.2 0.0 copy-start
  7.2 0.0 all-gather.3.cloned.1.call-start
  7.2 48.2 %shard_map.78 = (f32[16,96,128]{2,1,0:T(8,128)}, f32[16,96,128]{2,1,0:T(8,128)}) custom-call(f32[96,128]{1,0:T(8,128)} %block_ref.1), custom_call_target="tpu_custom_call" | custom-call | tf_op jit(solution)/shard_map/pallas_call | solution.py:125
  55.5 0.0 copy-done
  55.5 0.0 copy-start.5
  55.5 0.0 copy-start.4
  55.5 3.5 %fusion = f32[4,96,512]{2,1,0:T(8,128)} fusion(f32[512,512]{1,0:T(8,128)S(1)} %copy-done, f32[4,4,12,8,128]{4,3,2,1,0:T(8,128)} %bitcast.54), kind=kOutput, calls=%fused_computation.4 | convolution fusion | flops 1207959552 | bytes 2621440 | tf_op jit(solution)/shard_map/dot_general | solution.py:252
  59.0 0.0 all-gather.3.cloned.1.call-update
  59.0 0.0 copy-done.5
  59.0 0.0 copy-done.4
  59.0 0.1 iota_compare_fusion
  59.1 0.0 copy-start.2
  59.2 0.1 fusion.11
  59.4 0.2 fusion.14
  59.6 0.1 broadcast_in_dim.2
  59.7 0.1 scatter.15
  59.8 0.5 copy-done.2
  60.3 1.8 %scatter_custom_fusion = f32[256,1152]{1,0:T(8,128)S(1)} fusion(f32[256,1152]{1,0:T(8,128)S(1)} %scatter.15, s32[192]{0:T(256)S(1)} %bitcast.64, f32[192,128]{1,0:T(8,128)S(1)} %broadcast_in_dim.2, f32[]{:T(128)} %constant.109, f32[192,1024]{1,0:T(8,128)S(1)} %bitcast.52), kind=kCustom, calls=%fused_computation.6 | custom fusion | flops 221184 | bytes 2064388 | tf_op jit(solution)/shard_map/scatter | solution.py:225
  62.1 1.5 reshape.115.send_ref
  63.5 77.1 %shard_map.77 = f32[128,18,128]{2,1,0:T(8,128)} custom-call(f32[128,18,128]{2,1,0:T(8,128)} %reshape.115.send_ref), custom_call_target="tpu_custom_call" | custom-call | tf_op jit(solution)/shard_map/pallas_call | solution.py:185
  140.6 1.6 reshape.116
  142.3 0.1 copy.18
  142.3 0.1 slice_bitcast_fusion
  142.5 0.0 copy-start.3
  142.5 0.2 copy.20
  142.7 0.9 copy-done.3
  143.6 1.4 copy.28
  145.0 2.4 %reshape_reshape.3 = f32[4,96,512]{2,1,0:T(8,128)} reshape(f32[4,96,4,128]{3,2,1,0:T(4,128)} %bitcast.51) | data formatting | bytes 1572864 | tf_op jit(solution)/shard_map/reshape;reshape | solution.py:243
  147.5 11.5 %scatter_fusion = f32[12,8,24,128]{3,1,2,0:T(8,128)S(1)} fusion(f32[12,8,24,128]{3,1,2,0:T(8,128)S(1)} %bitcast.48, s32[256]{0:T(256)S(1)} %bitcast.47, f32[256,8,128]{2,1,0:T(8,128)S(1)} %bitcast.50), kind=kCustom, calls=%fused_computation.1 | custom fusion | flops 262144 | bytes 3147776 | tf_op jit(solution)/shard_map/scatter-add | solution.py:262
  159.0 2.1 %fusion.8 = f32[96,512]{1,0:T(8,128)S(1)} fusion(f32[512,512]{1,0:T(8,128)S(1)} %copy-done, f32[4,96,512]{2,1,0:T(8,128)} %reshape_reshape.3, s32[]{:T(128)S(6)} %select_n.44), kind=kOutput, calls=%fused_computation.13 | convolution fusion | flops 301989888 | bytes 1441796 | tf_op jit(solution)/shard_map/dot_general | solution.py:245
  161.0 0.6 constant_dynamic-slice_fusion
  161.7 9.9 %convolution_subtract_fusion = f32[96,3072]{1,0:T(8,128)} fusion(f32[96,512]{1,0:T(8,128)S(1)} %fusion.8, f32[3072,512]{1,0:T(8,128)} %bitcast.49, f32[12,8,24,128]{3,1,2,0:T(8,128)S(1)} %scatter_fusion), kind=kOutput, calls=%fused_computation.2 | convolution fusion | flops 1812234240 | bytes 8847360 | tf_op jit(solution)/shard_map/dot_general | solution.py:266
  (16 shorter events, 0.1 us)
Async XLA Ops:
  7.2 48.3 %copy-start = (f32[512,512]{1,0:T(8,128)S(1)}, f32[512,512]{1,0:T(8,128)}, u32[]{:S(2)}) copy-start(f32[512,512]{1,0:T(8,128)} %param.8) | copy-start | bytes 3145732
  7.2 154.5 %all-gather.3.cloned.1.call-start = ((), (), s32[]{:S(2)}) async-start(), calls=%async_computation | async-start | bytes 7077888 | tf_op jit(solution)/shard_map/all_gather | solution.py:258
  55.5 3.5 %copy-start.5 = (s32[1,1,192]{2,1,0:T(1,128)S(1)}, s32[1,1,192]{2,1,0:T(1,128)}, u32[]{:S(2)}) copy-start(s32[1,1,192]{2,1,0:T(1,128)} %param.13) | copy-start | bytes 2308
  55.5 3.5 %copy-start.4 = (s32[1,1,192,1]{2,3,1,0:T(1,128)S(1)}, s32[1,1,192,1]{2,3,1,0:T(1,128)}, u32[]{:S(2)}) copy-start(s32[1,1,192,1]{2,3,1,0:T(1,128)} %param.12) | copy-start | bytes 2308
  59.1 1.1 copy-start.2
  142.5 1.1 copy-start.3
  145.0 2.5 %copy-start.1 = (f32[96,3072]{1,0:T(8,128)S(1)}, f32[96,3072]{1,0:T(8,128)}, u32[]{:S(2)}) copy-start(f32[96,3072]{1,0:T(8,128)} %param.10) | copy-start | bytes 3538948
Sparse Core Ops, SparseCore 0:
  59.1 58.8 all-gather.2

commit v7 on v5

--- a/solution.py
+++ b/solution.py
@@ -15,8 +15,8 @@
 MESH_IDS = pl.DeviceIdType.MESH
 
 
-def _front_kernel(n_x, n_zh, n_c, block_ref, ring_ref, moved_ref, send_sem, recv_sem,
-                  xsend_sem, xrecv_sem, local_sem):
+def _front_kernel(n_x, n_zh, n_c, sizes, block_ref, slab_ref, ring_ref, moved_ref, got_ref,
+                  send_sem, recv_sem, xsend_sem, xrecv_sem, local_sem, agg_sem):
     n = n_zh * n_c
     col = lax.axis_index("col")
     x = lax.axis_index("x")
@@ -31,20 +31,57 @@
     def x_peer(k):
         return {"x": lax.rem(x + k, n_x)}
 
+    n_rows = 1
+    row_me = 0
+    for axis, size in zip(ROW_AXES, sizes):
+        row_me = row_me * size + lax.axis_index(axis)
+        n_rows *= size
+
+    def on_row(d):
+        place = {}
+        for axis, size in reversed(list(zip(ROW_AXES, sizes))):
+            place[axis] = lax.rem(d, size)
+            d = d // size
+        return place
+
     barrier = pltpu.get_barrier_semaphore()
     for other in (left, right):
         pl.semaphore_signal(barrier, 1, device_id=on_ring(other), device_id_type=MESH_IDS)
 
+    def greet(k, carry):
+        d = lax.rem(row_me + k, n_rows)
+        pl.semaphore_signal(barrier, 1, device_id=on_row(d), device_id_type=MESH_IDS)
+        return carry
+
+    lax.fori_loop(1, n_rows, greet, 0)
+
     @pl.when(is_source)
     def _():
         for k in range(1, n_x):
             pl.semaphore_signal(barrier, 1, device_id=x_peer(k), device_id_type=MESH_IDS)
-        pl.semaphore_wait(barrier, 2 + n_x - 1)
+        pl.semaphore_wait(barrier, 2 + n_x - 1 + n_rows - 1)
 
     @pl.when(jnp.logical_not(is_source))
     def _():
         pl.semaphore_signal(barrier, 1, device_id={"x": col}, device_id_type=MESH_IDS)
-        pl.semaphore_wait(barrier, 3)
+        pl.semaphore_wait(barrier, 3 + n_rows - 1)
+
+    own_slab = pltpu.make_async_copy(slab_ref.at[row_me], got_ref.at[row_me], local_sem.at[1])
+    own_slab.start()
+
+    def post(k, carry):
+        d = lax.rem(row_me + k, n_rows)
+        pltpu.make_async_remote_copy(
+            src_ref=slab_ref.at[d],
+            dst_ref=got_ref.at[row_me],
+            send_sem=agg_sem.at[0],
+            recv_sem=agg_sem.at[1],
+            device_id=on_row(d),
+            device_id_type=MESH_IDS,
+        ).start()
+        return carry
+
+    lax.fori_loop(1, n_rows, post, 0)
 
     ring_ref[me] = block_ref[...]
 
@@ -117,25 +154,41 @@
         )
         whole.wait_recv()
 
-
-def front_exchange(block, n_x, n_zh, n_c):
+    every = pltpu.make_async_remote_copy(
+        src_ref=slab_ref.at[pl.ds(0, n_rows - 1)],
+        dst_ref=got_ref.at[pl.ds(0, n_rows - 1)],
+        send_sem=agg_sem.at[0],
+        recv_sem=agg_sem.at[1],
+        device_id=on_row(lax.rem(row_me + 1, n_rows)),
+        device_id_type=MESH_IDS,
+    )
+    every.wait_send()
+    every.wait_recv()
+    own_slab.wait()
+
+
+def front_exchange(block, slabs, n_x, n_zh, n_c, sizes):
     n = n_zh * n_c
     steps = max(n // 2, 1)
     shape = jax.ShapeDtypeStruct((n,) + block.shape, block.dtype)
+    vmem = pl.BlockSpec(memory_space=pltpu.VMEM)
+    anywhere = pl.BlockSpec(memory_space=pl.ANY)
     return pl.pallas_call(
-        functools.partial(_front_kernel, n_x, n_zh, n_c),
-        out_shape=(shape, shape),
-        in_specs=[pl.BlockSpec(memory_space=pltpu.VMEM)],
-        out_specs=(pl.BlockSpec(memory_space=pltpu.VMEM), pl.BlockSpec(memory_space=pltpu.VMEM)),
+        functools.partial(_front_kernel, n_x, n_zh, n_c, sizes),
+        out_shape=(shape, shape, jax.ShapeDtypeStruct(slabs.shape, slabs.dtype)),
+        in_specs=[vmem, anywhere],
+        out_specs=(vmem, vmem, anywhere),
         scratch_shapes=[
             pltpu.SemaphoreType.DMA((2, steps)),
             pltpu.SemaphoreType.DMA((2, steps)),
             pltpu.SemaphoreType.DMA((n, max(n_x - 1, 1))),
             pltpu.SemaphoreType.DMA((1,)),
-            pltpu.SemaphoreType.DMA((1,)),
+            pltpu.SemaphoreType.DMA((2,)),
+            pltpu.SemaphoreType.DMA((2,)),
         ],
         compiler_params=pltpu.CompilerParams(collective_id=0, has_side_effects=True),
-    )(block)
+    )(block, slabs)
+
 
 def per_device(diag_inverse, panel, trailing, agg_vals, agg_dest, agg_tile):
     row_devices = lax.axis_size(ROW_AXES)
@@ -166,14 +219,16 @@
         .at[position]
         .set(payload)
     )
-    got = lax.all_to_all(send, ROW_AXES, split_axis=0, concat_axis=0, tiled=True)
-    got_values = got[:, : tile_values.shape[1]]
-    landing = got[:, tile_values.shape[1]].astype(jnp.int32)
+    row_sizes = tuple(lax.axis_size(axis) for axis in ROW_AXES)
+    slabs = send.reshape(row_devices, CAP * payload.shape[1] // TILE_COLS, TILE_COLS)
 
     n_zh = lax.axis_size("zh")
     n_c = lax.axis_size("col")
     n_x = lax.axis_size("x")
-    ring_panel, moved_panel = front_exchange(panel, n_x, n_zh, n_c)
+    ring_panel, moved_panel, got = front_exchange(panel, slabs, n_x, n_zh, n_c, row_sizes)
+    got = got.reshape(send.shape)
+    got_values = got[:, : tile_values.shape[1]]
+    landing = got[:, tile_values.shape[1]].astype(jnp.int32)
 
     def to_rows(blocks):
         blocks = blocks.reshape(n_zh, n_c, local_rows, part_width).transpose(0, 2, 1, 3)

time: 173 us -> 186 us (1.075); the launches traced: 170 us -> 185 us
  Pallas kernels: 48.2 us -> 109 us
  waiting for transfers between devices: 53.8 us -> 24.2 us
  starting transfers between devices: 16.1 us -> 0.04 us
    pallas_call x1, Pallas kernels: 48.2 us -> 109 us  [front_exchange(): pl.pallas_call(functools.partial(_front_kernel, n_x, n_zh, n_c, sizes), o...]
    all_to_all x1 -> x0, waiting for transfers between devices: 53.8 us -> none  [per_device(): lax.all_to_all(send, ROW_AXES, split_axis=0, concat_axis=0, tiled=True)]
    all_gather x1, waiting for transfers between devices: 0.02 us -> 24.2 us  [per_device(): gathered = lax.all_gather(chosen, ('y', 'core'), axis=1, tiled=False)]
    all_to_all x1 -> x0, starting transfers between devices: 16 us -> none  [per_device(): lax.all_to_all(send, ROW_AXES, split_axis=0, concat_axis=0, tiled=True)]
    reshape x0 -> x2, local copies, waits for them, and re-layouts: none -> 3.08 us  [the longest x1 1.6 us: per_device(): got = got.reshape(send.shape)]
    all_to_all x2 -> x0, local copies, waits for them, and re-layouts: 2.52 us -> none  [per_device(): lax.all_to_all(send, ROW_AXES, split_axis=0, concat_axis=0, tiled=True)]
  transfers between devices with their start and end apart: 2 -> 1, of which waited for: 1 -> 1; matrix products, arithmetic and copies ran while one was open for 12% -> 10% of each run, Pallas kernels for 0% -> 0%
where the time goes in v7:
time: 186 us; the launch traced here: 185 us
  Pallas kernels  109 us (59%)
  waiting for transfers between devices  24.2 us (13%)
  matrix products  15.5 us (8%)
  between operations  14.3 us (8%)
  other arithmetic  13.8 us (7%)
  local copies, waits for them, and re-layouts  8.14 us (4%)
    pallas_call x1, Pallas kernels, front_exchange(): pl.pallas_call(functools.partial(_front_kernel, n_x, n_zh, n_c, sizes), o...  109 us
    all_gather x1, waiting for transfers between devices, per_device(): gathered = lax.all_gather(chosen, ('y', 'core'), axis=1, tiled=False)  24.2 us
    scatter-add x1, other arithmetic, per_device(): blocked.at[landing // tile_cols, :, landing % tile_cols, :]  11.4 us
    dot_general x1, matrix products, per_device(): lax.dot_general(own_full, partner, (((1,), (1,)), ((), ())), precision=la...  9.87 us
  transfers between devices with their start and end apart: 1, of which 1 were waited for; matrix products, arithmetic and copies ran while one was open for 10% of the time, Pallas kernels for 0%

profile of v7, /device:TPU:1, one launch (start us, length us, event | category | flops | bytes accessed | tf_op | source)
XLA Modules:
  0.0 185.3 jit_solution(14249820388083474183)
XLA Ops:
  7.2 0.0 copy-start
  7.2 0.0 copy-start.4
  7.2 0.0 copy-start.5
  7.2 0.0 all-gather.3.cloned.1.call-start
  7.2 0.7 copy-done.4
  7.9 0.1 iota_compare_fusion
  8.0 0.0 copy-start.2
  8.1 0.1 fusion.11
  8.3 0.2 fusion.14
  8.5 0.0 copy-done.5
  8.6 0.1 scatter.15
  8.6 0.1 broadcast_in_dim.2
  8.7 0.5 copy-done.2
  9.2 1.8 scatter_custom_fusion
  11.0 1.5 reshape.115.slab_ref
  12.5 109.4 %shard_map.77 = (f32[16,96,128]{2,1,0:T(8,128)}, f32[16,96,128]{2,1,0:T(8,128)}, f32[128,18,128]{2,1,0:T(8,128)}) custom-call(f32[96,128]{1,0:T(8,128)} %block_ref.1, f32[128,18,128]{2,1,0:T(8,128)} %reshape.115.slab_ref), custom_call_target="tpu_custom_call" | custom-call | tf_op jit(solution)/shard_map/pallas_call | solution.py:176
  121.8 0.0 copy-done
  121.8 3.6 %fusion = f32[4,96,512]{2,1,0:T(8,128)} fusion(f32[512,512]{1,0:T(8,128)S(1)} %copy-done, f32[4,4,12,8,128]{4,3,2,1,0:T(8,128)} %bitcast.53), kind=kOutput, calls=%fused_computation.4 | convolution fusion | flops 1207959552 | bytes 2621440 | tf_op jit(solution)/shard_map/dot_general | solution.py:247
  125.5 0.0 all-gather.3.cloned.1.call-update
  125.5 0.5 copy.28
  126.0 1.2 reshape_reshape.3
  127.2 1.6 reshape.116
  128.8 0.1 slice_bitcast_fusion
  129.0 0.0 copy-start.1
  129.0 0.2 copy.20
  129.2 0.1 copy.18
  129.3 0.9 copy-done.1
  130.2 11.4 %scatter_fusion = f32[12,8,24,128]{3,1,2,0:T(8,128)S(1)} fusion(f32[12,8,24,128]{3,1,2,0:T(8,128)S(1)} %bitcast.47, s32[256]{0:T(256)S(1)} %bitcast.46, f32[256,8,128]{2,1,0:T(8,128)S(1)} %bitcast.49), kind=kCustom, calls=%fused_computation.1 | custom fusion | flops 262144 | bytes 3147776 | tf_op jit(solution)/shard_map/scatter-add | solution.py:257
  141.7 2.1 %fusion.8 = f32[96,512]{1,0:T(8,128)S(1)} fusion(f32[512,512]{1,0:T(8,128)S(1)} %copy-done, f32[4,96,512]{2,1,0:T(8,128)} %reshape_reshape.3, s32[]{:T(128)S(6)} %select_n.44), kind=kOutput, calls=%fused_computation.13 | convolution fusion | flops 301989888 | bytes 1441796 | tf_op jit(solution)/shard_map/dot_general | solution.py:240
  143.8 0.6 constant_dynamic-slice_fusion
  144.4 24.2 %all-gather.3.cloned.1.call-done = f32[4,768,512]{2,1,0:T(8,128)} async-done(((f32[4,96,512]{2,1,0:T(8,128)}), f32[4,768,512]{2,1,0:T(8,128)}) %all-gather.3.cloned.1.call-update) | async-done | bytes 6291472 | tf_op jit(solution)/shard_map/all_gather | solution.py:253
  168.6 9.9 %convolution_subtract_fusion = f32[96,3072]{1,0:T(8,128)} fusion(f32[96,512]{1,0:T(8,128)S(1)} %fusion.8, f32[3072,512]{1,0:T(8,128)} %bitcast.48, f32[12,8,24,128]{3,1,2,0:T(8,128)S(1)} %scatter_fusion), kind=kOutput, calls=%fused_computation.2 | convolution fusion | flops 1812234240 | bytes 8847360 | tf_op jit(solution)/shard_map/dot_general | solution.py:261
  (15 shorter events, 0.2 us)
Async XLA Ops:
  7.2 114.7 %copy-start = (f32[512,512]{1,0:T(8,128)S(1)}, f32[512,512]{1,0:T(8,128)}, u32[]{:S(2)}) copy-start(f32[512,512]{1,0:T(8,128)} %param.8) | copy-start | bytes 3145732
  7.2 0.8 copy-start.4
  7.2 1.3 copy-start.5
  7.2 161.4 %all-gather.3.cloned.1.call-start = ((), (), s32[]{:S(2)}) async-start(), calls=%async_computation | async-start | bytes 7077888 | tf_op jit(solution)/shard_map/all_gather | solution.py:253
  8.0 1.1 copy-start.2
  121.8 3.7 %copy-start.3 = (f32[16,96,128]{2,1,0:T(8,128)S(1)}, f32[16,96,128]{2,1,0:T(8,128)}, u32[]{:S(2)}) copy-start(f32[16,96,128]{2,1,0:T(8,128)} %get-tuple-element.18) | copy-start | bytes 2359300
  129.0 1.3 copy-start.1
Sparse Core Ops, SparseCore 0:
  125.6 42.9 all-gather.2

commit v8 on v5

--- a/solution.py
+++ b/solution.py
@@ -198,19 +198,18 @@
     gathered = lax.all_gather(chosen, ("y", "core"), axis=1, tiled=False)
     partner = gathered.reshape(local_cols, panel_width)
 
-    blocked = trailing.reshape(tile_rows, TILE_ROWS, tile_cols, TILE_COLS)
-    blocked = blocked.at[landing // tile_cols, :, landing % tile_cols, :].add(
-        got_values.reshape(-1, TILE_ROWS, TILE_COLS), mode="drop"
-    )
-    assembled = blocked.reshape(local_rows, local_cols)
     product = lax.dot_general(
         own_full,
         partner,
         (((1,), (1,)), ((), ())),
-        precision=lax.Precision.HIGHEST,
+        precision=lax.Precision.HIGH,
         preferred_element_type=jnp.float32,
     )
-    updated = assembled - product
+    reduced = (trailing - product).reshape(tile_rows, TILE_ROWS, tile_cols, TILE_COLS)
+    reduced = reduced.at[landing // tile_cols, :, landing % tile_cols, :].add(
+        got_values.reshape(-1, TILE_ROWS, TILE_COLS), mode="drop"
+    )
+    updated = reduced.reshape(local_rows, local_cols)
     return (updated, own_block)
 
 

time: 173 us -> 169 us (0.977)
  matrix products: 15.4 us -> 11.6 us
    dot_general x1, matrix products: 9.87 us -> 6.11 us  [per_device(): lax.dot_general(own_full, partner, (((1,), (1,)), ((), ())), precision=la...]
  transfers between devices with their start and end apart: 2 -> 2, of which waited for: 1 -> 1; matrix products, arithmetic and copies ran while one was open for 12% -> 5% of each run, Pallas kernels for 0% -> 0%
where the time goes in v8:
time: 169 us; the launch traced here: 167 us
  waiting for transfers between devices  53.8 us (32%)
  Pallas kernels  48.2 us (29%)
  starting transfers between devices  16.1 us (10%)
  between operations  14.2 us (8%)
  other arithmetic  13.8 us (8%)
  matrix products  11.6 us (7%)
  local copies, waits for them, and re-layouts  9.33 us (6%)
    all_to_all x1, waiting for transfers between devices, per_device(): lax.all_to_all(send, ROW_AXES, split_axis=0, concat_axis=0, tiled=True)  53.8 us
    pallas_call x1, Pallas kernels, front_exchange(): pl.pallas_call(functools.partial(_front_kernel, n_x, n_zh, n_c), out_shap...  48.2 us
    all_to_all x1, starting transfers between devices, per_device(): lax.all_to_all(send, ROW_AXES, split_axis=0, concat_axis=0, tiled=True)  16 us
    scatter-add x1, other arithmetic, per_device(): reduced.at[landing // tile_cols, :, landing % tile_cols, :]  11.5 us
    dot_general x1, matrix products, per_device(): lax.dot_general(own_full, partner, (((1,), (1,)), ((), ())), precision=la...  6.11 us
    dot_general x1, matrix products, per_device(): jnp.dot(to_rows(moved_panel), diag_inverse.T, precision=lax.Precision.HIG...  3.47 us
  transfers between devices with their start and end apart: 2, of which 1 were waited for; matrix products, arithmetic and copies ran while one was open for 5% of the time, Pallas kernels for 0%

profile of v8, /device:TPU:1, one launch (start us, length us, event | category | flops | bytes accessed | tf_op | source)
XLA Modules:
  0.0 167.1 jit_solution(9368772684166083999)
XLA Ops:
  7.2 0.0 copy-start
  7.2 0.0 all-gather.3.cloned.1.call-start
  7.2 48.2 %shard_map.77 = (f32[16,96,128]{2,1,0:T(8,128)}, f32[16,96,128]{2,1,0:T(8,128)}) custom-call(f32[96,128]{1,0:T(8,128)} %block_ref.1), custom_call_target="tpu_custom_call" | custom-call | tf_op jit(solution)/shard_map/pallas_call | solution.py:125
  55.5 0.0 copy-start.5
  55.5 3.5 %fusion.1 = f32[4,96,512]{2,1,0:T(8,128)} fusion(f32[512,512]{1,0:T(8,128)S(1)} %copy-done, f32[4,4,12,8,128]{4,3,2,1,0:T(8,128)} %bitcast.53), kind=kOutput, calls=%fused_computation.5 | convolution fusion | flops 1207959552 | bytes 2621440 | tf_op jit(solution)/shard_map/dot_general | solution.py:192
  59.0 0.0 all-gather.3.cloned.1.call-update
  59.0 0.1 iota_compare_fusion
  59.1 0.0 copy-start.4
  59.1 0.1 fusion.12
  59.3 0.3 copy-done.6
  59.6 0.2 fusion.15
  59.8 0.1 scatter.15
  59.9 0.1 broadcast_in_dim.2
  60.0 0.2 copy-done.4
  60.2 1.8 %scatter_custom_fusion = f32[256,1152]{1,0:T(8,128)S(1)} fusion(f32[256,1152]{1,0:T(8,128)S(1)} %scatter.15, s32[192]{0:T(256)S(1)} %bitcast.63, f32[192,128]{1,0:T(8,128)S(1)} %broadcast_in_dim.2, f32[]{:T(128)} %constant.109, f32[192,1024]{1,0:T(8,128)S(1)} %bitcast.51), kind=kCustom, calls=%fused_computation.7 | custom fusion | flops 221184 | bytes 2064388 | tf_op jit(solution)/shard_map/scatter | solution.py:167
  62.0 1.7 %all_to_all.8 = f32[128,2,1152]{2,1,0:T(2,128)} reshape(f32[256,1152]{1,0:T(8,128)S(1)} %scatter_custom_fusion) | data formatting | bytes 2359296 | tf_op jit(solution)/shard_map/all_to_all | solution.py:169
  63.7 16.0 %all-to-all-start = ((f32[128,2,1152]{2,1,0:T(2,128)}), f32[128,2,1152]{2,1,0:T(2,128)S(1)}, u32[]{:S(2)}, u32[]{:S(2)}) async-start(f32[128,2,1152]{2,1,0:T(2,128)} %all_to_all.8), calls=%async_computation | async-start | bytes 2359296 | tf_op jit(solution)/shard_map/all_to_all | solution.py:169
  79.8 1.6 copy.33
  81.4 1.2 reshape_reshape.3
  82.6 2.1 %fusion.9 = f32[96,512]{1,0:T(8,128)S(1)} fusion(f32[512,512]{1,0:T(8,128)S(1)} %copy-done, f32[4,96,512]{2,1,0:T(8,128)} %reshape_reshape.3, s32[]{:T(128)S(6)} %select_n.39), kind=kOutput, calls=%fused_computation.14 | convolution fusion | flops 301989888 | bytes 1441796 | tf_op jit(solution)/shard_map/dot_general | solution.py:185
  84.7 0.7 copy-done.2
  85.4 0.6 constant_dynamic-slice_fusion
  86.0 53.8 %all-to-all-done = f32[128,2,1152]{2,1,0:T(2,128)S(1)} async-done(((f32[128,2,1152]{2,1,0:T(2,128)}), f32[128,2,1152]{2,1,0:T(2,128)S(1)}, u32[]{:S(2)}, u32[]{:S(2)}) %all-to-all-start) | async-done | bytes 1179680 | tf_op jit(solution)/shard_map/all_to_all | solution.py:169
  139.7 0.8 all_to_all.10
  140.6 0.1 slice_bitcast_fusion
  140.7 0.2 copy.25
  140.9 0.1 copy.23
  141.0 0.0 all-gather.3.cloned.1.call-done
  141.1 0.6 copy-done.3
  141.6 6.1 %fusion = f32[12,8,24,128]{3,1,2,0:T(8,128)S(1)} fusion(f32[96,3072]{1,0:T(8,128)} %param.10, f32[96,512]{1,0:T(8,128)S(1)} %copy-done.3, f32[3072,512]{1,0:T(8,128)} %bitcast.47), kind=kOutput, calls=%fused_computation.3 | convolution fusion | flops 906264576 | bytes 8847360 | tf_op jit(solution)/shard_map/dot_general | solution.py:201
  147.7 11.5 %scatter_fusion = f32[12,8,24,128]{3,1,2,0:T(8,128)S(1)} fusion(f32[12,8,24,128]{3,1,2,0:T(8,128)S(1)} %fusion, s32[256]{0:T(256)S(1)} %bitcast.46, f32[256,8,128]{2,1,0:T(8,128)S(1)} %bitcast.49), kind=kCustom, calls=%fused_computation.1 | custom fusion | flops 262144 | bytes 3147776 | tf_op jit(solution)/shard_map/scatter-add | solution.py:209
  159.2 1.0 copy-done.1
  (19 shorter events, 0.2 us)
Async XLA Ops:
  7.2 48.3 %copy-start = (f32[512,512]{1,0:T(8,128)S(1)}, f32[512,512]{1,0:T(8,128)}, u32[]{:S(2)}) copy-start(f32[512,512]{1,0:T(8,128)} %param.8) | copy-start | bytes 3145732
  7.2 133.9 %all-gather.3.cloned.1.call-start = ((), (), s32[]{:S(2)}) async-start(), calls=%async_computation.1 | async-start | bytes 7077888 | tf_op jit(solution)/shard_map/all_gather | solution.py:198
  55.5 3.5 %copy-start.5 = (s32[1,1,192,1]{2,3,1,0:T(1,128)S(1)}, s32[1,1,192,1]{2,3,1,0:T(1,128)}, u32[]{:S(2)}) copy-start(s32[1,1,192,1]{2,3,1,0:T(1,128)} %param.12) | copy-start | bytes 2308
  58.9 0.7 copy-start.6
  59.1 1.1 copy-start.4
  63.7 76.0 %all-to-all-start = ((f32[128,2,1152]{2,1,0:T(2,128)}), f32[128,2,1152]{2,1,0:T(2,128)S(1)}, u32[]{:S(2)}, u32[]{:S(2)}) async-start(f32[128,2,1152]{2,1,0:T(2,128)} %all_to_all.8), calls=%async_computation | async-start | bytes 2359296 | tf_op jit(solution)/shard_map/all_to_all | solution.py:169
  84.7 0.7 copy-start.2
  140.7 0.9 copy-start.3
  159.2 1.0 copy-start.1
Sparse Core Ops, SparseCore 0:
  59.1 53.6 all-gather.2

commit v9 on v8

--- a/solution.py
+++ b/solution.py
@@ -137,6 +137,33 @@
         compiler_params=pltpu.CompilerParams(collective_id=0, has_side_effects=True),
     )(block)
 
+def _add_tiles_kernel(tile_cols, tiles_dev, ids_ref, base_ref, vals_ref, out_ref):
+    out_ref[...] = base_ref[...]
+    tile_rows, tile_width = vals_ref.shape[1], vals_ref.shape[2]
+
+    def body(i, carry):
+        tile = ids_ref[i]
+
+        @pl.when(tile < tiles_dev)
+        def _():
+            rows = pl.ds(pl.multiple_of((tile // tile_cols) * tile_rows, tile_rows), tile_rows)
+            cols = pl.ds(pl.multiple_of((tile % tile_cols) * tile_width, tile_width), tile_width)
+            out_ref[rows, cols] = out_ref[rows, cols] + vals_ref[i]
+
+        return carry
+
+    lax.fori_loop(0, vals_ref.shape[0], body, 0)
+
+
+def add_tiles(ids, base, vals, tile_cols, tiles_dev):
+    vmem = pl.BlockSpec(memory_space=pltpu.VMEM)
+    return pl.pallas_call(
+        functools.partial(_add_tiles_kernel, tile_cols, tiles_dev),
+        out_shape=jax.ShapeDtypeStruct(base.shape, base.dtype),
+        in_specs=[pl.BlockSpec(memory_space=pltpu.SMEM), vmem, vmem],
+        out_specs=vmem,
+    )(ids, base, vals)
+
 def per_device(diag_inverse, panel, trailing, agg_vals, agg_dest, agg_tile):
     row_devices = lax.axis_size(ROW_AXES)
     local_rows, local_cols = trailing.shape
@@ -205,11 +232,13 @@
         precision=lax.Precision.HIGH,
         preferred_element_type=jnp.float32,
     )
-    reduced = (trailing - product).reshape(tile_rows, TILE_ROWS, tile_cols, TILE_COLS)
-    reduced = reduced.at[landing // tile_cols, :, landing % tile_cols, :].add(
-        got_values.reshape(-1, TILE_ROWS, TILE_COLS), mode="drop"
-    )
-    updated = reduced.reshape(local_rows, local_cols)
+    updated = add_tiles(
+        landing,
+        trailing - product,
+        got_values.reshape(-1, TILE_ROWS, TILE_COLS),
+        tile_cols,
+        tiles_dev,
+    )
     return (updated, own_block)
 
 

time: 169 us -> 166 us (0.982)
  other arithmetic: 13.8 us -> 2.96 us
  Pallas kernels: 48.2 us -> 56 us
    scatter-add x1 -> x0, other arithmetic: 11.5 us -> none  [per_device(): reduced.at[landing // tile_cols, :, landing % tile_cols, :]]
    pallas_call x0 -> x1, Pallas kernels: none -> 7.79 us  [add_tiles(): pl.pallas_call(functools.partial(_add_tiles_kernel, tile_cols, tiles_dev)...]
  transfers between devices with their start and end apart: 2 -> 2, of which waited for: 1 -> 1; matrix products, arithmetic and copies ran while one was open for 5% -> 6% of each run, Pallas kernels for 0% -> 0%
where the time goes in v9:
time: 166 us; the launch traced here: 164 us
  Pallas kernels  56 us (34%)
  waiting for transfers between devices  53.8 us (32%)
  starting transfers between devices  16.1 us (10%)
  between operations  14.2 us (9%)
  matrix products  12.5 us (8%)
  local copies, waits for them, and re-layouts  8.68 us (5%)
  other arithmetic  2.96 us (2%)
    all_to_all x1, waiting for transfers between devices, per_device(): lax.all_to_all(send, ROW_AXES, split_axis=0, concat_axis=0, tiled=True)  53.8 us
    pallas_call x1, Pallas kernels, front_exchange(): pl.pallas_call(functools.partial(_front_kernel, n_x, n_zh, n_c), out_shap...  48.2 us
    all_to_all x1, starting transfers between devices, per_device(): lax.all_to_all(send, ROW_AXES, split_axis=0, concat_axis=0, tiled=True)  16 us
    pallas_call x1, Pallas kernels, add_tiles(): pl.pallas_call(functools.partial(_add_tiles_kernel, tile_cols, tiles_dev)...  7.79 us
    dot_general x1, matrix products, per_device(): lax.dot_general(own_full, partner, (((1,), (1,)), ((), ())), precision=la...  6.94 us
    dot_general x1, matrix products, per_device(): jnp.dot(to_rows(moved_panel), diag_inverse.T, precision=lax.Precision.HIG...  3.47 us
  transfers between devices with their start and end apart: 2, of which 1 were waited for; matrix products, arithmetic and copies ran while one was open for 6% of the time, Pallas kernels for 0%

profile of v9, /device:TPU:1, one launch (start us, length us, event | category | flops | bytes accessed | tf_op | source)
XLA Modules:
  0.0 164.2 jit_solution(11856079786496769105)
XLA Ops:
  7.2 0.0 copy-start
  7.2 0.0 all-gather.3.cloned.1.call-start
  7.2 48.2 %shard_map.77 = (f32[16,96,128]{2,1,0:T(8,128)}, f32[16,96,128]{2,1,0:T(8,128)}) custom-call(f32[96,128]{1,0:T(8,128)} %block_ref.1), custom_call_target="tpu_custom_call" | custom-call | tf_op jit(solution)/shard_map/pallas_call | solution.py:125
  55.5 0.0 copy-start.4
  55.5 3.5 %fusion = f32[4,96,512]{2,1,0:T(8,128)} fusion(f32[512,512]{1,0:T(8,128)S(1)} %copy-done, f32[4,4,12,8,128]{4,3,2,1,0:T(8,128)} %bitcast.47), kind=kOutput, calls=%fused_computation.3 | convolution fusion | flops 1207959552 | bytes 2621440 | tf_op jit(solution)/shard_map/dot_general | solution.py:219
  59.0 0.0 all-gather.3.cloned.1.call-update
  59.0 0.1 iota_compare_fusion
  59.1 0.0 copy-start.3
  59.1 0.1 fusion.12
  59.3 0.3 copy-done.5
  59.6 0.2 fusion.15
  59.8 0.1 scatter.15
  59.9 0.1 broadcast_in_dim.2
  60.0 0.2 copy-done.3
  60.2 1.8 %scatter_custom_fusion = f32[256,1152]{1,0:T(8,128)S(1)} fusion(f32[256,1152]{1,0:T(8,128)S(1)} %scatter.15, s32[192]{0:T(256)S(1)} %bitcast.57, f32[192,128]{1,0:T(8,128)S(1)} %broadcast_in_dim.2, f32[]{:T(128)} %constant.71, f32[192,1024]{1,0:T(8,128)S(1)} %bitcast.45), kind=kCustom, calls=%fused_computation.5 | custom fusion | flops 221184 | bytes 2064388 | tf_op jit(solution)/shard_map/scatter | solution.py:194
  62.0 1.7 %all_to_all.8 = f32[128,2,1152]{2,1,0:T(2,128)} reshape(f32[256,1152]{1,0:T(8,128)S(1)} %scatter_custom_fusion) | data formatting | bytes 2359296 | tf_op jit(solution)/shard_map/all_to_all | solution.py:196
  63.7 16.0 %all-to-all-start = ((f32[128,2,1152]{2,1,0:T(2,128)}), f32[128,2,1152]{2,1,0:T(2,128)S(1)}, u32[]{:S(2)}, u32[]{:S(2)}) async-start(f32[128,2,1152]{2,1,0:T(2,128)} %all_to_all.8), calls=%async_computation | async-start | bytes 2359296 | tf_op jit(solution)/shard_map/all_to_all | solution.py:196
  79.8 1.6 %copy.27 = f32[4,4,96,128]{3,1,2,0:T(4,128)S(1)} copy(f32[4,4,96,128]{3,2,1,0:T(8,128)} %bitcast.46) | data formatting | bytes 1572864 | tf_op jit(solution)/shard_map/reshape | solution.py:206
  81.4 1.2 reshape_reshape.3
  82.6 2.1 %fusion.8 = f32[96,512]{1,0:T(8,128)S(1)} fusion(f32[512,512]{1,0:T(8,128)S(1)} %copy-done, f32[4,96,512]{2,1,0:T(8,128)} %reshape_reshape.3, s32[]{:T(128)S(6)} %select_n.18), kind=kOutput, calls=%fused_computation.12 | convolution fusion | flops 301989888 | bytes 1441796 | tf_op jit(solution)/shard_map/dot_general | solution.py:212
  84.7 0.0 copy-start.2
  84.7 0.7 copy-done.2
  85.4 0.6 constant_dynamic-slice_fusion
  86.0 53.8 %all-to-all-done = f32[128,2,1152]{2,1,0:T(2,128)S(1)} async-done(((f32[128,2,1152]{2,1,0:T(2,128)}), f32[128,2,1152]{2,1,0:T(2,128)S(1)}, u32[]{:S(2)}, u32[]{:S(2)}) %all-to-all-start) | async-done | bytes 1179680 | tf_op jit(solution)/shard_map/all_to_all | solution.py:196
  139.7 0.8 all_to_all.10
  140.6 0.1 slice_bitcast_fusion
  140.7 0.0 copy-start.1
  140.7 1.2 copy.19
  141.9 0.7 fusion.11.ids_ref
  142.6 0.0 copy-done.1
  142.6 6.9 %convolution_subtract_fusion.base_ref = f32[96,3072]{1,0:T(8,128)} fusion(f32[96,3072]{1,0:T(8,128)S(1)} %copy-done.1, f32[96,512]{1,0:T(8,128)} %copy-done.2, f32[3072,512]{1,0:T(8,128)} %bitcast.42), kind=kOutput, calls=%fused_computation.1 | convolution fusion | flops 906264576 | bytes 8847360 | tf_op jit(solution)/shard_map/dot_general | solution.py:228
  149.5 7.8 %shard_map.78 = f32[96,3072]{1,0:T(8,128)} custom-call(s32[256]{0:T(256)} %fusion.11.ids_ref, f32[96,3072]{1,0:T(8,128)} %convolution_subtract_fusion.base_ref, f32[256,8,128]{2,1,0:T(8,128)} %bitcast.43), custom_call_target="tpu_custom_call" | custom-call | tf_op jit(solution)/shard_map/pallas_call | solution.py:160
  (15 shorter events, 0.1 us)
Async XLA Ops:
  7.2 48.3 %copy-start = (f32[512,512]{1,0:T(8,128)S(1)}, f32[512,512]{1,0:T(8,128)}, u32[]{:S(2)}) copy-start(f32[512,512]{1,0:T(8,128)} %param.8) | copy-start | bytes 3145732
  7.2 135.4 %all-gather.3.cloned.1.call-start = ((), (), s32[]{:S(2)}) async-start(), calls=%async_computation.1 | async-start | bytes 7077888 | tf_op jit(solution)/shard_map/all_gather | solution.py:225
  55.5 3.5 %copy-start.4 = (s32[1,1,192,1]{2,3,1,0:T(1,128)S(1)}, s32[1,1,192,1]{2,3,1,0:T(1,128)}, u32[]{:S(2)}) copy-start(s32[1,1,192,1]{2,3,1,0:T(1,128)} %param.12) | copy-start | bytes 2308
  58.9 0.7 copy-start.5
  59.1 1.1 copy-start.3
  63.7 76.0 %all-to-all-start = ((f32[128,2,1152]{2,1,0:T(2,128)}), f32[128,2,1152]{2,1,0:T(2,128)S(1)}, u32[]{:S(2)}, u32[]{:S(2)}) async-start(f32[128,2,1152]{2,1,0:T(2,128)} %all_to_all.8), calls=%async_computation | async-start | bytes 2359296 | tf_op jit(solution)/shard_map/all_to_all | solution.py:196
  84.7 0.7 copy-start.2
  140.7 1.9 %copy-start.1 = (f32[96,3072]{1,0:T(8,128)S(1)}, f32[96,3072]{1,0:T(8,128)}, u32[]{:S(2)}) copy-start(f32[96,3072]{1,0:T(8,128)} %param.10) | copy-start | bytes 3538948
Sparse Core Ops, SparseCore 0:
  59.1 53.6 all-gather.2

commit v10 on v9

--- a/solution.py
+++ b/solution.py
@@ -16,55 +16,58 @@
 
 
 def _front_kernel(n_x, n_zh, n_c, block_ref, ring_ref, moved_ref, send_sem, recv_sem,
-                  xsend_sem, xrecv_sem, local_sem):
+                  xsend_sem, xrecv_sem, xfwd_sem, local_sem):
     n = n_zh * n_c
     col = lax.axis_index("col")
     x = lax.axis_index("x")
     me = lax.axis_index("zh") * n_c + col
     right = lax.rem(me + 1, n)
     left = lax.rem(me + n - 1, n)
-    is_source = x == col
+    shift = lax.rem(x - col + n_x, n_x)
+    x_up = lax.rem(x + 1, n_x)
+    x_down = lax.rem(x + n_x - 1, n_x)
 
     def on_ring(p):
         return {"zh": p // n_c, "col": lax.rem(p, n_c)}
-
-    def x_peer(k):
-        return {"x": lax.rem(x + k, n_x)}
 
     barrier = pltpu.get_barrier_semaphore()
     for other in (left, right):
         pl.semaphore_signal(barrier, 1, device_id=on_ring(other), device_id_type=MESH_IDS)
-
-    @pl.when(is_source)
-    def _():
-        for k in range(1, n_x):
-            pl.semaphore_signal(barrier, 1, device_id=x_peer(k), device_id_type=MESH_IDS)
-        pl.semaphore_wait(barrier, 2 + n_x - 1)
-
-    @pl.when(jnp.logical_not(is_source))
-    def _():
-        pl.semaphore_signal(barrier, 1, device_id={"x": col}, device_id_type=MESH_IDS)
-        pl.semaphore_wait(barrier, 3)
+    for other in (x_up, x_down):
+        pl.semaphore_signal(barrier, 1, device_id={"x": other}, device_id_type=MESH_IDS)
+    pl.semaphore_wait(barrier, 4)
 
     ring_ref[me] = block_ref[...]
 
-    def x_copy(slot, src, k):
+    def x_copy(slot, src, target, send):
         return pltpu.make_async_remote_copy(
             src_ref=src,
             dst_ref=moved_ref.at[slot],
-            send_sem=xsend_sem.at[slot, k - 1],
-            recv_sem=xrecv_sem.at[0],
-            device_id=x_peer(k),
+            send_sem=send,
+            recv_sem=xrecv_sem.at[slot],
+            device_id={"x": target},
             device_id_type=MESH_IDS,
         )
 
-    def forward_x(slot, src):
-        @pl.when(is_source)
+    order = []
+
+    def x_stage(slot, src):
+        t = len(order)
+        order.append(slot)
+
+        @pl.when(shift == 0)
         def _():
-            for k in range(1, n_x):
-                x_copy(slot, src, k).start()
-
-    forward_x(me, block_ref)
+            x_copy(slot, src, x_up, xsend_sem.at[slot, 0]).start()
+            x_copy(slot, src, x_down, xsend_sem.at[slot, 1]).start()
+
+        for role, parity, onward in ((1, 0, x_up), (n_x - 1, 1, x_down)):
+            @pl.when(shift == role)
+            def _():
+                x_copy(slot, moved_ref.at[slot], onward, xfwd_sem.at[slot]).wait_recv()
+                if t % 2 == parity:
+                    x_copy(slot, moved_ref.at[slot], onward, xfwd_sem.at[slot]).start()
+
+    x_stage(me, block_ref)
     counts = (n // 2, n - 1 - n // 2)
     targets = (right, left)
     signs = (-1, 1)
@@ -76,7 +79,7 @@
             slot = lax.rem(me + signs[d] * step + n, n)
             if step > 0:
                 sent[d][step - 1].wait_recv()
-                forward_x(slot, ring_ref.at[slot])
+                x_stage(slot, ring_ref.at[slot])
             src = block_ref if step == 0 else ring_ref.at[slot]
             copy = pltpu.make_async_remote_copy(
                 src_ref=src,
@@ -92,30 +95,30 @@
         if sent[d]:
             sent[d][-1].wait_recv()
             last = lax.rem(me + signs[d] * counts[d] + n, n)
-            forward_x(last, ring_ref.at[last])
+            x_stage(last, ring_ref.at[last])
         for copy in sent[d]:
             copy.wait_send()
 
-    @pl.when(is_source)
+    @pl.when(shift == 0)
     def _():
-        for slot in range(n):
-            for k in range(1, n_x):
-                x_copy(slot, ring_ref.at[slot], k).wait_send()
+        for slot in order:
+            x_copy(slot, ring_ref.at[slot], x_up, xsend_sem.at[slot, 0]).wait_send()
+            x_copy(slot, ring_ref.at[slot], x_down, xsend_sem.at[slot, 1]).wait_send()
         local = pltpu.make_async_copy(ring_ref, moved_ref, local_sem.at[0])
         local.start()
         local.wait()
 
-    @pl.when(jnp.logical_not(is_source))
+    for role, parity, onward in ((1, 0, x_up), (n_x - 1, 1, x_down)):
+        @pl.when(shift == role)
+        def _():
+            for t, slot in enumerate(order):
+                if t % 2 == parity:
+                    x_copy(slot, moved_ref.at[slot], onward, xfwd_sem.at[slot]).wait_send()
+
+    @pl.when(shift == 2)
     def _():
-        whole = pltpu.make_async_remote_copy(
-            src_ref=ring_ref,
-            dst_ref=moved_ref,
-            send_sem=local_sem.at[0],
-            recv_sem=xrecv_sem.at[0],
-            device_id={"x": col},
-            device_id_type=MESH_IDS,
-        )
-        whole.wait_recv()
+        for slot in order:
+            x_copy(slot, moved_ref.at[slot], x_up, xfwd_sem.at[slot]).wait_recv()
 
 
 def front_exchange(block, n_x, n_zh, n_c):
@@ -130,8 +133,9 @@
         scratch_shapes=[
             pltpu.SemaphoreType.DMA((2, steps)),
             pltpu.SemaphoreType.DMA((2, steps)),
-            pltpu.SemaphoreType.DMA((n, max(n_x - 1, 1))),
-            pltpu.SemaphoreType.DMA((1,)),
+            pltpu.SemaphoreType.DMA((n, 2)),
+            pltpu.SemaphoreType.DMA((n,)),
+            pltpu.SemaphoreType.DMA((n,)),
             pltpu.SemaphoreType.DMA((1,)),
         ],
         compiler_params=pltpu.CompilerParams(collective_id=0, has_side_effects=True),

time: 166 us -> 188 us (1.13)
  starting transfers between devices: 16.1 us -> 29.3 us
  Pallas kernels: 56 us -> 65.3 us
    all_to_all x1, starting transfers between devices: 16 us -> 29.3 us  [per_device(): lax.all_to_all(send, ROW_AXES, split_axis=0, concat_axis=0, tiled=True)]
    pallas_call x1, Pallas kernels: 48.2 us -> 57.5 us  [front_exchange(): pl.pallas_call(functools.partial(_front_kernel, n_x, n_zh, n_c), out_shap...]
  transfers between devices with their start and end apart: 2 -> 2, of which waited for: 1 -> 1; matrix products, arithmetic and copies ran while one was open for 6% -> 5% of each run, Pallas kernels for 0% -> 0%
where the time goes in v10:
time: 188 us
  Pallas kernels  65.3 us (35%)
  waiting for transfers between devices  55 us (29%)
  starting transfers between devices  29.3 us (16%)
  between operations  14.2 us (8%)
  matrix products  12.5 us (7%)
  local copies, waits for them, and re-layouts  8.68 us (5%)
  other arithmetic  2.96 us (2%)
    pallas_call x1, Pallas kernels, front_exchange(): pl.pallas_call(functools.partial(_front_kernel, n_x, n_zh, n_c), out_shap...  57.5 us
    all_to_all x1, waiting for transfers between devices, per_device(): lax.all_to_all(send, ROW_AXES, split_axis=0, concat_axis=0, tiled=True)  55 us
    all_to_all x1, starting transfers between devices, per_device(): lax.all_to_all(send, ROW_AXES, split_axis=0, concat_axis=0, tiled=True)  29.3 us
    pallas_call x1, Pallas kernels, add_tiles(): pl.pallas_call(functools.partial(_add_tiles_kernel, tile_cols, tiles_dev)...  7.79 us
    dot_general x1, matrix products, per_device(): lax.dot_general(own_full, partner, (((1,), (1,)), ((), ())), precision=la...  6.94 us
  transfers between devices with their start and end apart: 2, of which 1 were waited for; matrix products, arithmetic and copies ran while one was open for 5% of the time, Pallas kernels for 0%

profile of v10, /device:TPU:1, one launch (start us, length us, event | category | flops | bytes accessed | tf_op | source)
XLA Modules:
  0.0 187.9 jit_solution(7735122416985702043)
XLA Ops:
  7.2 0.0 copy-start
  7.2 0.0 all-gather.3.cloned.1.call-start
  7.2 57.5 %shard_map.77 = (f32[16,96,128]{2,1,0:T(8,128)}, f32[16,96,128]{2,1,0:T(8,128)}) custom-call(f32[96,128]{1,0:T(8,128)} %block_ref.1), custom_call_target="tpu_custom_call" | custom-call | tf_op jit(solution)/shard_map/pallas_call | solution.py:128
  64.7 0.0 copy-done
  64.7 0.0 copy-start.4
  64.7 3.5 %fusion = f32[4,96,512]{2,1,0:T(8,128)} fusion(f32[512,512]{1,0:T(8,128)S(1)} %copy-done, f32[4,4,12,8,128]{4,3,2,1,0:T(8,128)} %bitcast.47), kind=kOutput, calls=%fused_computation.3 | convolution fusion | flops 1207959552 | bytes 2621440 | tf_op jit(solution)/shard_map/dot_general | solution.py:223
  68.2 0.0 all-gather.3.cloned.1.call-update
  68.2 0.1 iota_compare_fusion
  68.3 0.0 copy-start.3
  68.4 0.1 fusion.12
  68.6 0.3 copy-done.5
  68.9 0.2 fusion.15
  69.1 0.1 scatter.15
  69.2 0.1 broadcast_in_dim.2
  69.3 0.2 copy-done.3
  69.5 1.8 scatter_custom_fusion
  71.3 1.7 all_to_all.8
  73.0 29.3 %all-to-all-start = ((f32[128,2,1152]{2,1,0:T(2,128)}), f32[128,2,1152]{2,1,0:T(2,128)S(1)}, u32[]{:S(2)}, u32[]{:S(2)}) async-start(f32[128,2,1152]{2,1,0:T(2,128)} %all_to_all.8), calls=%async_computation | async-start | bytes 2359296 | tf_op jit(solution)/shard_map/all_to_all | solution.py:200
  102.3 1.6 copy.27
  103.9 1.2 reshape_reshape.3
  105.1 2.1 %fusion.8 = f32[96,512]{1,0:T(8,128)S(1)} fusion(f32[512,512]{1,0:T(8,128)S(1)} %copy-done, f32[4,96,512]{2,1,0:T(8,128)} %reshape_reshape.3, s32[]{:T(128)S(6)} %select_n.18), kind=kOutput, calls=%fused_computation.12 | convolution fusion | flops 301989888 | bytes 1441796 | tf_op jit(solution)/shard_map/dot_general | solution.py:216
  107.2 0.7 copy-done.2
  107.8 0.6 constant_dynamic-slice_fusion
  108.5 55.0 %all-to-all-done = f32[128,2,1152]{2,1,0:T(2,128)S(1)} async-done(((f32[128,2,1152]{2,1,0:T(2,128)}), f32[128,2,1152]{2,1,0:T(2,128)S(1)}, u32[]{:S(2)}, u32[]{:S(2)}) %all-to-all-start) | async-done | bytes 1179680 | tf_op jit(solution)/shard_map/all_to_all | solution.py:200
  163.5 0.8 all_to_all.10
  164.3 0.1 slice_bitcast_fusion
  164.4 0.0 copy-start.1
  164.4 1.2 copy.19
  165.6 0.7 fusion.11.ids_ref
  166.3 0.0 copy-done.1
  166.3 6.9 %convolution_subtract_fusion.base_ref = f32[96,3072]{1,0:T(8,128)} fusion(f32[96,3072]{1,0:T(8,128)S(1)} %copy-done.1, f32[96,512]{1,0:T(8,128)} %copy-done.2, f32[3072,512]{1,0:T(8,128)} %bitcast.42), kind=kOutput, calls=%fused_computation.1 | convolution fusion | flops 906264576 | bytes 8847360 | tf_op jit(solution)/shard_map/dot_general | solution.py:232
  173.2 7.8 %shard_map.78 = f32[96,3072]{1,0:T(8,128)} custom-call(s32[256]{0:T(256)} %fusion.11.ids_ref, f32[96,3072]{1,0:T(8,128)} %convolution_subtract_fusion.base_ref, f32[256,8,128]{2,1,0:T(8,128)} %bitcast.43), custom_call_target="tpu_custom_call" | custom-call | tf_op jit(solution)/shard_map/pallas_call | solution.py:164
  (15 shorter events, 0.1 us)
Async XLA Ops:
  7.2 57.6 %copy-start = (f32[512,512]{1,0:T(8,128)S(1)}, f32[512,512]{1,0:T(8,128)}, u32[]{:S(2)}) copy-start(f32[512,512]{1,0:T(8,128)} %param.8) | copy-start | bytes 3145732
  7.2 159.1 %all-gather.3.cloned.1.call-start = ((), (), s32[]{:S(2)}) async-start(), calls=%async_computation.1 | async-start | bytes 7077888 | tf_op jit(solution)/shard_map/all_gather | solution.py:229
  64.7 3.5 %copy-start.4 = (s32[1,1,192,1]{2,3,1,0:T(1,128)S(1)}, s32[1,1,192,1]{2,3,1,0:T(1,128)}, u32[]{:S(2)}) copy-start(s32[1,1,192,1]{2,3,1,0:T(1,128)} %param.12) | copy-start | bytes 2308
  68.2 0.7 copy-start.5
  68.3 1.1 copy-start.3
  73.0 90.5 %all-to-all-start = ((f32[128,2,1152]{2,1,0:T(2,128)}), f32[128,2,1152]{2,1,0:T(2,128)S(1)}, u32[]{:S(2)}, u32[]{:S(2)}) async-start(f32[128,2,1152]{2,1,0:T(2,128)} %all_to_all.8), calls=%async_computation | async-start | bytes 2359296 | tf_op jit(solution)/shard_map/all_to_all | solution.py:200
  107.2 0.7 copy-start.2
  164.4 1.9 %copy-start.1 = (f32[96,3072]{1,0:T(8,128)S(1)}, f32[96,3072]{1,0:T(8,128)}, u32[]{:S(2)}) copy-start(f32[96,3072]{1,0:T(8,128)} %param.10) | copy-start | bytes 3538948
Sparse Core Ops, SparseCore 0:
  68.4 64.2 all-gather.2

commit v11 on v9

--- a/solution.py
+++ b/solution.py
@@ -64,35 +64,36 @@
             for k in range(1, n_x):
                 x_copy(slot, src, k).start()
 
-    forward_x(me, block_ref)
     counts = (n // 2, n - 1 - n // 2)
     targets = (right, left)
     signs = (-1, 1)
     sent = ([], [])
-    for step in range(max(counts)):
+    for step in range(max(counts) + 1):
+        ready = []
         for d in range(2):
-            if step >= counts[d]:
+            if step > counts[d]:
                 continue
             slot = lax.rem(me + signs[d] * step + n, n)
             if step > 0:
                 sent[d][step - 1].wait_recv()
-                forward_x(slot, ring_ref.at[slot])
-            src = block_ref if step == 0 else ring_ref.at[slot]
-            copy = pltpu.make_async_remote_copy(
-                src_ref=src,
-                dst_ref=ring_ref.at[slot],
-                send_sem=send_sem.at[d, step],
-                recv_sem=recv_sem.at[d, step],
-                device_id=on_ring(targets[d]),
-                device_id_type=MESH_IDS,
-            )
-            copy.start()
-            sent[d].append(copy)
+                ready.append(slot)
+            if step < counts[d]:
+                src = block_ref if step == 0 else ring_ref.at[slot]
+                copy = pltpu.make_async_remote_copy(
+                    src_ref=src,
+                    dst_ref=ring_ref.at[slot],
+                    send_sem=send_sem.at[d, step],
+                    recv_sem=recv_sem.at[d, step],
+                    device_id=on_ring(targets[d]),
+                    device_id_type=MESH_IDS,
+                )
+                copy.start()
+                sent[d].append(copy)
+        if step == 0:
+            forward_x(me, block_ref)
+        for slot in ready:
+            forward_x(slot, ring_ref.at[slot])
     for d in range(2):
-        if sent[d]:
-            sent[d][-1].wait_recv()
-            last = lax.rem(me + signs[d] * counts[d] + n, n)
-            forward_x(last, ring_ref.at[last])
         for copy in sent[d]:
             copy.wait_send()
 

time: 166 us -> 168 us (1.012)
  the two profiles are of different devices: /device:TPU:1 before, /device:TPU:64 now
where the time goes in v11:
time: 168 us; the launch traced here: 167 us
  waiting for transfers between devices  59.5 us (35%)
  Pallas kernels  56.1 us (33%)
  between operations  14.2 us (8%)
  starting transfers between devices  13.3 us (8%)
  matrix products  12.5 us (7%)
  local copies, waits for them, and re-layouts  8.68 us (5%)
  other arithmetic  2.96 us (2%)
    all_to_all x1, waiting for transfers between devices, per_device(): lax.all_to_all(send, ROW_AXES, split_axis=0, concat_axis=0, tiled=True)  59.4 us
    pallas_call x1, Pallas kernels, front_exchange(): pl.pallas_call(functools.partial(_front_kernel, n_x, n_zh, n_c), out_shap...  46.9 us
    all_to_all x1, starting transfers between devices, per_device(): lax.all_to_all(send, ROW_AXES, split_axis=0, concat_axis=0, tiled=True)  13.3 us
    pallas_call x1, Pallas kernels, add_tiles(): pl.pallas_call(functools.partial(_add_tiles_kernel, tile_cols, tiles_dev)...  9.28 us
    dot_general x1, matrix products, per_device(): lax.dot_general(own_full, partner, (((1,), (1,)), ((), ())), precision=la...  6.94 us
    dot_general x1, matrix products, per_device(): jnp.dot(to_rows(moved_panel), diag_inverse.T, precision=lax.Precision.HIG...  3.47 us
  transfers between devices with their start and end apart: 2, of which 1 were waited for; matrix products, arithmetic and copies ran while one was open for 6% of the time, Pallas kernels for 0%

profile of v11, /device:TPU:64, one launch (start us, length us, event | category | flops | bytes accessed | tf_op | source)
XLA Modules:
  0.0 167.2 jit_solution(1408367094254024960)
XLA Ops:
  7.2 0.0 copy-start
  7.2 0.0 all-gather.3.cloned.1.call-start
  7.2 46.9 %shard_map.77 = (f32[16,96,128]{2,1,0:T(8,128)}, f32[16,96,128]{2,1,0:T(8,128)}) custom-call(f32[96,128]{1,0:T(8,128)} %block_ref.1), custom_call_target="tpu_custom_call" | custom-call | tf_op jit(solution)/shard_map/pallas_call | solution.py:126
  54.1 0.0 copy-done
  54.1 0.0 copy-start.4
  54.1 3.5 %fusion = f32[4,96,512]{2,1,0:T(8,128)} fusion(f32[512,512]{1,0:T(8,128)S(1)} %copy-done, f32[4,4,12,8,128]{4,3,2,1,0:T(8,128)} %bitcast.47), kind=kOutput, calls=%fused_computation.3 | convolution fusion | flops 1207959552 | bytes 2621440 | tf_op jit(solution)/shard_map/dot_general | solution.py:220
  57.6 0.0 all-gather.3.cloned.1.call-update
  57.6 0.0 copy-done.4
  57.6 0.1 iota_compare_fusion
  57.7 0.0 copy-start.3
  57.7 0.1 fusion.12
  58.0 0.3 copy-done.5
  58.3 0.2 fusion.15
  58.5 0.1 scatter.15
  58.6 0.1 broadcast_in_dim.2
  58.6 0.2 copy-done.3
  58.9 1.8 %scatter_custom_fusion = f32[256,1152]{1,0:T(8,128)S(1)} fusion(f32[256,1152]{1,0:T(8,128)S(1)} %scatter.15, s32[192]{0:T(256)S(1)} %bitcast.57, f32[192,128]{1,0:T(8,128)S(1)} %broadcast_in_dim.2, f32[]{:T(128)} %constant.71, f32[192,1024]{1,0:T(8,128)S(1)} %bitcast.45), kind=kCustom, calls=%fused_computation.5 | custom fusion | flops 221184 | bytes 2064388 | tf_op jit(solution)/shard_map/scatter | solution.py:195
  60.6 1.7 %all_to_all.8 = f32[128,2,1152]{2,1,0:T(2,128)} reshape(f32[256,1152]{1,0:T(8,128)S(1)} %scatter_custom_fusion) | data formatting | bytes 2359296 | tf_op jit(solution)/shard_map/all_to_all | solution.py:197
  62.4 13.3 %all-to-all-start = ((f32[128,2,1152]{2,1,0:T(2,128)}), f32[128,2,1152]{2,1,0:T(2,128)S(1)}, u32[]{:S(2)}, u32[]{:S(2)}) async-start(f32[128,2,1152]{2,1,0:T(2,128)} %all_to_all.8), calls=%async_computation | async-start | bytes 2359296 | tf_op jit(solution)/shard_map/all_to_all | solution.py:197
  75.6 1.6 copy.27
  77.3 1.2 reshape_reshape.3
  78.5 2.1 %fusion.8 = f32[96,512]{1,0:T(8,128)S(1)} fusion(f32[512,512]{1,0:T(8,128)S(1)} %copy-done, f32[4,96,512]{2,1,0:T(8,128)} %reshape_reshape.3, s32[]{:T(128)S(6)} %select_n.18), kind=kOutput, calls=%fused_computation.12 | convolution fusion | flops 301989888 | bytes 1441796 | tf_op jit(solution)/shard_map/dot_general | solution.py:213
  80.5 0.7 copy-done.2
  81.2 0.6 constant_dynamic-slice_fusion
  81.8 59.4 %all-to-all-done = f32[128,2,1152]{2,1,0:T(2,128)S(1)} async-done(((f32[128,2,1152]{2,1,0:T(2,128)}), f32[128,2,1152]{2,1,0:T(2,128)S(1)}, u32[]{:S(2)}, u32[]{:S(2)}) %all-to-all-start) | async-done | bytes 1179680 | tf_op jit(solution)/shard_map/all_to_all | solution.py:197
  141.3 0.8 all_to_all.10
  142.1 0.1 slice_bitcast_fusion
  142.2 0.0 copy-start.1
  142.2 1.2 copy.19
  143.4 0.7 fusion.11.ids_ref
  144.1 6.9 %convolution_subtract_fusion.base_ref = f32[96,3072]{1,0:T(8,128)} fusion(f32[96,3072]{1,0:T(8,128)S(1)} %copy-done.1, f32[96,512]{1,0:T(8,128)} %copy-done.2, f32[3072,512]{1,0:T(8,128)} %bitcast.42), kind=kOutput, calls=%fused_computation.1 | convolution fusion | flops 906264576 | bytes 8847360 | tf_op jit(solution)/shard_map/dot_general | solution.py:229
  151.1 9.3 %shard_map.78 = f32[96,3072]{1,0:T(8,128)} custom-call(s32[256]{0:T(256)} %fusion.11.ids_ref, f32[96,3072]{1,0:T(8,128)} %convolution_subtract_fusion.base_ref, f32[256,8,128]{2,1,0:T(8,128)} %bitcast.43), custom_call_target="tpu_custom_call" | custom-call | tf_op jit(solution)/shard_map/pallas_call | solution.py:161
  (15 shorter events, 0.1 us)
Async XLA Ops:
  7.2 46.9 %copy-start = (f32[512,512]{1,0:T(8,128)S(1)}, f32[512,512]{1,0:T(8,128)}, u32[]{:S(2)}) copy-start(f32[512,512]{1,0:T(8,128)} %param.8) | copy-start | bytes 3145732
  7.2 136.9 %all-gather.3.cloned.1.call-start = ((), (), s32[]{:S(2)}) async-start(), calls=%async_computation.1 | async-start | bytes 7077888 | tf_op jit(solution)/shard_map/all_gather | solution.py:226
  54.1 3.5 %copy-start.4 = (s32[1,1,192,1]{2,3,1,0:T(1,128)S(1)}, s32[1,1,192,1]{2,3,1,0:T(1,128)}, u32[]{:S(2)}) copy-start(s32[1,1,192,1]{2,3,1,0:T(1,128)} %param.12) | copy-start | bytes 2308
  57.6 0.7 copy-start.5
  57.7 1.1 copy-start.3
  62.4 78.9 %all-to-all-start = ((f32[128,2,1152]{2,1,0:T(2,128)}), f32[128,2,1152]{2,1,0:T(2,128)S(1)}, u32[]{:S(2)}, u32[]{:S(2)}) async-start(f32[128,2,1152]{2,1,0:T(2,128)} %all_to_all.8), calls=%async_computation | async-start | bytes 2359296 | tf_op jit(solution)/shard_map/all_to_all | solution.py:197
  80.5 0.7 copy-start.2
  142.2 1.9 %copy-start.1 = (f32[96,3072]{1,0:T(8,128)S(1)}, f32[96,3072]{1,0:T(8,128)}, u32[]{:S(2)}) copy-start(f32[96,3072]{1,0:T(8,128)} %param.10) | copy-start | bytes 3538948
Sparse Core Ops, SparseCore 0:
  57.7 55.8 all-gather.2

commit v12 on v11

--- a/solution.py
+++ b/solution.py
@@ -165,6 +165,65 @@
         out_specs=vmem,
     )(ids, base, vals)
 
+def _spread_kernel(n_y, n_core, block_ref, out_ref, send_sem, recv_sem, local_sem):
+    n = n_y * n_core
+    me = lax.axis_index("y") * n_core + lax.axis_index("core")
+
+    def where(p):
+        return {"y": p // n_core, "core": lax.rem(p, n_core)}
+
+    barrier = pltpu.get_barrier_semaphore()
+    for k in range(1, n):
+        pl.semaphore_signal(barrier, 1, device_id=where(lax.rem(me + k, n)), device_id_type=MESH_IDS)
+    pl.semaphore_wait(barrier, n - 1)
+    parts = block_ref.shape[0]
+    local = []
+    for j in range(parts):
+        copy = pltpu.make_async_copy(block_ref.at[j], out_ref.at[j, me], local_sem.at[j])
+        copy.start()
+        local.append(copy)
+    for k in range(1, n):
+        peer = where(lax.rem(me + k, n))
+        for j in range(parts):
+            pltpu.make_async_remote_copy(
+                src_ref=block_ref.at[j],
+                dst_ref=out_ref.at[j, me],
+                send_sem=send_sem.at[0],
+                recv_sem=recv_sem.at[0],
+                device_id=peer,
+                device_id_type=MESH_IDS,
+            ).start()
+    every = pltpu.make_async_remote_copy(
+        src_ref=out_ref.at[:, pl.ds(0, n - 1)],
+        dst_ref=out_ref.at[:, pl.ds(0, n - 1)],
+        send_sem=send_sem.at[0],
+        recv_sem=recv_sem.at[0],
+        device_id=where(lax.rem(me + 1, n)),
+        device_id_type=MESH_IDS,
+    )
+    every.wait_send()
+    every.wait_recv()
+    for copy in local:
+        copy.wait()
+
+
+def spread(block, n_y, n_core):
+    n = n_y * n_core
+    parts = block.shape[0]
+    anywhere = pl.BlockSpec(memory_space=pl.ANY)
+    return pl.pallas_call(
+        functools.partial(_spread_kernel, n_y, n_core),
+        out_shape=jax.ShapeDtypeStruct((parts, n) + block.shape[1:], block.dtype),
+        in_specs=[anywhere],
+        out_specs=anywhere,
+        scratch_shapes=[
+            pltpu.SemaphoreType.DMA((1,)),
+            pltpu.SemaphoreType.DMA((1,)),
+            pltpu.SemaphoreType.DMA((parts,)),
+        ],
+        compiler_params=pltpu.CompilerParams(collective_id=1, has_side_effects=True),
+    )(block)
+
 def per_device(diag_inverse, panel, trailing, agg_vals, agg_dest, agg_tile):
     row_devices = lax.axis_size(ROW_AXES)
     local_rows, local_cols = trailing.shape
@@ -223,7 +282,7 @@
         precision=lax.Precision.HIGHEST,
         preferred_element_type=jnp.float32,
     ).reshape(n_zh, local_rows, panel_width)
-    gathered = lax.all_gather(chosen, ("y", "core"), axis=1, tiled=False)
+    gathered = spread(chosen, lax.axis_size("y"), lax.axis_size("core"))
     partner = gathered.reshape(local_cols, panel_width)
 
     product = lax.dot_general(

time: 168 us -> 222 us (1.32)
  the two profiles are of different devices: /device:TPU:64 before, /device:TPU:1 now
where the time goes in v12:
time: 222 us; the launch traced here: 221 us
  Pallas kernels  172 us (77%)
  starting transfers between devices  23 us (10%)
  matrix products  12.4 us (6%)
  local copies, waits for them, and re-layouts  7.52 us (3%)
  other arithmetic  5.8 us (3%)
    pallas_call x1, Pallas kernels, front_exchange(): pl.pallas_call(functools.partial(_front_kernel, n_x, n_zh, n_c), out_shap...  87 us
    pallas_call x1, Pallas kernels, spread(): pl.pallas_call(functools.partial(_spread_kernel, n_y, n_core), out_shape=...  75.5 us
    all_to_all x1, starting transfers between devices, per_device(): lax.all_to_all(send, ROW_AXES, split_axis=0, concat_axis=0, tiled=True)  23 us
    pallas_call x1, Pallas kernels, add_tiles(): pl.pallas_call(functools.partial(_add_tiles_kernel, tile_cols, tiles_dev)...  9.28 us
    dot_general x1, matrix products, per_device(): lax.dot_general(own_full, partner, (((1,), (1,)), ((), ())), precision=la...  6.82 us
  transfers between devices with their start and end apart: 1, of which 0 were waited for; matrix products, arithmetic and copies ran while one was open for 7% of the time, Pallas kernels for 73%

profile of v12, /device:TPU:1, one launch (start us, length us, event | category | flops | bytes accessed | tf_op | source)
XLA Modules:
  0.0 221.3 jit_solution(1935044102085455733)
XLA Ops:
  0.6 0.0 copy-start
  0.6 0.9 iota_compare_fusion
  1.5 0.0 copy-start.2
  1.5 0.1 fusion.12
  1.8 0.9 fusion.15
  2.6 0.7 compare_select_fusion
  3.3 0.7 convert_element_type.20
  4.0 0.1 scatter.15
  4.1 0.1 broadcast_in_dim.2
  4.2 0.0 copy-done.2
  4.2 1.8 scatter_custom_fusion
  6.0 1.7 all_to_all.8
  7.7 23.0 %all-to-all-start = ((f32[128,2,1152]{2,1,0:T(2,128)}), f32[128,2,1152]{2,1,0:T(2,128)S(1)}, u32[]{:S(2)}, u32[]{:S(2)}) async-start(f32[128,2,1152]{2,1,0:T(2,128)} %all_to_all.8), calls=%async_computation | async-start | bytes 2359296 | tf_op jit(solution)/shard_map/all_to_all | solution.py:256
  30.8 87.0 %shard_map.77 = (f32[16,96,128]{2,1,0:T(8,128)}, f32[16,96,128]{2,1,0:T(8,128)}) custom-call(f32[96,128]{1,0:T(8,128)} %block_ref.1), custom_call_target="tpu_custom_call" | custom-call | tf_op jit(solution)/shard_map/pallas_call | solution.py:126
  117.7 1.6 copy.27
  119.4 1.2 reshape_reshape.3
  120.6 0.0 copy-done
  120.6 3.4 %fusion.block_ref = f32[4,96,512]{2,1,0:T(8,128)} fusion(f32[512,512]{1,0:T(8,128)S(1)} %copy-done, f32[4,4,12,8,128]{4,3,2,1,0:T(8,128)} %bitcast.47), kind=kOutput, calls=%fused_computation.3 | convolution fusion | flops 1207959552 | bytes 2621440 | tf_op jit(solution)/shard_map/dot_general | solution.py:279
  124.0 75.5 %shard_map.78 = f32[4,8,96,512]{3,2,1,0:T(8,128)} custom-call(f32[4,96,512]{2,1,0:T(8,128)} %fusion.block_ref), custom_call_target="tpu_custom_call" | custom-call | tf_op jit(solution)/shard_map/pallas_call | solution.py:214
  199.5 0.0 copy-start.1
  199.5 2.2 fusion.8
  201.7 0.6 constant_dynamic-slice_fusion
  202.3 0.0 copy-done.1
  202.3 6.8 %convolution_subtract_fusion.base_ref = f32[96,3072]{1,0:T(8,128)} fusion(f32[96,3072]{1,0:T(8,128)S(1)} %copy-done.1, f32[96,512]{1,0:T(8,128)S(1)} %fusion.8, f32[3072,512]{1,0:T(8,128)} %bitcast.42), kind=kOutput, calls=%fused_computation.1 | convolution fusion | flops 906264576 | bytes 8847360 | tf_op jit(solution)/shard_map/dot_general | solution.py:288
  209.2 0.0 all-to-all-done
  209.2 0.8 all_to_all.10
  210.0 0.1 slice_bitcast_fusion
  210.1 0.7 fusion.11.ids_ref
  210.8 1.2 copy.19
  212.0 9.3 %shard_map.79 = f32[96,3072]{1,0:T(8,128)} custom-call(s32[256]{0:T(256)} %fusion.11.ids_ref, f32[96,3072]{1,0:T(8,128)} %convolution_subtract_fusion.base_ref, f32[256,8,128]{2,1,0:T(8,128)} %bitcast.43), custom_call_target="tpu_custom_call" | custom-call | tf_op jit(solution)/shard_map/pallas_call | solution.py:161
  (9 shorter events, 0.1 us)
Async XLA Ops:
  0.6 119.9 %copy-start = (f32[512,512]{1,0:T(8,128)S(1)}, f32[512,512]{1,0:T(8,128)}, u32[]{:S(2)}) copy-start(f32[512,512]{1,0:T(8,128)} %param.8) | copy-start | bytes 3145732
  1.5 2.7 %copy-start.2 = (f32[1,1,192,1024]{3,2,1,0:T(8,128)S(1)}, f32[1,1,192,1024]{3,2,1,0:T(8,128)}, u32[]{:S(2)}) copy-start(f32[1,1,192,1024]{3,2,1,0:T(8,128)} %param.11) | copy-start | bytes 2359300
  7.7 201.4 %all-to-all-start = ((f32[128,2,1152]{2,1,0:T(2,128)}), f32[128,2,1152]{2,1,0:T(2,128)S(1)}, u32[]{:S(2)}, u32[]{:S(2)}) async-start(f32[128,2,1152]{2,1,0:T(2,128)} %all_to_all.8), calls=%async_computation | async-start | bytes 2359296 | tf_op jit(solution)/shard_map/all_to_all | solution.py:256
  199.5 2.8 %copy-start.1 = (f32[96,3072]{1,0:T(8,128)S(1)}, f32[96,3072]{1,0:T(8,128)}, u32[]{:S(2)}) copy-start(f32[96,3072]{1,0:T(8,128)} %param.10) | copy-start | bytes 3538948

commit v13 on v11

--- a/solution.py
+++ b/solution.py
@@ -153,7 +153,7 @@
 
         return carry
 
-    lax.fori_loop(0, vals_ref.shape[0], body, 0)
+    lax.fori_loop(0, vals_ref.shape[0], body, 0, unroll=8)
 
 
 def add_tiles(ids, base, vals, tile_cols, tiles_dev):

time: 168 us -> 166 us (0.988)
  no operation moved by 1% of the time
where the time goes in v13:
time: 166 us
  waiting for transfers between devices  59.5 us (36%)
  Pallas kernels  55 us (33%)
  between operations  14.2 us (9%)
  starting transfers between devices  13.3 us (8%)
  matrix products  12.5 us (8%)
  local copies, waits for them, and re-layouts  8.68 us (5%)
  other arithmetic  2.96 us (2%)
    all_to_all x1, waiting for transfers between devices, per_device(): lax.all_to_all(send, ROW_AXES, split_axis=0, concat_axis=0, tiled=True)  59.4 us
    pallas_call x1, Pallas kernels, front_exchange(): pl.pallas_call(functools.partial(_front_kernel, n_x, n_zh, n_c), out_shap...  46.9 us
    all_to_all x1, starting transfers between devices, per_device(): lax.all_to_all(send, ROW_AXES, split_axis=0, concat_axis=0, tiled=True)  13.3 us
    pallas_call x1, Pallas kernels, add_tiles(): pl.pallas_call(functools.partial(_add_tiles_kernel, tile_cols, tiles_dev)...  8.1 us
    dot_general x1, matrix products, per_device(): lax.dot_general(own_full, partner, (((1,), (1,)), ((), ())), precision=la...  6.94 us
    dot_general x1, matrix products, per_device(): jnp.dot(to_rows(moved_panel), diag_inverse.T, precision=lax.Precision.HIG...  3.47 us
  transfers between devices with their start and end apart: 2, of which 1 were waited for; matrix products, arithmetic and copies ran while one was open for 6% of the time, Pallas kernels for 0%

profile of v13, /device:TPU:64, one launch (start us, length us, event | category | flops | bytes accessed | tf_op | source)
XLA Modules:
  0.0 166.0 jit_solution(2000830119156885178)
XLA Ops:
  7.2 0.0 copy-start
  7.2 0.0 all-gather.3.cloned.1.call-start
  7.2 46.9 %shard_map.77 = (f32[16,96,128]{2,1,0:T(8,128)}, f32[16,96,128]{2,1,0:T(8,128)}) custom-call(f32[96,128]{1,0:T(8,128)} %block_ref.1), custom_call_target="tpu_custom_call" | custom-call | tf_op jit(solution)/shard_map/pallas_call | solution.py:126
  54.1 0.0 copy-done
  54.1 0.0 copy-start.4
  54.1 3.5 %fusion = f32[4,96,512]{2,1,0:T(8,128)} fusion(f32[512,512]{1,0:T(8,128)S(1)} %copy-done, f32[4,4,12,8,128]{4,3,2,1,0:T(8,128)} %bitcast.47), kind=kOutput, calls=%fused_computation.3 | convolution fusion | flops 1207959552 | bytes 2621440 | tf_op jit(solution)/shard_map/dot_general | solution.py:220
  57.6 0.0 all-gather.3.cloned.1.call-update
  57.6 0.0 copy-done.4
  57.6 0.1 iota_compare_fusion
  57.7 0.0 copy-start.3
  57.7 0.1 fusion.12
  58.0 0.3 copy-done.5
  58.3 0.2 fusion.15
  58.5 0.1 scatter.15
  58.6 0.1 broadcast_in_dim.2
  58.6 0.2 copy-done.3
  58.9 1.8 %scatter_custom_fusion = f32[256,1152]{1,0:T(8,128)S(1)} fusion(f32[256,1152]{1,0:T(8,128)S(1)} %scatter.15, s32[192]{0:T(256)S(1)} %bitcast.57, f32[192,128]{1,0:T(8,128)S(1)} %broadcast_in_dim.2, f32[]{:T(128)} %constant.71, f32[192,1024]{1,0:T(8,128)S(1)} %bitcast.45), kind=kCustom, calls=%fused_computation.5 | custom fusion | flops 221184 | bytes 2064388 | tf_op jit(solution)/shard_map/scatter | solution.py:195
  60.6 1.7 %all_to_all.8 = f32[128,2,1152]{2,1,0:T(2,128)} reshape(f32[256,1152]{1,0:T(8,128)S(1)} %scatter_custom_fusion) | data formatting | bytes 2359296 | tf_op jit(solution)/shard_map/all_to_all | solution.py:197
  62.4 13.3 %all-to-all-start = ((f32[128,2,1152]{2,1,0:T(2,128)}), f32[128,2,1152]{2,1,0:T(2,128)S(1)}, u32[]{:S(2)}, u32[]{:S(2)}) async-start(f32[128,2,1152]{2,1,0:T(2,128)} %all_to_all.8), calls=%async_computation | async-start | bytes 2359296 | tf_op jit(solution)/shard_map/all_to_all | solution.py:197
  75.6 1.6 copy.27
  77.3 1.2 reshape_reshape.3
  78.5 2.1 %fusion.8 = f32[96,512]{1,0:T(8,128)S(1)} fusion(f32[512,512]{1,0:T(8,128)S(1)} %copy-done, f32[4,96,512]{2,1,0:T(8,128)} %reshape_reshape.3, s32[]{:T(128)S(6)} %select_n.18), kind=kOutput, calls=%fused_computation.12 | convolution fusion | flops 301989888 | bytes 1441796 | tf_op jit(solution)/shard_map/dot_general | solution.py:213
  80.5 0.7 copy-done.2
  81.2 0.6 constant_dynamic-slice_fusion
  81.8 59.4 %all-to-all-done = f32[128,2,1152]{2,1,0:T(2,128)S(1)} async-done(((f32[128,2,1152]{2,1,0:T(2,128)}), f32[128,2,1152]{2,1,0:T(2,128)S(1)}, u32[]{:S(2)}, u32[]{:S(2)}) %all-to-all-start) | async-done | bytes 1179680 | tf_op jit(solution)/shard_map/all_to_all | solution.py:197
  141.3 0.8 all_to_all.10
  142.1 0.1 slice_bitcast_fusion
  142.2 0.0 copy-start.1
  142.2 1.2 copy.19
  143.4 0.7 fusion.11.ids_ref
  144.1 6.9 %convolution_subtract_fusion.base_ref = f32[96,3072]{1,0:T(8,128)} fusion(f32[96,3072]{1,0:T(8,128)S(1)} %copy-done.1, f32[96,512]{1,0:T(8,128)} %copy-done.2, f32[3072,512]{1,0:T(8,128)} %bitcast.42), kind=kOutput, calls=%fused_computation.1 | convolution fusion | flops 906264576 | bytes 8847360 | tf_op jit(solution)/shard_map/dot_general | solution.py:229
  151.1 8.1 %shard_map.78 = f32[96,3072]{1,0:T(8,128)} custom-call(s32[256]{0:T(256)} %fusion.11.ids_ref, f32[96,3072]{1,0:T(8,128)} %convolution_subtract_fusion.base_ref, f32[256,8,128]{2,1,0:T(8,128)} %bitcast.43), custom_call_target="tpu_custom_call" | custom-call | tf_op jit(solution)/shard_map/pallas_call | solution.py:161
  (15 shorter events, 0.1 us)
Async XLA Ops:
  7.2 46.9 %copy-start = (f32[512,512]{1,0:T(8,128)S(1)}, f32[512,512]{1,0:T(8,128)}, u32[]{:S(2)}) copy-start(f32[512,512]{1,0:T(8,128)} %param.8) | copy-start | bytes 3145732
  7.2 136.9 %all-gather.3.cloned.1.call-start = ((), (), s32[]{:S(2)}) async-start(), calls=%async_computation.1 | async-start | bytes 7077888 | tf_op jit(solution)/shard_map/all_gather | solution.py:226
  54.1 3.5 %copy-start.4 = (s32[1,1,192,1]{2,3,1,0:T(1,128)S(1)}, s32[1,1,192,1]{2,3,1,0:T(1,128)}, u32[]{:S(2)}) copy-start(s32[1,1,192,1]{2,3,1,0:T(1,128)} %param.12) | copy-start | bytes 2308
  57.6 0.7 copy-start.5
  57.7 1.1 copy-start.3
  62.4 78.9 %all-to-all-start = ((f32[128,2,1152]{2,1,0:T(2,128)}), f32[128,2,1152]{2,1,0:T(2,128)S(1)}, u32[]{:S(2)}, u32[]{:S(2)}) async-start(f32[128,2,1152]{2,1,0:T(2,128)} %all_to_all.8), calls=%async_computation | async-start | bytes 2359296 | tf_op jit(solution)/shard_map/all_to_all | solution.py:197
  80.5 0.7 copy-start.2
  142.2 1.9 %copy-start.1 = (f32[96,3072]{1,0:T(8,128)S(1)}, f32[96,3072]{1,0:T(8,128)}, u32[]{:S(2)}) copy-start(f32[96,3072]{1,0:T(8,128)} %param.10) | copy-start | bytes 3538948
Sparse Core Ops, SparseCore 0:
  57.7 55.8 all-gather.2

commit v14 on v13

--- a/solution.py
+++ b/solution.py
@@ -194,6 +194,7 @@
         .at[position]
         .set(payload)
     )
+    send, panel = lax.optimization_barrier((send, panel))
     got = lax.all_to_all(send, ROW_AXES, split_axis=0, concat_axis=0, tiled=True)
     got_values = got[:, : tile_values.shape[1]]
     landing = got[:, tile_values.shape[1]].astype(jnp.int32)
@@ -220,7 +221,7 @@
     chosen = jnp.dot(
         to_rows(moved_panel),
         diag_inverse.T,
-        precision=lax.Precision.HIGHEST,
+        precision=lax.Precision.HIGH,
         preferred_element_type=jnp.float32,
     ).reshape(n_zh, local_rows, panel_width)
     gathered = lax.all_gather(chosen, ("y", "core"), axis=1, tiled=False)

time: 166 us -> 167 us (level)
  the two profiles are of different devices: /device:TPU:64 before, /device:TPU:1 now
where the time goes in v14:
time: 167 us; the launch traced here: 165 us
  Pallas kernels  54.7 us (33%)
  waiting for transfers between devices  53.8 us (32%)
  starting transfers between devices  16.1 us (10%)
  between operations  14.2 us (9%)
  matrix products  11.8 us (7%)
  local copies, waits for them, and re-layouts  8.23 us (5%)
  other arithmetic  5.77 us (3%)
    all_to_all x1, waiting for transfers between devices, per_device(): lax.all_to_all(send, ROW_AXES, split_axis=0, concat_axis=0, tiled=True)  53.7 us
    pallas_call x1, Pallas kernels, front_exchange(): pl.pallas_call(functools.partial(_front_kernel, n_x, n_zh, n_c), out_shap...  48.1 us
    all_to_all x1, starting transfers between devices, per_device(): lax.all_to_all(send, ROW_AXES, split_axis=0, concat_axis=0, tiled=True)  16 us
    dot_general x1, matrix products, per_device(): lax.dot_general(own_full, partner, (((1,), (1,)), ((), ())), precision=la...  6.94 us
    pallas_call x1, Pallas kernels, add_tiles(): pl.pallas_call(functools.partial(_add_tiles_kernel, tile_cols, tiles_dev)...  6.62 us
  transfers between devices with their start and end apart: 2, of which 1 were waited for; matrix products, arithmetic and copies ran while one was open for 5% of the time, Pallas kernels for 0%

profile of v14, /device:TPU:1, one launch (start us, length us, event | category | flops | bytes accessed | tf_op | source)
XLA Modules:
  0.0 164.6 jit_solution(4716722348757027545)
XLA Ops:
  7.2 0.0 copy-start
  7.2 0.0 all-gather.3.cloned.1.call-start
  7.2 0.8 convert_element_type.20
  8.0 0.8 iota_compare_fusion
  8.8 0.0 copy-start.3
  8.8 0.1 fusion.12
  9.0 0.9 fusion.15
  9.9 0.7 compare_select_fusion
  10.6 0.1 broadcast_in_dim.2
  10.7 0.1 scatter.15
  10.8 0.0 copy-done.3
  10.8 1.8 %scatter_custom_fusion = f32[256,1152]{1,0:T(8,128)S(1)} fusion(f32[256,1152]{1,0:T(8,128)S(1)} %scatter.15, s32[192]{0:T(256)S(1)} %bitcast.58, f32[192,128]{1,0:T(8,128)S(1)} %broadcast_in_dim.2, f32[]{:T(128)} %constant.71, f32[192,1024]{1,0:T(8,128)S(1)} %bitcast.46), kind=kCustom, calls=%fused_computation.5 | custom fusion | flops 221184 | bytes 2064388 | tf_op jit(solution)/shard_map/scatter | solution.py:195
  12.6 48.1 %shard_map.77 = (f32[16,96,128]{2,1,0:T(8,128)}, f32[16,96,128]{2,1,0:T(8,128)}) custom-call(f32[96,128]{1,0:T(8,128)} %block_ref), custom_call_target="tpu_custom_call" | custom-call | tf_op jit(solution)/shard_map/pallas_call | solution.py:126
  60.7 0.0 copy-done
  60.7 2.8 %fusion = f32[4,96,512]{2,1,0:T(8,128)} fusion(f32[512,512]{1,0:T(8,128)S(1)} %copy-done, f32[4,4,12,8,128]{4,3,2,1,0:T(8,128)} %bitcast.48), kind=kOutput, calls=%fused_computation.3 | convolution fusion | flops 603979776 | bytes 2621440 | tf_op jit(solution)/shard_map/dot_general | solution.py:221
  63.5 0.0 all-gather.3.cloned.1.call-update
  63.6 1.7 %all_to_all.8 = f32[128,2,1152]{2,1,0:T(2,128)} reshape(f32[256,1152]{1,0:T(8,128)S(1)} %scatter_custom_fusion) | data formatting | bytes 2359296 | tf_op jit(solution)/shard_map/all_to_all | solution.py:198
  65.3 16.0 %all-to-all-start = ((f32[128,2,1152]{2,1,0:T(2,128)}), f32[128,2,1152]{2,1,0:T(2,128)S(1)}, u32[]{:S(2)}, u32[]{:S(2)}) async-start(f32[128,2,1152]{2,1,0:T(2,128)} %all_to_all.8), calls=%async_computation | async-start | bytes 2359296 | tf_op jit(solution)/shard_map/all_to_all | solution.py:198
  81.3 1.7 %copy.27 = f32[4,4,96,128]{3,1,2,0:T(4,128)S(1)} copy(f32[4,4,96,128]{3,2,1,0:T(8,128)} %bitcast.47) | data formatting | bytes 1572864 | tf_op jit(solution)/shard_map/reshape | solution.py:208
  83.0 1.2 reshape_reshape.3
  84.2 2.1 %fusion.8 = f32[96,512]{1,0:T(8,128)S(1)} fusion(f32[512,512]{1,0:T(8,128)S(1)} %copy-done, f32[4,96,512]{2,1,0:T(8,128)} %reshape_reshape.3, s32[]{:T(128)S(6)} %select_n.18), kind=kOutput, calls=%fused_computation.12 | convolution fusion | flops 301989888 | bytes 1441796 | tf_op jit(solution)/shard_map/dot_general | solution.py:214
  86.3 0.0 copy-start.2
  86.3 0.7 copy-done.2
  87.0 0.6 constant_dynamic-slice_fusion
  87.6 53.7 %all-to-all-done = f32[128,2,1152]{2,1,0:T(2,128)S(1)} async-done(((f32[128,2,1152]{2,1,0:T(2,128)}), f32[128,2,1152]{2,1,0:T(2,128)S(1)}, u32[]{:S(2)}, u32[]{:S(2)}) %all-to-all-start) | async-done | bytes 1179680 | tf_op jit(solution)/shard_map/all_to_all | solution.py:198
  141.3 0.8 all_to_all.10
  142.1 0.1 slice_bitcast_fusion
  142.3 0.0 copy-start.1
  142.3 1.2 copy.19
  143.5 0.7 fusion.11.ids_ref
  144.2 6.9 %convolution_subtract_fusion.base_ref = f32[96,3072]{1,0:T(8,128)} fusion(f32[96,3072]{1,0:T(8,128)S(1)} %copy-done.1, f32[96,512]{1,0:T(8,128)} %copy-done.2, f32[3072,512]{1,0:T(8,128)} %bitcast.43), kind=kOutput, calls=%fused_computation.1 | convolution fusion | flops 906264576 | bytes 8847360 | tf_op jit(solution)/shard_map/dot_general | solution.py:230
  151.1 6.6 %shard_map.78 = f32[96,3072]{1,0:T(8,128)} custom-call(s32[256]{0:T(256)} %fusion.11.ids_ref, f32[96,3072]{1,0:T(8,128)} %convolution_subtract_fusion.base_ref, f32[256,8,128]{2,1,0:T(8,128)} %bitcast.44), custom_call_target="tpu_custom_call" | custom-call | tf_op jit(solution)/shard_map/pallas_call | solution.py:161
  (11 shorter events, 0.1 us)
Async XLA Ops:
  7.2 53.5 %copy-start = (f32[512,512]{1,0:T(8,128)S(1)}, f32[512,512]{1,0:T(8,128)}, u32[]{:S(2)}) copy-start(f32[512,512]{1,0:T(8,128)} %param.8) | copy-start | bytes 3145732
  7.2 137.0 %all-gather.3.cloned.1.call-start = ((), (), s32[]{:S(2)}) async-start(), calls=%async_computation.1 | async-start | bytes 7077888 | tf_op jit(solution)/shard_map/all_gather | solution.py:227
  8.8 2.0 %copy-start.3 = (f32[1,1,192,1024]{3,2,1,0:T(8,128)S(1)}, f32[1,1,192,1024]{3,2,1,0:T(8,128)}, u32[]{:S(2)}) copy-start(f32[1,1,192,1024]{3,2,1,0:T(8,128)} %param.11) | copy-start | bytes 2359300
  65.3 76.1 %all-to-all-start = ((f32[128,2,1152]{2,1,0:T(2,128)}), f32[128,2,1152]{2,1,0:T(2,128)S(1)}, u32[]{:S(2)}, u32[]{:S(2)}) async-start(f32[128,2,1152]{2,1,0:T(2,128)} %all_to_all.8), calls=%async_computation | async-start | bytes 2359296 | tf_op jit(solution)/shard_map/all_to_all | solution.py:198
  86.3 0.7 copy-start.2
  142.3 1.9 %copy-start.1 = (f32[96,3072]{1,0:T(8,128)S(1)}, f32[96,3072]{1,0:T(8,128)}, u32[]{:S(2)}) copy-start(f32[96,3072]{1,0:T(8,128)} %param.10) | copy-start | bytes 3538948
Sparse Core Ops, SparseCore 0:
  63.7 54.1 all-gather.2

commit v15 on v13

--- a/solution.py
+++ b/solution.py
@@ -35,16 +35,9 @@
     for other in (left, right):
         pl.semaphore_signal(barrier, 1, device_id=on_ring(other), device_id_type=MESH_IDS)
 
-    @pl.when(is_source)
-    def _():
-        for k in range(1, n_x):
-            pl.semaphore_signal(barrier, 1, device_id=x_peer(k), device_id_type=MESH_IDS)
-        pl.semaphore_wait(barrier, 2 + n_x - 1)
-
-    @pl.when(jnp.logical_not(is_source))
-    def _():
-        pl.semaphore_signal(barrier, 1, device_id={"x": col}, device_id_type=MESH_IDS)
-        pl.semaphore_wait(barrier, 3)
+    for k in (1, n_x - 1):
+        pl.semaphore_signal(barrier, 1, device_id=x_peer(k), device_id_type=MESH_IDS)
+    pl.semaphore_wait(barrier, 4)
 
     ring_ref[me] = block_ref[...]
 
@@ -52,7 +45,7 @@
         return pltpu.make_async_remote_copy(
             src_ref=src,
             dst_ref=moved_ref.at[slot],
-            send_sem=xsend_sem.at[slot, k - 1],
+            send_sem=xsend_sem.at[slot, 0 if k == 1 else 1],
             recv_sem=xrecv_sem.at[0],
             device_id=x_peer(k),
             device_id_type=MESH_IDS,
@@ -61,7 +54,7 @@
     def forward_x(slot, src):
         @pl.when(is_source)
         def _():
-            for k in range(1, n_x):
+            for k in (1, n_x - 1):
                 x_copy(slot, src, k).start()
 
     counts = (n // 2, n - 1 - n // 2)
@@ -100,11 +93,13 @@
     @pl.when(is_source)
     def _():
         for slot in range(n):
-            for k in range(1, n_x):
+            for k in (1, n_x - 1):
                 x_copy(slot, ring_ref.at[slot], k).wait_send()
         local = pltpu.make_async_copy(ring_ref, moved_ref, local_sem.at[0])
         local.start()
         local.wait()
+
+    shift = lax.rem(x - col + n_x, n_x)
 
     @pl.when(jnp.logical_not(is_source))
     def _():
@@ -117,6 +112,22 @@
             device_id_type=MESH_IDS,
         )
         whole.wait_recv()
+
+    half = n // 2
+    for role, first, k in ((1, 0, 1), (n_x - 1, half, n_x - 1)):
+        @pl.when(shift == role)
+        def _():
+            part = pl.ds(first, half)
+            onward = pltpu.make_async_remote_copy(
+                src_ref=moved_ref.at[part],
+                dst_ref=moved_ref.at[part],
+                send_sem=xsend_sem.at[0, 2],
+                recv_sem=xrecv_sem.at[0],
+                device_id=x_peer(k),
+                device_id_type=MESH_IDS,
+            )
+            onward.start()
+            onward.wait_send()
 
 
 def front_exchange(block, n_x, n_zh, n_c):

time: 166 us -> 165 us (level)
  the two profiles are of different devices: /device:TPU:64 before, /device:TPU:1 now
where the time goes in v15:
time: 165 us
  waiting for transfers between devices  56 us (34%)
  Pallas kernels  44.2 us (27%)
  starting transfers between devices  26.2 us (16%)
  between operations  14.2 us (9%)
  matrix products  12.5 us (8%)
  local copies, waits for them, and re-layouts  8.68 us (5%)
  other arithmetic  2.96 us (2%)
    all_to_all x1, waiting for transfers between devices, per_device(): lax.all_to_all(send, ROW_AXES, split_axis=0, concat_axis=0, tiled=True)  55.9 us
    pallas_call x1, Pallas kernels, front_exchange(): pl.pallas_call(functools.partial(_front_kernel, n_x, n_zh, n_c), out_shap...  37.6 us
    all_to_all x1, starting transfers between devices, per_device(): lax.all_to_all(send, ROW_AXES, split_axis=0, concat_axis=0, tiled=True)  26.2 us
    dot_general x1, matrix products, per_device(): lax.dot_general(own_full, partner, (((1,), (1,)), ((), ())), precision=la...  6.94 us
    pallas_call x1, Pallas kernels, add_tiles(): pl.pallas_call(functools.partial(_add_tiles_kernel, tile_cols, tiles_dev)...  6.62 us
    dot_general x1, matrix products, per_device(): jnp.dot(to_rows(moved_panel), diag_inverse.T, precision=lax.Precision.HIG...  3.47 us
  transfers between devices with their start and end apart: 2, of which 1 were waited for; matrix products, arithmetic and copies ran while one was open for 6% of the time, Pallas kernels for 0%

profile of v15, /device:TPU:1, one launch (start us, length us, event | category | flops | bytes accessed | tf_op | source)
XLA Modules:
  0.0 164.7 jit_solution(16604160357101214587)
XLA Ops:
  7.2 0.0 copy-start
  7.2 0.0 all-gather.3.cloned.1.call-start
  7.2 37.6 %shard_map.77 = (f32[16,96,128]{2,1,0:T(8,128)}, f32[16,96,128]{2,1,0:T(8,128)}) custom-call(f32[96,128]{1,0:T(8,128)} %block_ref.1), custom_call_target="tpu_custom_call" | custom-call | tf_op jit(solution)/shard_map/pallas_call | solution.py:137
  44.8 0.0 copy-done
  44.8 0.0 copy-start.4
  44.8 3.5 %fusion = f32[4,96,512]{2,1,0:T(8,128)} fusion(f32[512,512]{1,0:T(8,128)S(1)} %copy-done, f32[4,4,12,8,128]{4,3,2,1,0:T(8,128)} %bitcast.47), kind=kOutput, calls=%fused_computation.3 | convolution fusion | flops 1207959552 | bytes 2621440 | tf_op jit(solution)/shard_map/dot_general | solution.py:231
  48.3 0.0 all-gather.3.cloned.1.call-update
  48.3 0.0 copy-done.4
  48.3 0.1 iota_compare_fusion
  48.4 0.0 copy-start.3
  48.5 0.1 fusion.12
  48.7 0.3 copy-done.5
  49.0 0.2 fusion.15
  49.2 0.1 scatter.15
  49.3 0.1 broadcast_in_dim.2
  49.4 0.2 copy-done.3
  49.6 1.8 %scatter_custom_fusion = f32[256,1152]{1,0:T(8,128)S(1)} fusion(f32[256,1152]{1,0:T(8,128)S(1)} %scatter.15, s32[192]{0:T(256)S(1)} %bitcast.57, f32[192,128]{1,0:T(8,128)S(1)} %broadcast_in_dim.2, f32[]{:T(128)} %constant.71, f32[192,1024]{1,0:T(8,128)S(1)} %bitcast.45), kind=kCustom, calls=%fused_computation.5 | custom fusion | flops 221184 | bytes 2064388 | tf_op jit(solution)/shard_map/scatter | solution.py:206
  51.4 1.7 %all_to_all.8 = f32[128,2,1152]{2,1,0:T(2,128)} reshape(f32[256,1152]{1,0:T(8,128)S(1)} %scatter_custom_fusion) | data formatting | bytes 2359296 | tf_op jit(solution)/shard_map/all_to_all | solution.py:208
  53.1 26.2 %all-to-all-start = ((f32[128,2,1152]{2,1,0:T(2,128)}), f32[128,2,1152]{2,1,0:T(2,128)S(1)}, u32[]{:S(2)}, u32[]{:S(2)}) async-start(f32[128,2,1152]{2,1,0:T(2,128)} %all_to_all.8), calls=%async_computation | async-start | bytes 2359296 | tf_op jit(solution)/shard_map/all_to_all | solution.py:208
  79.2 1.6 copy.27
  80.9 1.2 reshape_reshape.3
  82.1 2.1 %fusion.8 = f32[96,512]{1,0:T(8,128)S(1)} fusion(f32[512,512]{1,0:T(8,128)S(1)} %copy-done, f32[4,96,512]{2,1,0:T(8,128)} %reshape_reshape.3, s32[]{:T(128)S(6)} %select_n.18), kind=kOutput, calls=%fused_computation.12 | convolution fusion | flops 301989888 | bytes 1441796 | tf_op jit(solution)/shard_map/dot_general | solution.py:224
  84.2 0.7 copy-done.2
  84.8 0.6 constant_dynamic-slice_fusion
  85.5 55.9 %all-to-all-done = f32[128,2,1152]{2,1,0:T(2,128)S(1)} async-done(((f32[128,2,1152]{2,1,0:T(2,128)}), f32[128,2,1152]{2,1,0:T(2,128)S(1)}, u32[]{:S(2)}, u32[]{:S(2)}) %all-to-all-start) | async-done | bytes 1179680 | tf_op jit(solution)/shard_map/all_to_all | solution.py:208
  141.4 0.8 all_to_all.10
  142.2 0.1 slice_bitcast_fusion
  142.3 0.0 copy-start.1
  142.4 1.2 copy.19
  143.6 0.7 fusion.11.ids_ref
  144.3 6.9 %convolution_subtract_fusion.base_ref = f32[96,3072]{1,0:T(8,128)} fusion(f32[96,3072]{1,0:T(8,128)S(1)} %copy-done.1, f32[96,512]{1,0:T(8,128)} %copy-done.2, f32[3072,512]{1,0:T(8,128)} %bitcast.42), kind=kOutput, calls=%fused_computation.1 | convolution fusion | flops 906264576 | bytes 8847360 | tf_op jit(solution)/shard_map/dot_general | solution.py:240
  151.2 6.6 %shard_map.78 = f32[96,3072]{1,0:T(8,128)} custom-call(s32[256]{0:T(256)} %fusion.11.ids_ref, f32[96,3072]{1,0:T(8,128)} %convolution_subtract_fusion.base_ref, f32[256,8,128]{2,1,0:T(8,128)} %bitcast.43), custom_call_target="tpu_custom_call" | custom-call | tf_op jit(solution)/shard_map/pallas_call | solution.py:172
  (15 shorter events, 0.1 us)
Async XLA Ops:
  7.2 37.6 %copy-start = (f32[512,512]{1,0:T(8,128)S(1)}, f32[512,512]{1,0:T(8,128)}, u32[]{:S(2)}) copy-start(f32[512,512]{1,0:T(8,128)} %param.8) | copy-start | bytes 3145732
  7.2 137.1 %all-gather.3.cloned.1.call-start = ((), (), s32[]{:S(2)}) async-start(), calls=%async_computation.1 | async-start | bytes 7077888 | tf_op jit(solution)/shard_map/all_gather | solution.py:237
  44.8 3.5 %copy-start.4 = (s32[1,1,192,1]{2,3,1,0:T(1,128)S(1)}, s32[1,1,192,1]{2,3,1,0:T(1,128)}, u32[]{:S(2)}) copy-start(s32[1,1,192,1]{2,3,1,0:T(1,128)} %param.12) | copy-start | bytes 2308
  48.3 0.7 copy-start.5
  48.4 1.1 copy-start.3
  53.1 88.3 %all-to-all-start = ((f32[128,2,1152]{2,1,0:T(2,128)}), f32[128,2,1152]{2,1,0:T(2,128)S(1)}, u32[]{:S(2)}, u32[]{:S(2)}) async-start(f32[128,2,1152]{2,1,0:T(2,128)} %all_to_all.8), calls=%async_computation | async-start | bytes 2359296 | tf_op jit(solution)/shard_map/all_to_all | solution.py:208
  84.1 0.7 copy-start.2
  142.3 1.9 %copy-start.1 = (f32[96,3072]{1,0:T(8,128)S(1)}, f32[96,3072]{1,0:T(8,128)}, u32[]{:S(2)}) copy-start(f32[96,3072]{1,0:T(8,128)} %param.10) | copy-start | bytes 3538948
Sparse Core Ops, SparseCore 0:
  48.4 62.8 all-gather.2

commit v16 on v15

--- a/solution.py
+++ b/solution.py
@@ -231,7 +231,7 @@
     chosen = jnp.dot(
         to_rows(moved_panel),
         diag_inverse.T,
-        precision=lax.Precision.HIGHEST,
+        precision=lax.Precision.HIGH,
         preferred_element_type=jnp.float32,
     ).reshape(n_zh, local_rows, panel_width)
     gathered = lax.all_gather(chosen, ("y", "core"), axis=1, tiled=False)

time: 165 us -> 166 us (level)
  no operation moved by 1% of the time
where the time goes in v16:
time: 166 us
  waiting for transfers between devices  56 us (34%)
  Pallas kernels  45.7 us (28%)
  starting transfers between devices  26.2 us (16%)
  between operations  14.2 us (9%)
  matrix products  11.8 us (7%)
  local copies, waits for them, and re-layouts  8.68 us (5%)
  other arithmetic  2.96 us (2%)
    all_to_all x1, waiting for transfers between devices, per_device(): lax.all_to_all(send, ROW_AXES, split_axis=0, concat_axis=0, tiled=True)  55.9 us
    pallas_call x1, Pallas kernels, front_exchange(): pl.pallas_call(functools.partial(_front_kernel, n_x, n_zh, n_c), out_shap...  37.6 us
    all_to_all x1, starting transfers between devices, per_device(): lax.all_to_all(send, ROW_AXES, split_axis=0, concat_axis=0, tiled=True)  26.2 us
    pallas_call x1, Pallas kernels, add_tiles(): pl.pallas_call(functools.partial(_add_tiles_kernel, tile_cols, tiles_dev)...  8.1 us
    dot_general x1, matrix products, per_device(): lax.dot_general(own_full, partner, (((1,), (1,)), ((), ())), precision=la...  6.94 us
  transfers between devices with their start and end apart: 2, of which 1 were waited for; matrix products, arithmetic and copies ran while one was open for 6% of the time, Pallas kernels for 0%

profile of v16, /device:TPU:1, one launch (start us, length us, event | category | flops | bytes accessed | tf_op | source)
XLA Modules:
  0.0 165.5 jit_solution(16272118599000652869)
XLA Ops:
  7.2 0.0 copy-start
  7.2 0.0 all-gather.3.cloned.1.call-start
  7.2 37.6 %shard_map.77 = (f32[16,96,128]{2,1,0:T(8,128)}, f32[16,96,128]{2,1,0:T(8,128)}) custom-call(f32[96,128]{1,0:T(8,128)} %block_ref.1), custom_call_target="tpu_custom_call" | custom-call | tf_op jit(solution)/shard_map/pallas_call | solution.py:137
  44.8 0.0 copy-done
  44.8 0.0 copy-start.4
  44.8 2.9 %fusion = f32[4,96,512]{2,1,0:T(8,128)} fusion(f32[512,512]{1,0:T(8,128)S(1)} %copy-done, f32[4,4,12,8,128]{4,3,2,1,0:T(8,128)} %bitcast.47), kind=kOutput, calls=%fused_computation.3 | convolution fusion | flops 603979776 | bytes 2621440 | tf_op jit(solution)/shard_map/dot_general | solution.py:231
  47.7 0.0 all-gather.3.cloned.1.call-update
  47.7 0.0 copy-done.4
  47.7 0.1 iota_compare_fusion
  47.8 0.0 copy-start.3
  47.9 0.1 fusion.12
  48.1 0.3 copy-done.5
  48.4 0.2 fusion.15
  48.6 0.1 scatter.15
  48.7 0.1 broadcast_in_dim.2
  48.7 0.2 copy-done.3
  49.0 1.8 %scatter_custom_fusion = f32[256,1152]{1,0:T(8,128)S(1)} fusion(f32[256,1152]{1,0:T(8,128)S(1)} %scatter.15, s32[192]{0:T(256)S(1)} %bitcast.57, f32[192,128]{1,0:T(8,128)S(1)} %broadcast_in_dim.2, f32[]{:T(128)} %constant.71, f32[192,1024]{1,0:T(8,128)S(1)} %bitcast.45), kind=kCustom, calls=%fused_computation.5 | custom fusion | flops 221184 | bytes 2064388 | tf_op jit(solution)/shard_map/scatter | solution.py:206
  50.8 1.7 %all_to_all.8 = f32[128,2,1152]{2,1,0:T(2,128)} reshape(f32[256,1152]{1,0:T(8,128)S(1)} %scatter_custom_fusion) | data formatting | bytes 2359296 | tf_op jit(solution)/shard_map/all_to_all | solution.py:208
  52.5 26.2 %all-to-all-start = ((f32[128,2,1152]{2,1,0:T(2,128)}), f32[128,2,1152]{2,1,0:T(2,128)S(1)}, u32[]{:S(2)}, u32[]{:S(2)}) async-start(f32[128,2,1152]{2,1,0:T(2,128)} %all_to_all.8), calls=%async_computation | async-start | bytes 2359296 | tf_op jit(solution)/shard_map/all_to_all | solution.py:208
  78.6 1.6 copy.27
  80.3 1.2 reshape_reshape.3
  81.5 2.1 %fusion.8 = f32[96,512]{1,0:T(8,128)S(1)} fusion(f32[512,512]{1,0:T(8,128)S(1)} %copy-done, f32[4,96,512]{2,1,0:T(8,128)} %reshape_reshape.3, s32[]{:T(128)S(6)} %select_n.18), kind=kOutput, calls=%fused_computation.12 | convolution fusion | flops 301989888 | bytes 1441796 | tf_op jit(solution)/shard_map/dot_general | solution.py:224
  83.5 0.7 copy-done.2
  84.2 0.6 constant_dynamic-slice_fusion
  84.8 55.9 %all-to-all-done = f32[128,2,1152]{2,1,0:T(2,128)S(1)} async-done(((f32[128,2,1152]{2,1,0:T(2,128)}), f32[128,2,1152]{2,1,0:T(2,128)S(1)}, u32[]{:S(2)}, u32[]{:S(2)}) %all-to-all-start) | async-done | bytes 1179680 | tf_op jit(solution)/shard_map/all_to_all | solution.py:208
  140.8 0.8 all_to_all.10
  141.6 0.1 slice_bitcast_fusion
  141.7 0.0 copy-start.1
  141.7 1.2 copy.19
  142.9 0.7 fusion.11.ids_ref
  143.6 6.9 %convolution_subtract_fusion.base_ref = f32[96,3072]{1,0:T(8,128)} fusion(f32[96,3072]{1,0:T(8,128)S(1)} %copy-done.1, f32[96,512]{1,0:T(8,128)} %copy-done.2, f32[3072,512]{1,0:T(8,128)} %bitcast.42), kind=kOutput, calls=%fused_computation.1 | convolution fusion | flops 906264576 | bytes 8847360 | tf_op jit(solution)/shard_map/dot_general | solution.py:240
  150.6 8.1 %shard_map.78 = f32[96,3072]{1,0:T(8,128)} custom-call(s32[256]{0:T(256)} %fusion.11.ids_ref, f32[96,3072]{1,0:T(8,128)} %convolution_subtract_fusion.base_ref, f32[256,8,128]{2,1,0:T(8,128)} %bitcast.43), custom_call_target="tpu_custom_call" | custom-call | tf_op jit(solution)/shard_map/pallas_call | solution.py:172
  (15 shorter events, 0.1 us)
Async XLA Ops:
  7.2 37.6 %copy-start = (f32[512,512]{1,0:T(8,128)S(1)}, f32[512,512]{1,0:T(8,128)}, u32[]{:S(2)}) copy-start(f32[512,512]{1,0:T(8,128)} %param.8) | copy-start | bytes 3145732
  7.2 136.5 %all-gather.3.cloned.1.call-start = ((), (), s32[]{:S(2)}) async-start(), calls=%async_computation.1 | async-start | bytes 7077888 | tf_op jit(solution)/shard_map/all_gather | solution.py:237
  44.8 2.9 %copy-start.4 = (s32[1,1,192,1]{2,3,1,0:T(1,128)S(1)}, s32[1,1,192,1]{2,3,1,0:T(1,128)}, u32[]{:S(2)}) copy-start(s32[1,1,192,1]{2,3,1,0:T(1,128)} %param.12) | copy-start | bytes 2308
  47.7 0.7 copy-start.5
  47.8 1.1 copy-start.3
  52.5 88.3 %all-to-all-start = ((f32[128,2,1152]{2,1,0:T(2,128)}), f32[128,2,1152]{2,1,0:T(2,128)S(1)}, u32[]{:S(2)}, u32[]{:S(2)}) async-start(f32[128,2,1152]{2,1,0:T(2,128)} %all_to_all.8), calls=%async_computation | async-start | bytes 2359296 | tf_op jit(solution)/shard_map/all_to_all | solution.py:208
  83.5 0.7 copy-start.2
  141.7 1.9 %copy-start.1 = (f32[96,3072]{1,0:T(8,128)S(1)}, f32[96,3072]{1,0:T(8,128)}, u32[]{:S(2)}) copy-start(f32[96,3072]{1,0:T(8,128)} %param.10) | copy-start | bytes 3538948
Sparse Core Ops, SparseCore 0:
  47.8 62.8 all-gather.2

commit v17 on v15

--- a/solution.py
+++ b/solution.py
@@ -199,13 +199,15 @@
     id_lanes = jnp.broadcast_to(tile_ids.astype(jnp.float32)[:, None], (tile_ids.shape[0], TILE_COLS))
     payload = jnp.concatenate([tile_values, id_lanes], axis=1)
     send = (
-        jnp.zeros((row_devices * CAP, payload.shape[1]), jnp.float32)
-        .at[:, tile_values.shape[1]:]
+        jnp.zeros((row_devices, CAP, payload.shape[1]), jnp.float32)
+        .at[:, :, tile_values.shape[1]:]
         .set(float(tiles_dev))
-        .at[position]
+        .at[targets, ranks]
         .set(payload)
     )
+    send, panel = lax.optimization_barrier((send, panel))
     got = lax.all_to_all(send, ROW_AXES, split_axis=0, concat_axis=0, tiled=True)
+    got = got.reshape(row_devices * CAP, payload.shape[1])
     got_values = got[:, : tile_values.shape[1]]
     landing = got[:, tile_values.shape[1]].astype(jnp.int32)
 

time: 165 us -> 193 us (1.17)
  local copies, waits for them, and re-layouts: 8.68 us -> 34.7 us
    scatter x2 -> x1, local copies, waits for them, and re-layouts: 0.09 us -> 25.8 us  [per_device(): send = jnp.zeros((row_devices, CAP, payload.shape[1]), jnp.float32).at[:,...]
    all_to_all x2 -> x0, local copies, waits for them, and re-layouts: 2.52 us -> none  [per_device(): lax.all_to_all(send, ROW_AXES, split_axis=0, concat_axis=0, tiled=True)]
    unnamed x15 -> x12, local copies, waits for them, and re-layouts: 2.52 us -> 4.49 us
  transfers between devices with their start and end apart: 2 -> 2, of which waited for: 1 -> 1; matrix products, arithmetic and copies ran while one was open for 6% -> 4% of each run, Pallas kernels for 0% -> 0%
where the time goes in v17:
time: 193 us; the launch traced here: 192 us
  waiting for transfers between devices  55.9 us (29%)
  Pallas kernels  44.1 us (23%)
  local copies, waits for them, and re-layouts  34.7 us (18%)
  starting transfers between devices  26.2 us (14%)
  between operations  14.2 us (7%)
  matrix products  12.5 us (6%)
  other arithmetic  4.04 us (2%)
    all_to_all x1, waiting for transfers between devices, per_device(): lax.all_to_all(send, ROW_AXES, split_axis=0, concat_axis=0, tiled=True)  55.9 us
    pallas_call x1, Pallas kernels, front_exchange(): pl.pallas_call(functools.partial(_front_kernel, n_x, n_zh, n_c), out_shap...  37.4 us
    all_to_all x1, starting transfers between devices, per_device(): lax.all_to_all(send, ROW_AXES, split_axis=0, concat_axis=0, tiled=True)  26.2 us
    scatter x1, local copies, waits for them, and re-layouts, per_device(): send = jnp.zeros((row_devices, CAP, payload.shape[1]), jnp.float32).at[:,...  25.8 us
    dot_general x1, matrix products, per_device(): lax.dot_general(own_full, partner, (((1,), (1,)), ((), ())), precision=la...  6.94 us
    pallas_call x1, Pallas kernels, add_tiles(): pl.pallas_call(functools.partial(_add_tiles_kernel, tile_cols, tiles_dev)...  6.62 us
    unnamed x12, local copies, waits for them, and re-layouts  4.49 us
  transfers between devices with their start and end apart: 2, of which 1 were waited for; matrix products, arithmetic and copies ran while one was open for 4% of the time, Pallas kernels for 0%

profile of v17, /device:TPU:1, one launch (start us, length us, event | category | flops | bytes accessed | tf_op | source)
XLA Modules:
  0.0 191.5 jit_solution(13661376741256917887)
XLA Ops:
  7.2 0.0 copy-start
  7.2 0.0 all-gather.3.cloned.1.call-start
  7.2 0.8 convert_element_type.20
  8.0 0.8 iota_compare_fusion
  8.8 0.1 fusion.8
  9.0 0.9 fusion.11
  9.9 0.7 or_select_fusion
  10.6 2.5 %copy.30 = f32[128,2,1152]{2,1,0:T(2,128)} copy(f32[128,2,1152]{2,1,0:T(2,128)} %constant.51.clone.1) | data formatting | bytes 2359296
  13.1 0.1 broadcast_in_dim.2
  13.1 0.0 copy-done.3
  13.1 0.1 pad_maximum_fusion
  13.2 25.8 %scatter_fusion = f32[128,2,1152]{2,1,0:T(2,128)} fusion(f32[128,2,1152]{2,1,0:T(2,128)} %copy.30, s32[192]{0:T(256)S(1)} %bitcast.41, f32[192,1152]{1,0:T(8,128)S(1)} %pad_maximum_fusion), kind=kCustom, calls=%fused_computation | custom fusion | bytes 2655744 | tf_op jit(solution)/shard_map/scatter | solution.py:206
  39.0 37.4 %shard_map.77 = (f32[16,96,128]{2,1,0:T(8,128)}, f32[16,96,128]{2,1,0:T(8,128)}) custom-call(f32[96,128]{1,0:T(8,128)} %block_ref), custom_call_target="tpu_custom_call" | custom-call | tf_op jit(solution)/shard_map/pallas_call | solution.py:137
  76.5 0.0 copy-done
  76.5 3.5 %fusion = f32[4,96,512]{2,1,0:T(8,128)} fusion(f32[512,512]{1,0:T(8,128)S(1)} %copy-done, f32[4,4,12,8,128]{4,3,2,1,0:T(8,128)} %bitcast.47), kind=kOutput, calls=%fused_computation.3 | convolution fusion | flops 1207959552 | bytes 2621440 | tf_op jit(solution)/shard_map/dot_general | solution.py:233
  79.9 0.0 all-gather.3.cloned.1.call-update
  80.0 26.2 %all-to-all-start = ((f32[128,2,1152]{2,1,0:T(2,128)}), f32[128,2,1152]{2,1,0:T(2,128)S(1)}, u32[]{:S(2)}, u32[]{:S(2)}) async-start(f32[128,2,1152]{2,1,0:T(2,128)} %scatter_fusion), calls=%async_computation | async-start | bytes 2359296 | tf_op jit(solution)/shard_map/all_to_all | solution.py:209
  106.1 1.7 copy.27
  107.8 1.2 reshape_reshape.3
  109.0 2.1 %fusion.4 = f32[96,512]{1,0:T(8,128)S(1)} fusion(f32[512,512]{1,0:T(8,128)S(1)} %copy-done, f32[4,96,512]{2,1,0:T(8,128)} %reshape_reshape.3, s32[]{:T(128)S(6)} %select_n.29), kind=kOutput, calls=%fused_computation.9 | convolution fusion | flops 301989888 | bytes 1441796 | tf_op jit(solution)/shard_map/dot_general | solution.py:226
  111.1 0.0 copy-start.2
  111.1 0.7 copy-done.2
  111.8 0.6 constant_dynamic-slice_fusion
  112.4 55.9 %all-to-all-done = f32[128,2,1152]{2,1,0:T(2,128)S(1)} async-done(((f32[128,2,1152]{2,1,0:T(2,128)}), f32[128,2,1152]{2,1,0:T(2,128)S(1)}, u32[]{:S(2)}, u32[]{:S(2)}) %all-to-all-start) | async-done | bytes 1179680 | tf_op jit(solution)/shard_map/all_to_all | solution.py:209
  168.3 0.8 reshape.127
  169.1 0.1 slice_bitcast_fusion
  169.2 0.0 copy-start.1
  169.2 1.2 copy.19
  170.4 0.7 fusion.7.ids_ref
  171.1 0.0 copy-done.1
  171.1 6.9 %convolution_subtract_fusion.base_ref = f32[96,3072]{1,0:T(8,128)} fusion(f32[96,3072]{1,0:T(8,128)S(1)} %copy-done.1, f32[96,512]{1,0:T(8,128)} %copy-done.2, f32[3072,512]{1,0:T(8,128)} %bitcast.42), kind=kOutput, calls=%fused_computation.1 | convolution fusion | flops 906264576 | bytes 8847360 | tf_op jit(solution)/shard_map/dot_general | solution.py:242
  178.1 6.6 %shard_map.78 = f32[96,3072]{1,0:T(8,128)} custom-call(s32[256]{0:T(256)} %fusion.7.ids_ref, f32[96,3072]{1,0:T(8,128)} %convolution_subtract_fusion.base_ref, f32[256,8,128]{2,1,0:T(8,128)} %bitcast.43), custom_call_target="tpu_custom_call" | custom-call | tf_op jit(solution)/shard_map/pallas_call | solution.py:172
  (9 shorter events, 0.1 us)
Async XLA Ops:
  7.2 69.3 %copy-start = (f32[512,512]{1,0:T(8,128)S(1)}, f32[512,512]{1,0:T(8,128)}, u32[]{:S(2)}) copy-start(f32[512,512]{1,0:T(8,128)} %param.8) | copy-start | bytes 3145732
  7.2 164.0 %all-gather.3.cloned.1.call-start = ((), (), s32[]{:S(2)}) async-start(), calls=%async_computation.1 | async-start | bytes 7077888 | tf_op jit(solution)/shard_map/all_gather | solution.py:239
  10.6 2.6 %copy-start.3 = (f32[1,1,192,1024]{3,2,1,0:T(8,128)S(1)}, f32[1,1,192,1024]{3,2,1,0:T(8,128)}, u32[]{:S(2)}) copy-start(f32[1,1,192,1024]{3,2,1,0:T(8,128)} %param.11) | copy-start | bytes 2359300
  80.0 88.3 %all-to-all-start = ((f32[128,2,1152]{2,1,0:T(2,128)}), f32[128,2,1152]{2,1,0:T(2,128)S(1)}, u32[]{:S(2)}, u32[]{:S(2)}) async-start(f32[128,2,1152]{2,1,0:T(2,128)} %scatter_fusion), calls=%async_computation | async-start | bytes 2359296 | tf_op jit(solution)/shard_map/all_to_all | solution.py:209
  111.1 0.7 copy-start.2
  169.2 1.9 copy-start.1
Sparse Core Ops, SparseCore 0:
  80.1 62.9 all-gather.2

commit v18 on v15

--- a/solution.py
+++ b/solution.py
@@ -205,7 +205,10 @@
         .at[position]
         .set(payload)
     )
+    send = send.reshape(row_devices, CAP, payload.shape[1])
+    send, panel = lax.optimization_barrier((send, panel))
     got = lax.all_to_all(send, ROW_AXES, split_axis=0, concat_axis=0, tiled=True)
+    got = got.reshape(row_devices * CAP, payload.shape[1])
     got_values = got[:, : tile_values.shape[1]]
     landing = got[:, tile_values.shape[1]].astype(jnp.int32)
 

time: 165 us -> 168 us (1.018)
  other arithmetic: 2.96 us -> 5.77 us
    all_to_all x2 -> x0, local copies, waits for them, and re-layouts: 2.52 us -> none  [per_device(): lax.all_to_all(send, ROW_AXES, split_axis=0, concat_axis=0, tiled=True)]
    reshape x0 -> x2, local copies, waits for them, and re-layouts: none -> 2.52 us  [the longest x1 1.71 us: per_device(): send = send.reshape(row_devices, CAP, payload.shape[1])]
  transfers between devices with their start and end apart: 2 -> 2, of which waited for: 1 -> 1; matrix products, arithmetic and copies ran while one was open for 6% -> 5% of each run, Pallas kernels for 0% -> 0%
where the time goes in v18:
time: 168 us; the launch traced here: 167 us
  waiting for transfers between devices  55.9 us (33%)
  Pallas kernels  44.1 us (26%)
  starting transfers between devices  26.2 us (16%)
  between operations  14.2 us (8%)
  matrix products  12.5 us (7%)
  local copies, waits for them, and re-layouts  8.23 us (5%)
  other arithmetic  5.77 us (3%)
    all_to_all x1, waiting for transfers between devices, per_device(): lax.all_to_all(send, ROW_AXES, split_axis=0, concat_axis=0, tiled=True)  55.9 us
    pallas_call x1, Pallas kernels, front_exchange(): pl.pallas_call(functools.partial(_front_kernel, n_x, n_zh, n_c), out_shap...  37.4 us
    all_to_all x1, starting transfers between devices, per_device(): lax.all_to_all(send, ROW_AXES, split_axis=0, concat_axis=0, tiled=True)  26.2 us
    dot_general x1, matrix products, per_device(): lax.dot_general(own_full, partner, (((1,), (1,)), ((), ())), precision=la...  6.94 us
    pallas_call x1, Pallas kernels, add_tiles(): pl.pallas_call(functools.partial(_add_tiles_kernel, tile_cols, tiles_dev)...  6.62 us
    dot_general x1, matrix products, per_device(): jnp.dot(to_rows(moved_panel), diag_inverse.T, precision=lax.Precision.HIG...  3.47 us
  transfers between devices with their start and end apart: 2, of which 1 were waited for; matrix products, arithmetic and copies ran while one was open for 5% of the time, Pallas kernels for 0%

profile of v18, /device:TPU:1, one launch (start us, length us, event | category | flops | bytes accessed | tf_op | source)
XLA Modules:
  0.0 166.8 jit_solution(17304739315765919532)
XLA Ops:
  7.2 0.0 copy-start
  7.2 0.0 all-gather.3.cloned.1.call-start
  7.2 0.8 convert_element_type.20
  8.0 0.8 iota_compare_fusion
  8.8 0.0 copy-start.3
  8.8 0.1 fusion.12
  9.0 0.9 fusion.15
  9.9 0.7 compare_select_fusion
  10.6 0.1 broadcast_in_dim.2
  10.7 0.1 scatter.15
  10.8 0.0 copy-done.3
  10.8 1.8 %scatter_custom_fusion = f32[256,1152]{1,0:T(8,128)S(1)} fusion(f32[256,1152]{1,0:T(8,128)S(1)} %scatter.15, s32[192]{0:T(256)S(1)} %bitcast.58, f32[192,128]{1,0:T(8,128)S(1)} %broadcast_in_dim.2, f32[]{:T(128)} %constant.71, f32[192,1024]{1,0:T(8,128)S(1)} %bitcast.46), kind=kCustom, calls=%fused_computation.5 | custom fusion | flops 221184 | bytes 2064388 | tf_op jit(solution)/shard_map/scatter | solution.py:206
  12.6 1.7 %reshape.109 = f32[128,2,1152]{2,1,0:T(2,128)} reshape(f32[256,1152]{1,0:T(8,128)S(1)} %scatter_custom_fusion) | data formatting | bytes 2359296 | tf_op jit(solution)/shard_map/reshape | solution.py:208
  14.3 37.4 %shard_map.77 = (f32[16,96,128]{2,1,0:T(8,128)}, f32[16,96,128]{2,1,0:T(8,128)}) custom-call(f32[96,128]{1,0:T(8,128)} %block_ref), custom_call_target="tpu_custom_call" | custom-call | tf_op jit(solution)/shard_map/pallas_call | solution.py:137
  51.7 0.0 copy-done
  51.7 3.5 %fusion = f32[4,96,512]{2,1,0:T(8,128)} fusion(f32[512,512]{1,0:T(8,128)S(1)} %copy-done, f32[4,4,12,8,128]{4,3,2,1,0:T(8,128)} %bitcast.48), kind=kOutput, calls=%fused_computation.3 | convolution fusion | flops 1207959552 | bytes 2621440 | tf_op jit(solution)/shard_map/dot_general | solution.py:234
  55.2 0.0 all-gather.3.cloned.1.call-update
  55.2 26.2 %all-to-all-start = ((f32[128,2,1152]{2,1,0:T(2,128)}), f32[128,2,1152]{2,1,0:T(2,128)S(1)}, u32[]{:S(2)}, u32[]{:S(2)}) async-start(f32[128,2,1152]{2,1,0:T(2,128)} %reshape.109), calls=%async_computation | async-start | bytes 2359296 | tf_op jit(solution)/shard_map/all_to_all | solution.py:210
  81.4 1.7 %copy.27 = f32[4,4,96,128]{3,1,2,0:T(4,128)S(1)} copy(f32[4,4,96,128]{3,2,1,0:T(8,128)} %bitcast.47) | data formatting | bytes 1572864 | tf_op jit(solution)/shard_map/reshape | solution.py:221
  83.1 1.2 reshape_reshape.3
  84.3 2.1 %fusion.8 = f32[96,512]{1,0:T(8,128)S(1)} fusion(f32[512,512]{1,0:T(8,128)S(1)} %copy-done, f32[4,96,512]{2,1,0:T(8,128)} %reshape_reshape.3, s32[]{:T(128)S(6)} %select_n.18), kind=kOutput, calls=%fused_computation.12 | convolution fusion | flops 301989888 | bytes 1441796 | tf_op jit(solution)/shard_map/dot_general | solution.py:227
  86.4 0.7 copy-done.2
  87.1 0.6 constant_dynamic-slice_fusion
  87.7 55.9 %all-to-all-done = f32[128,2,1152]{2,1,0:T(2,128)S(1)} async-done(((f32[128,2,1152]{2,1,0:T(2,128)}), f32[128,2,1152]{2,1,0:T(2,128)S(1)}, u32[]{:S(2)}, u32[]{:S(2)}) %all-to-all-start) | async-done | bytes 1179680 | tf_op jit(solution)/shard_map/all_to_all | solution.py:210
  143.6 0.8 reshape.110
  144.4 0.1 slice_bitcast_fusion
  144.5 0.0 copy-start.1
  144.5 1.2 copy.19
  145.7 0.7 fusion.11.ids_ref
  146.4 0.0 copy-done.1
  146.4 6.9 %convolution_subtract_fusion.base_ref = f32[96,3072]{1,0:T(8,128)} fusion(f32[96,3072]{1,0:T(8,128)S(1)} %copy-done.1, f32[96,512]{1,0:T(8,128)} %copy-done.2, f32[3072,512]{1,0:T(8,128)} %bitcast.43), kind=kOutput, calls=%fused_computation.1 | convolution fusion | flops 906264576 | bytes 8847360 | tf_op jit(solution)/shard_map/dot_general | solution.py:243
  153.4 6.6 %shard_map.78 = f32[96,3072]{1,0:T(8,128)} custom-call(s32[256]{0:T(256)} %fusion.11.ids_ref, f32[96,3072]{1,0:T(8,128)} %convolution_subtract_fusion.base_ref, f32[256,8,128]{2,1,0:T(8,128)} %bitcast.44), custom_call_target="tpu_custom_call" | custom-call | tf_op jit(solution)/shard_map/pallas_call | solution.py:172
  (11 shorter events, 0.1 us)
Async XLA Ops:
  7.2 44.6 %copy-start = (f32[512,512]{1,0:T(8,128)S(1)}, f32[512,512]{1,0:T(8,128)}, u32[]{:S(2)}) copy-start(f32[512,512]{1,0:T(8,128)} %param.8) | copy-start | bytes 3145732
  7.2 139.2 %all-gather.3.cloned.1.call-start = ((), (), s32[]{:S(2)}) async-start(), calls=%async_computation.1 | async-start | bytes 7077888 | tf_op jit(solution)/shard_map/all_gather | solution.py:240
  8.8 2.0 %copy-start.3 = (f32[1,1,192,1024]{3,2,1,0:T(8,128)S(1)}, f32[1,1,192,1024]{3,2,1,0:T(8,128)}, u32[]{:S(2)}) copy-start(f32[1,1,192,1024]{3,2,1,0:T(8,128)} %param.11) | copy-start | bytes 2359300
  55.2 88.3 %all-to-all-start = ((f32[128,2,1152]{2,1,0:T(2,128)}), f32[128,2,1152]{2,1,0:T(2,128)S(1)}, u32[]{:S(2)}, u32[]{:S(2)}) async-start(f32[128,2,1152]{2,1,0:T(2,128)} %reshape.109), calls=%async_computation | async-start | bytes 2359296 | tf_op jit(solution)/shard_map/all_to_all | solution.py:210
  86.4 0.7 copy-start.2
  144.5 1.9 %copy-start.1 = (f32[96,3072]{1,0:T(8,128)S(1)}, f32[96,3072]{1,0:T(8,128)}, u32[]{:S(2)}) copy-start(f32[96,3072]{1,0:T(8,128)} %param.10) | copy-start | bytes 3538948
Sparse Core Ops, SparseCore 0:
  55.4 62.8 all-gather.2

commit v19 on v15

--- a/solution.py
+++ b/solution.py
@@ -164,7 +164,7 @@
 
         return carry
 
-    lax.fori_loop(0, vals_ref.shape[0], body, 0, unroll=8)
+    lax.fori_loop(0, vals_ref.shape[0], body, 0, unroll=32)
 
 
 def add_tiles(ids, base, vals, tile_cols, tiles_dev):

time: 165 us -> 166 us (level)
  no operation moved by 1% of the time
where the time goes in v19:
time: 166 us
  waiting for transfers between devices  56 us (34%)
  Pallas kernels  45.5 us (27%)
  starting transfers between devices  26.2 us (16%)
  between operations  14.2 us (9%)
  matrix products  12.5 us (8%)
  local copies, waits for them, and re-layouts  8.68 us (5%)
  other arithmetic  2.96 us (2%)
    all_to_all x1, waiting for transfers between devices, per_device(): lax.all_to_all(send, ROW_AXES, split_axis=0, concat_axis=0, tiled=True)  55.9 us
    pallas_call x1, Pallas kernels, front_exchange(): pl.pallas_call(functools.partial(_front_kernel, n_x, n_zh, n_c), out_shap...  37.6 us
    all_to_all x1, starting transfers between devices, per_device(): lax.all_to_all(send, ROW_AXES, split_axis=0, concat_axis=0, tiled=True)  26.2 us
    pallas_call x1, Pallas kernels, add_tiles(): pl.pallas_call(functools.partial(_add_tiles_kernel, tile_cols, tiles_dev)...  7.97 us
    dot_general x1, matrix products, per_device(): lax.dot_general(own_full, partner, (((1,), (1,)), ((), ())), precision=la...  6.94 us
    dot_general x1, matrix products, per_device(): jnp.dot(to_rows(moved_panel), diag_inverse.T, precision=lax.Precision.HIG...  3.47 us
  transfers between devices with their start and end apart: 2, of which 1 were waited for; matrix products, arithmetic and copies ran while one was open for 6% of the time, Pallas kernels for 0%

profile of v19, /device:TPU:1, one launch (start us, length us, event | category | flops | bytes accessed | tf_op | source)
XLA Modules:
  0.0 166.0 jit_solution(9752299824792786850)
XLA Ops:
  7.2 0.0 copy-start
  7.2 0.0 all-gather.3.cloned.1.call-start
  7.2 37.6 %shard_map.77 = (f32[16,96,128]{2,1,0:T(8,128)}, f32[16,96,128]{2,1,0:T(8,128)}) custom-call(f32[96,128]{1,0:T(8,128)} %block_ref.1), custom_call_target="tpu_custom_call" | custom-call | tf_op jit(solution)/shard_map/pallas_call | solution.py:137
  44.8 0.0 copy-start.4
  44.8 3.5 %fusion = f32[4,96,512]{2,1,0:T(8,128)} fusion(f32[512,512]{1,0:T(8,128)S(1)} %copy-done, f32[4,4,12,8,128]{4,3,2,1,0:T(8,128)} %bitcast.47), kind=kOutput, calls=%fused_computation.3 | convolution fusion | flops 1207959552 | bytes 2621440 | tf_op jit(solution)/shard_map/dot_general | solution.py:231
  48.3 0.0 all-gather.3.cloned.1.call-update
  48.3 0.1 iota_compare_fusion
  48.4 0.0 copy-start.3
  48.5 0.1 fusion.12
  48.7 0.3 copy-done.5
  49.0 0.2 fusion.15
  49.2 0.1 scatter.15
  49.3 0.1 broadcast_in_dim.2
  49.4 0.2 copy-done.3
  49.6 1.8 %scatter_custom_fusion = f32[256,1152]{1,0:T(8,128)S(1)} fusion(f32[256,1152]{1,0:T(8,128)S(1)} %scatter.15, s32[192]{0:T(256)S(1)} %bitcast.57, f32[192,128]{1,0:T(8,128)S(1)} %broadcast_in_dim.2, f32[]{:T(128)} %constant.71, f32[192,1024]{1,0:T(8,128)S(1)} %bitcast.45), kind=kCustom, calls=%fused_computation.5 | custom fusion | flops 221184 | bytes 2064388 | tf_op jit(solution)/shard_map/scatter | solution.py:206
  51.4 1.7 %all_to_all.8 = f32[128,2,1152]{2,1,0:T(2,128)} reshape(f32[256,1152]{1,0:T(8,128)S(1)} %scatter_custom_fusion) | data formatting | bytes 2359296 | tf_op jit(solution)/shard_map/all_to_all | solution.py:208
  53.1 26.2 %all-to-all-start = ((f32[128,2,1152]{2,1,0:T(2,128)}), f32[128,2,1152]{2,1,0:T(2,128)S(1)}, u32[]{:S(2)}, u32[]{:S(2)}) async-start(f32[128,2,1152]{2,1,0:T(2,128)} %all_to_all.8), calls=%async_computation | async-start | bytes 2359296 | tf_op jit(solution)/shard_map/all_to_all | solution.py:208
  79.3 1.6 copy.27
  80.9 1.2 reshape_reshape.3
  82.1 2.1 %fusion.8 = f32[96,512]{1,0:T(8,128)S(1)} fusion(f32[512,512]{1,0:T(8,128)S(1)} %copy-done, f32[4,96,512]{2,1,0:T(8,128)} %reshape_reshape.3, s32[]{:T(128)S(6)} %select_n.18), kind=kOutput, calls=%fused_computation.12 | convolution fusion | flops 301989888 | bytes 1441796 | tf_op jit(solution)/shard_map/dot_general | solution.py:224
  84.2 0.0 copy-start.2
  84.2 0.7 copy-done.2
  84.8 0.6 constant_dynamic-slice_fusion
  85.5 55.9 %all-to-all-done = f32[128,2,1152]{2,1,0:T(2,128)S(1)} async-done(((f32[128,2,1152]{2,1,0:T(2,128)}), f32[128,2,1152]{2,1,0:T(2,128)S(1)}, u32[]{:S(2)}, u32[]{:S(2)}) %all-to-all-start) | async-done | bytes 1179680 | tf_op jit(solution)/shard_map/all_to_all | solution.py:208
  141.4 0.8 all_to_all.10
  142.2 0.1 slice_bitcast_fusion
  142.3 0.0 copy-start.1
  142.4 1.2 copy.19
  143.6 0.7 fusion.11.ids_ref
  144.2 0.0 copy-done.1
  144.2 6.9 %convolution_subtract_fusion.base_ref = f32[96,3072]{1,0:T(8,128)} fusion(f32[96,3072]{1,0:T(8,128)S(1)} %copy-done.1, f32[96,512]{1,0:T(8,128)} %copy-done.2, f32[3072,512]{1,0:T(8,128)} %bitcast.42), kind=kOutput, calls=%fused_computation.1 | convolution fusion | flops 906264576 | bytes 8847360 | tf_op jit(solution)/shard_map/dot_general | solution.py:240
  151.2 8.0 %shard_map.78 = f32[96,3072]{1,0:T(8,128)} custom-call(s32[256]{0:T(256)} %fusion.11.ids_ref, f32[96,3072]{1,0:T(8,128)} %convolution_subtract_fusion.base_ref, f32[256,8,128]{2,1,0:T(8,128)} %bitcast.43), custom_call_target="tpu_custom_call" | custom-call | tf_op jit(solution)/shard_map/pallas_call | solution.py:172
  (15 shorter events, 0.1 us)
Async XLA Ops:
  7.2 37.6 %copy-start = (f32[512,512]{1,0:T(8,128)S(1)}, f32[512,512]{1,0:T(8,128)}, u32[]{:S(2)}) copy-start(f32[512,512]{1,0:T(8,128)} %param.8) | copy-start | bytes 3145732
  7.2 137.1 %all-gather.3.cloned.1.call-start = ((), (), s32[]{:S(2)}) async-start(), calls=%async_computation.1 | async-start | bytes 7077888 | tf_op jit(solution)/shard_map/all_gather | solution.py:237
  44.8 3.5 %copy-start.4 = (s32[1,1,192,1]{2,3,1,0:T(1,128)S(1)}, s32[1,1,192,1]{2,3,1,0:T(1,128)}, u32[]{:S(2)}) copy-start(s32[1,1,192,1]{2,3,1,0:T(1,128)} %param.12) | copy-start | bytes 2308
  48.3 0.7 copy-start.5
  48.4 1.1 copy-start.3
  53.1 88.3 %all-to-all-start = ((f32[128,2,1152]{2,1,0:T(2,128)}), f32[128,2,1152]{2,1,0:T(2,128)S(1)}, u32[]{:S(2)}, u32[]{:S(2)}) async-start(f32[128,2,1152]{2,1,0:T(2,128)} %all_to_all.8), calls=%async_computation | async-start | bytes 2359296 | tf_op jit(solution)/shard_map/all_to_all | solution.py:208
  84.2 0.7 copy-start.2
  142.3 1.9 %copy-start.1 = (f32[96,3072]{1,0:T(8,128)S(1)}, f32[96,3072]{1,0:T(8,128)}, u32[]{:S(2)}) copy-start(f32[96,3072]{1,0:T(8,128)} %param.10) | copy-start | bytes 3538948
Sparse Core Ops, SparseCore 0:
  48.4 62.8 all-gather.2

commit v20 on v15

--- a/solution.py
+++ b/solution.py
@@ -24,6 +24,8 @@
     right = lax.rem(me + 1, n)
     left = lax.rem(me + n - 1, n)
     is_source = x == col
+    direct_from = n - n // 3
+    relay_a = direct_from // 2
 
     def on_ring(p):
         return {"zh": p // n_c, "col": lax.rem(p, n_c)}
@@ -35,9 +37,9 @@
     for other in (left, right):
         pl.semaphore_signal(barrier, 1, device_id=on_ring(other), device_id_type=MESH_IDS)
 
-    for k in (1, n_x - 1):
+    for k in (1, 2, n_x - 1):
         pl.semaphore_signal(barrier, 1, device_id=x_peer(k), device_id_type=MESH_IDS)
-    pl.semaphore_wait(barrier, 4)
+    pl.semaphore_wait(barrier, 5)
 
     ring_ref[me] = block_ref[...]
 
@@ -45,7 +47,7 @@
         return pltpu.make_async_remote_copy(
             src_ref=src,
             dst_ref=moved_ref.at[slot],
-            send_sem=xsend_sem.at[slot, 0 if k == 1 else 1],
+            send_sem=xsend_sem.at[slot, {1: 0, 2: 2}.get(k, 1)],
             recv_sem=xrecv_sem.at[0],
             device_id=x_peer(k),
             device_id_type=MESH_IDS,
@@ -56,6 +58,10 @@
         def _():
             for k in (1, n_x - 1):
                 x_copy(slot, src, k).start()
+
+            @pl.when(slot >= direct_from)
+            def _():
+                x_copy(slot, src, 2).start()
 
     counts = (n // 2, n - 1 - n // 2)
     targets = (right, left)
@@ -95,6 +101,8 @@
         for slot in range(n):
             for k in (1, n_x - 1):
                 x_copy(slot, ring_ref.at[slot], k).wait_send()
+        for slot in range(direct_from, n):
+            x_copy(slot, ring_ref.at[slot], 2).wait_send()
         local = pltpu.make_async_copy(ring_ref, moved_ref, local_sem.at[0])
         local.start()
         local.wait()
@@ -113,11 +121,10 @@
         )
         whole.wait_recv()
 
-    half = n // 2
-    for role, first, k in ((1, 0, 1), (n_x - 1, half, n_x - 1)):
+    for role, first, size, k in ((1, 0, relay_a, 1), (n_x - 1, relay_a, direct_from - relay_a, n_x - 1)):
         @pl.when(shift == role)
         def _():
-            part = pl.ds(first, half)
+            part = pl.ds(first, size)
             onward = pltpu.make_async_remote_copy(
                 src_ref=moved_ref.at[part],
                 dst_ref=moved_ref.at[part],
@@ -142,7 +149,7 @@
         scratch_shapes=[
             pltpu.SemaphoreType.DMA((2, steps)),
             pltpu.SemaphoreType.DMA((2, steps)),
-            pltpu.SemaphoreType.DMA((n, max(n_x - 1, 1))),
+            pltpu.SemaphoreType.DMA((n, max(n_x - 1, 3))),
             pltpu.SemaphoreType.DMA((1,)),
             pltpu.SemaphoreType.DMA((1,)),
         ],

time: 165 us -> 164 us (level)
  no operation moved by 1% of the time
where the time goes in v20:
time: 164 us; the launch traced here: 165 us
  waiting for transfers between devices  55.2 us (34%)
  Pallas kernels  45.8 us (28%)
  starting transfers between devices  25.3 us (15%)
  between operations  14.2 us (9%)
  matrix products  12.5 us (8%)
  local copies, waits for them, and re-layouts  8.68 us (5%)
  other arithmetic  2.96 us (2%)
    all_to_all x1, waiting for transfers between devices, per_device(): lax.all_to_all(send, ROW_AXES, split_axis=0, concat_axis=0, tiled=True)  55.2 us
    pallas_call x1, Pallas kernels, front_exchange(): pl.pallas_call(functools.partial(_front_kernel, n_x, n_zh, n_c), out_shap...  37.7 us
    all_to_all x1, starting transfers between devices, per_device(): lax.all_to_all(send, ROW_AXES, split_axis=0, concat_axis=0, tiled=True)  25.3 us
    pallas_call x1, Pallas kernels, add_tiles(): pl.pallas_call(functools.partial(_add_tiles_kernel, tile_cols, tiles_dev)...  8.1 us
    dot_general x1, matrix products, per_device(): lax.dot_general(own_full, partner, (((1,), (1,)), ((), ())), precision=la...  6.94 us
    dot_general x1, matrix products, per_device(): jnp.dot(to_rows(moved_panel), diag_inverse.T, precision=lax.Precision.HIG...  3.47 us
  transfers between devices with their start and end apart: 2, of which 1 were waited for; matrix products, arithmetic and copies ran while one was open for 6% of the time, Pallas kernels for 0%

profile of v20, /device:TPU:1, one launch (start us, length us, event | category | flops | bytes accessed | tf_op | source)
XLA Modules:
  0.0 164.6 jit_solution(12403451247705500511)
XLA Ops:
  7.2 0.0 copy-start
  7.2 0.0 all-gather.3.cloned.1.call-start
  7.2 37.7 %shard_map.77 = (f32[16,96,128]{2,1,0:T(8,128)}, f32[16,96,128]{2,1,0:T(8,128)}) custom-call(f32[96,128]{1,0:T(8,128)} %block_ref.1), custom_call_target="tpu_custom_call" | custom-call | tf_op jit(solution)/shard_map/pallas_call | solution.py:144
  44.9 0.0 copy-done
  44.9 0.0 copy-start.4
  44.9 3.5 %fusion = f32[4,96,512]{2,1,0:T(8,128)} fusion(f32[512,512]{1,0:T(8,128)S(1)} %copy-done, f32[4,4,12,8,128]{4,3,2,1,0:T(8,128)} %bitcast.47), kind=kOutput, calls=%fused_computation.3 | convolution fusion | flops 1207959552 | bytes 2621440 | tf_op jit(solution)/shard_map/dot_general | solution.py:238
  48.4 0.0 all-gather.3.cloned.1.call-update
  48.4 0.0 copy-done.4
  48.5 0.1 iota_compare_fusion
  48.5 0.0 copy-start.3
  48.6 0.1 fusion.12
  48.8 0.3 copy-done.5
  49.1 0.2 fusion.15
  49.3 0.1 scatter.15
  49.4 0.1 broadcast_in_dim.2
  49.5 0.2 copy-done.3
  49.7 1.8 %scatter_custom_fusion = f32[256,1152]{1,0:T(8,128)S(1)} fusion(f32[256,1152]{1,0:T(8,128)S(1)} %scatter.15, s32[192]{0:T(256)S(1)} %bitcast.57, f32[192,128]{1,0:T(8,128)S(1)} %broadcast_in_dim.2, f32[]{:T(128)} %constant.71, f32[192,1024]{1,0:T(8,128)S(1)} %bitcast.45), kind=kCustom, calls=%fused_computation.5 | custom fusion | flops 221184 | bytes 2064388 | tf_op jit(solution)/shard_map/scatter | solution.py:213
  51.5 1.7 %all_to_all.8 = f32[128,2,1152]{2,1,0:T(2,128)} reshape(f32[256,1152]{1,0:T(8,128)S(1)} %scatter_custom_fusion) | data formatting | bytes 2359296 | tf_op jit(solution)/shard_map/all_to_all | solution.py:215
  53.2 25.3 %all-to-all-start = ((f32[128,2,1152]{2,1,0:T(2,128)}), f32[128,2,1152]{2,1,0:T(2,128)S(1)}, u32[]{:S(2)}, u32[]{:S(2)}) async-start(f32[128,2,1152]{2,1,0:T(2,128)} %all_to_all.8), calls=%async_computation | async-start | bytes 2359296 | tf_op jit(solution)/shard_map/all_to_all | solution.py:215
  78.5 1.6 copy.27
  80.1 1.2 reshape_reshape.3
  81.3 2.1 %fusion.8 = f32[96,512]{1,0:T(8,128)S(1)} fusion(f32[512,512]{1,0:T(8,128)S(1)} %copy-done, f32[4,96,512]{2,1,0:T(8,128)} %reshape_reshape.3, s32[]{:T(128)S(6)} %select_n.18), kind=kOutput, calls=%fused_computation.12 | convolution fusion | flops 301989888 | bytes 1441796 | tf_op jit(solution)/shard_map/dot_general | solution.py:231
  83.4 0.7 copy-done.2
  84.1 0.6 constant_dynamic-slice_fusion
  84.7 55.2 %all-to-all-done = f32[128,2,1152]{2,1,0:T(2,128)S(1)} async-done(((f32[128,2,1152]{2,1,0:T(2,128)}), f32[128,2,1152]{2,1,0:T(2,128)S(1)}, u32[]{:S(2)}, u32[]{:S(2)}) %all-to-all-start) | async-done | bytes 1179680 | tf_op jit(solution)/shard_map/all_to_all | solution.py:215
  139.9 0.8 all_to_all.10
  140.7 0.1 slice_bitcast_fusion
  140.8 0.0 copy-start.1
  140.8 1.2 copy.19
  142.0 0.7 fusion.11.ids_ref
  142.7 6.9 %convolution_subtract_fusion.base_ref = f32[96,3072]{1,0:T(8,128)} fusion(f32[96,3072]{1,0:T(8,128)S(1)} %copy-done.1, f32[96,512]{1,0:T(8,128)} %copy-done.2, f32[3072,512]{1,0:T(8,128)} %bitcast.42), kind=kOutput, calls=%fused_computation.1 | convolution fusion | flops 906264576 | bytes 8847360 | tf_op jit(solution)/shard_map/dot_general | solution.py:247
  149.6 8.1 %shard_map.78 = f32[96,3072]{1,0:T(8,128)} custom-call(s32[256]{0:T(256)} %fusion.11.ids_ref, f32[96,3072]{1,0:T(8,128)} %convolution_subtract_fusion.base_ref, f32[256,8,128]{2,1,0:T(8,128)} %bitcast.43), custom_call_target="tpu_custom_call" | custom-call | tf_op jit(solution)/shard_map/pallas_call | solution.py:179
  (15 shorter events, 0.1 us)
Async XLA Ops:
  7.2 37.8 %copy-start = (f32[512,512]{1,0:T(8,128)S(1)}, f32[512,512]{1,0:T(8,128)}, u32[]{:S(2)}) copy-start(f32[512,512]{1,0:T(8,128)} %param.8) | copy-start | bytes 3145732
  7.2 135.5 %all-gather.3.cloned.1.call-start = ((), (), s32[]{:S(2)}) async-start(), calls=%async_computation.1 | async-start | bytes 7077888 | tf_op jit(solution)/shard_map/all_gather | solution.py:244
  44.9 3.5 %copy-start.4 = (s32[1,1,192,1]{2,3,1,0:T(1,128)S(1)}, s32[1,1,192,1]{2,3,1,0:T(1,128)}, u32[]{:S(2)}) copy-start(s32[1,1,192,1]{2,3,1,0:T(1,128)} %param.12) | copy-start | bytes 2308
  48.4 0.7 copy-start.5
  48.5 1.1 copy-start.3
  53.2 86.7 %all-to-all-start = ((f32[128,2,1152]{2,1,0:T(2,128)}), f32[128,2,1152]{2,1,0:T(2,128)S(1)}, u32[]{:S(2)}, u32[]{:S(2)}) async-start(f32[128,2,1152]{2,1,0:T(2,128)} %all_to_all.8), calls=%async_computation | async-start | bytes 2359296 | tf_op jit(solution)/shard_map/all_to_all | solution.py:215
  83.4 0.7 copy-start.2
  140.8 1.9 %copy-start.1 = (f32[96,3072]{1,0:T(8,128)S(1)}, f32[96,3072]{1,0:T(8,128)}, u32[]{:S(2)}) copy-start(f32[96,3072]{1,0:T(8,128)} %param.10) | copy-start | bytes 3538948
Sparse Core Ops, SparseCore 0:
  48.6 60.9 all-gather.2
